TPU v7x, 32 devices: a whole 2x2x4 slice. The times are simulated.
32 devices in a mesh: batch: 8 (over z, x), head: 4 (over y, core).
Axes of the slice: x: 2, y: 2, z: 4, core: 2. Of those that a mesh axis runs over, the one named last changes fastest.
Arguments:
- tokens: bfloat16 [16, 1024, 768], P('batch', 'head'), may hold values from -6 to 6
- memory: bfloat16 [16, 1024, 768], P('batch', 'head'), may hold values from -6 to 6
- cotangent: bfloat16 [16, 1024, 768], P('batch', 'head'), may hold values from -6 to 6
- target_segments: int32 [16, 1024], P('batch'), may hold values from 0 to 7, as said below
- memory_segments: int32 [16, 1024], P('batch'), may hold values from -1 to 7, as said below
- self_gain: float32 [768], replicated, may hold values from 0.5 to 1.5
- self_query: bfloat16 [768, 768], P(None, 'head'), may hold values from -0.109375 to 0.109375
- self_key: bfloat16 [768, 768], P(None, 'head'), may hold values from -0.109375 to 0.109375
- self_value: bfloat16 [768, 768], P(None, 'head'), may hold values from -0.21875 to 0.21875
- self_out: bfloat16 [768, 768], replicated, may hold values from -0.875 to 0.875
- position_bias: float32 [32, 12], P(None, 'head'), may hold values from -4 to 4
- cross_gain: float32 [768], replicated, may hold values from 0.5 to 1.5
- cross_query: bfloat16 [768, 768], P(None, 'head'), may hold values from -0.109375 to 0.109375
- cross_key: bfloat16 [768, 768], P(None, 'head'), may hold values from -0.109375 to 0.109375
- cross_value: bfloat16 [768, 768], P(None, 'head'), may hold values from -0.21875 to 0.21875
- cross_out: bfloat16 [768, 768], replicated, may hold values from -0.875 to 0.875
- ff_gain: float32 [768], replicated, may hold values from 0.5 to 1.5
- ff_gate: bfloat16 [768, 2048], replicated, may hold values from -0.21875 to 0.21875
- ff_up: bfloat16 [768, 2048], replicated, may hold values from -0.21875 to 0.21875
- ff_down: bfloat16 [2048, 768], replicated, may hold values from -0.125 to 0.125
Outputs:
- layer_out: bfloat16 [16, 1024, 768], P('batch', 'head')
- tokens_grad: bfloat16 [16, 1024, 768], P('batch', 'head')
- memory_grad: bfloat16 [16, 1024, 768], P('batch', 'head')
- self_gain_grad: float32 [768], P(('batch', 'head'))
- self_query_grad: float32 [768, 768], P('batch', 'head')
- self_key_grad: float32 [768, 768], P('batch', 'head')
- self_value_grad: float32 [768, 768], P('batch', 'head')
- self_out_grad: float32 [768, 768], P(None, ('batch', 'head'))
- position_bias_grad: float32 [32, 12], P(None, 'head')
- cross_gain_grad: float32 [768], P(('batch', 'head'))
- cross_query_grad: float32 [768, 768], P('batch', 'head')
- cross_key_grad: float32 [768, 768], P('batch', 'head')
- cross_value_grad: float32 [768, 768], P('batch', 'head')
- cross_out_grad: float32 [768, 768], P(None, ('batch', 'head'))
- ff_gain_grad: float32 [768], P(('batch', 'head'))
- ff_gate_grad: float32 [768, 2048], P(None, ('batch', 'head'))
- ff_up_grad: float32 [768, 2048], P(None, ('batch', 'head'))
- ff_down_grad: float32 [2048, 768], P(None, ('batch', 'head'))
Inputs may be any that keep to these rules, and one draw needn't show every extreme that they name: `target_segments`: each row is cut into aligned blocks of 512 tokens; each block is split into whole segments of 128, 256 or 512 tokens, numbered along the row from 0 without falling. The first row has segments of 128 tokens only. `memory_segments`: each row repeats its target_segments row, except that in every segment between 1 and 64 of the last tokens are padding, marked -1.
All inputs are finite; a program needn't handle non-finite values.
Results may differ from a plain program's by a relative error of at most 0.023.
The roundings to bfloat16 on the way count: a program that leaves them out, or rounds other values in their place, can miss the bound.
Values may be sent and summed in bfloat16 or wider, within the bound.
A program may use at most 384 MiB of HBM per device.

v0:
```python
import jax
import jax.numpy as jnp
import numpy as np
from jax import lax
from jax.sharding import PartitionSpec as P

NORM_EPS = 1e-06
MASKED_SCORE = -1e30


def in_blocks(shard, dim, size):
    shape = shard.shape
    parts = shard.reshape(*shape[:dim], size, shape[dim] // size, *shape[dim + 1 :])
    return jnp.moveaxis(parts, dim, 0)


def sent_and_summed(shard, axis, dim):
    size = lax.axis_size(axis)
    parts = lax.all_to_all(in_blocks(shard, dim, size), axis, 0, 0, tiled=True)
    return jnp.sum(parts.astype(jnp.float32), axis=0)


def side_by_side(arrays, axis, dim, along):
    both = jnp.concatenate(arrays, axis=along)
    result, at, done = (sent_and_summed(both, axis, dim), 0, [])
    for a in arrays:
        done.append(lax.slice_in_dim(result, at, at + a.shape[along], axis=along))
        at += a.shape[along]
    return tuple(done)


def bucket_edges():
    distance = np.arange(1.0, 8192.0)
    far_bucket = 16.0 + np.floor(np.log(np.maximum(distance, 16.0) / 16.0) / np.log(8.0) * 16.0)
    bucket_value = np.where(distance < 16, distance, np.minimum(far_bucket, 31.0))
    return [int(distance[np.argmax(bucket_value >= bucket_level)]) for bucket_level in range(1, 32)]


def distance_rows(row_start, row_count, length):
    query_pos = row_start + lax.broadcasted_iota(jnp.int32, (row_count, length), 0)
    key_pos = lax.broadcasted_iota(jnp.int32, (row_count, length), 1)
    return query_pos - key_pos


def bucket_of(distance):
    bucket_ids = jnp.zeros(distance.shape, jnp.int32)
    for edge_value in bucket_edges():
        bucket_ids = bucket_ids + (distance >= edge_value).astype(jnp.int32)
    return bucket_ids


def bias_from_table(table, bucket_ids):
    result = jnp.zeros((table.shape[1],) + bucket_ids.shape, jnp.float32)
    for bucket_index in range(table.shape[0]):
        result = (
            result
            + jnp.where(bucket_ids == bucket_index, 1.0, 0.0)[None]
            * table[bucket_index][:, None, None]
        )
    return result


def causal_mask(segment_row):

    def causal_build_mask(row_start, row_count):
        same_doc = segment_row[row_start : row_start + row_count][:, None] == segment_row[None, :]
        return same_doc & (distance_rows(row_start, row_count, segment_row.shape[0]) >= 0)

    return causal_build_mask


def cross_mask(segment_row, memory_row):

    def cross_build_mask(row_start, row_count):
        return segment_row[row_start : row_start + row_count][:, None] == memory_row[None, :]

    return cross_build_mask


def rms_norm(hidden, gain_vector):
    inv_scale = lax.rsqrt(jnp.mean(hidden * hidden, axis=-1, keepdims=True) + NORM_EPS)
    return hidden * inv_scale * gain_vector


def norm_back(hidden, gain_vector, grad_out):
    unused, pullback = jax.vjp(rms_norm, hidden, gain_vector)
    return pullback(grad_out)


def gated(gate_value, up_value):
    return jax.nn.gelu(gate_value, approximate=True) * up_value


def contract_rows(left_side, right_side):
    return lax.dot_general(
        left_side, right_side, (((0,), (0,)), ((), ())), preferred_element_type=jnp.float32
    )


def times_transpose(left_side, right_side):
    return lax.dot_general(
        left_side, right_side, (((1,), (1,)), ((), ())), preferred_element_type=jnp.float32
    )


def block_scores(query_block, key_heads, mask_fn, table, row_start):
    row_count = query_block.shape[0]
    scores = jnp.einsum("qhd,khd->hqk", query_block, key_heads, preferred_element_type=jnp.float32)
    bucket_ids = None
    if table is not None:
        bucket_ids = bucket_of(distance_rows(row_start, row_count, key_heads.shape[0]))
        scores = scores + bias_from_table(table, bucket_ids)
    return (jnp.where(mask_fn(row_start, row_count)[None], scores, MASKED_SCORE), bucket_ids)


def attend_forward(query_heads, key_heads, value_heads, mask_fn, table):
    length = query_heads.shape[0]
    block_rows = min(512, length)
    contexts = []
    log_totals = []
    for row_start in range(0, length, block_rows):
        query_block = query_heads[row_start : row_start + block_rows]
        masked, unused = block_scores(query_block, key_heads, mask_fn, table, row_start)
        row_max = jnp.max(masked, axis=-1, keepdims=True)
        exp_scores = jnp.exp(masked - row_max)
        row_total = jnp.sum(exp_scores, axis=-1, keepdims=True)
        weights = (exp_scores / row_total).astype(jnp.bfloat16)
        contexts.append(
            jnp.einsum("hqk,khd->qhd", weights, value_heads, preferred_element_type=jnp.float32)
        )
        log_totals.append(row_max + jnp.log(row_total))
    return (jnp.concatenate(contexts, axis=0), jnp.concatenate(log_totals, axis=1))


def attend_backward(query_heads, key_heads, value_heads, grad_context, log_totals, mask_fn, table):
    length = query_heads.shape[0]
    block_rows = min(512, length)
    key_grad = jnp.zeros(key_heads.shape, jnp.float32)
    value_grad = jnp.zeros(value_heads.shape, jnp.float32)
    query_grads = []
    bias_grad = None
    if table is not None:
        bias_grad = jnp.zeros((table.shape[1], table.shape[0]), jnp.float32)
    for row_start in range(0, length, block_rows):
        query_block = query_heads[row_start : row_start + block_rows]
        grad_block = grad_context[row_start : row_start + block_rows]
        masked, bucket_ids = block_scores(query_block, key_heads, mask_fn, table, row_start)
        prob_rows = jnp.exp(masked - log_totals[:, row_start : row_start + block_rows])
        grad_probs = jnp.einsum(
            "qhd,khd->hqk", grad_block, value_heads, preferred_element_type=jnp.float32
        )
        inner_sum = jnp.sum(grad_probs * prob_rows, axis=-1, keepdims=True)
        grad_scores = (prob_rows * (grad_probs - inner_sum)).astype(jnp.bfloat16)
        query_grads.append(
            jnp.einsum("hqk,khd->qhd", grad_scores, key_heads, preferred_element_type=jnp.float32)
        )
        key_grad = key_grad + jnp.einsum(
            "hqk,qhd->khd", grad_scores, query_block, preferred_element_type=jnp.float32
        )
        value_grad = value_grad + jnp.einsum(
            "hqk,qhd->khd",
            prob_rows.astype(jnp.bfloat16),
            grad_block,
            preferred_element_type=jnp.float32,
        )
        if table is not None:
            bucket_table = jax.nn.one_hot(bucket_ids, table.shape[0], dtype=jnp.bfloat16)
            bias_grad = bias_grad + jnp.einsum(
                "hqk,qkb->hb", grad_scores, bucket_table, preferred_element_type=jnp.float32
            )
    if table is not None:
        bias_grad = jnp.transpose(bias_grad)
    return (jnp.concatenate(query_grads, axis=0), key_grad, value_grad, bias_grad)


def on_device(
    tokens,
    memory,
    cotangent,
    target_segments,
    memory_segments,
    self_gain,
    self_query,
    self_key,
    self_value,
    self_out,
    position_bias,
    cross_gain,
    cross_query,
    cross_key,
    cross_value,
    cross_out,
    ff_gain,
    ff_gate,
    ff_up,
    ff_down,
):
    inner_local = self_query.shape[1]
    heads_local = position_bias.shape[1]
    head_size = inner_local // heads_local
    self_proj = jnp.concatenate((self_query, self_key, self_value), axis=1)
    cross_pair = jnp.concatenate((cross_key, cross_value), axis=1)
    weight_set = (
        self_gain,
        self_query,
        self_key,
        self_value,
        self_out,
        position_bias,
        cross_gain,
        cross_query,
        cross_key,
        cross_value,
        cross_out,
        ff_gain,
        ff_gate,
        ff_up,
        ff_down,
    )
    zero_grads = tuple((jnp.zeros(weight_item.shape, jnp.float32) for weight_item in weight_set))

    def split_heads(matrix):
        return matrix.reshape(matrix.shape[0], heads_local, head_size)

    def micro_step(grad_sums, micro_items):
        tok_in, mem_in, cot_in, target_row, memory_row = micro_items
        self_allowed = causal_mask(target_row)
        cross_allowed = cross_mask(target_row, memory_row)
        tok_wide = tok_in.astype(jnp.float32)
        normed_one = rms_norm(tok_wide, self_gain).astype(jnp.bfloat16)
        normed_all = lax.all_gather(normed_one, "head", axis=0, tiled=True)
        projected = jnp.dot(normed_all, self_proj, preferred_element_type=jnp.float32)
        query_one = projected[:, :inner_local].astype(jnp.bfloat16)
        key_one = projected[:, inner_local : 2 * inner_local].astype(jnp.bfloat16)
        value_one = projected[:, 2 * inner_local :].astype(jnp.bfloat16)
        context_one, totals_one = attend_forward(
            split_heads(query_one),
            split_heads(key_one),
            split_heads(value_one),
            self_allowed,
            position_bias,
        )
        context_one = context_one.reshape(-1, inner_local).astype(jnp.bfloat16)
        context_tok = lax.all_to_all(context_one, "head", split_axis=0, concat_axis=1, tiled=True)
        first_sum = tok_wide + jnp.dot(context_tok, self_out, preferred_element_type=jnp.float32)
        normed_two = rms_norm(first_sum, cross_gain).astype(jnp.bfloat16)
        normed_two_all, memory_all = (
            lax.all_gather(normed_two, "head", axis=0, tiled=True),
            lax.all_gather(mem_in, "head", axis=0, tiled=True),
        )
        query_two = jnp.dot(normed_two_all, cross_query, preferred_element_type=jnp.float32).astype(
            jnp.bfloat16
        )
        pair_two = jnp.dot(memory_all, cross_pair, preferred_element_type=jnp.float32)
        key_two = pair_two[:, :inner_local].astype(jnp.bfloat16)
        value_two = pair_two[:, inner_local:].astype(jnp.bfloat16)
        context_two, totals_two = attend_forward(
            split_heads(query_two),
            split_heads(key_two),
            split_heads(value_two),
            cross_allowed,
            None,
        )
        context_two = context_two.reshape(-1, inner_local).astype(jnp.bfloat16)
        context_two_tok = lax.all_to_all(
            context_two, "head", split_axis=0, concat_axis=1, tiled=True
        )
        second_sum = first_sum + jnp.dot(
            context_two_tok, cross_out, preferred_element_type=jnp.float32
        )
        normed_three = rms_norm(second_sum, ff_gain).astype(jnp.bfloat16)
        gate_value = jnp.dot(normed_three, ff_gate, preferred_element_type=jnp.float32)
        up_value = jnp.dot(normed_three, ff_up, preferred_element_type=jnp.float32)
        activation = gated(gate_value, up_value).astype(jnp.bfloat16)
        layer_out = (
            second_sum + jnp.dot(activation, ff_down, preferred_element_type=jnp.float32)
        ).astype(jnp.bfloat16)
        down_grad = contract_rows(activation, cot_in)
        grad_act = times_transpose(cot_in, ff_down)
        unused, gate_pull = jax.vjp(gated, gate_value, up_value)
        grad_gate, grad_up = gate_pull(grad_act)
        grad_gate = grad_gate.astype(jnp.bfloat16)
        grad_up = grad_up.astype(jnp.bfloat16)
        gate_grad = contract_rows(normed_three, grad_gate)
        up_grad = contract_rows(normed_three, grad_up)
        grad_normed_three = times_transpose(grad_gate, ff_gate) + times_transpose(grad_up, ff_up)
        back_second, ff_gain_grad = norm_back(second_sum, ff_gain, grad_normed_three)
        grad_second = cot_in.astype(jnp.float32) + back_second
        branch_two = grad_second.astype(jnp.bfloat16)
        cross_out_grad = contract_rows(context_two_tok, branch_two)
        grad_context_two = times_transpose(branch_two, cross_out).astype(jnp.bfloat16)
        grad_context_two = lax.all_to_all(
            grad_context_two, "head", split_axis=1, concat_axis=0, tiled=True
        )
        grad_q_two, grad_k_two, grad_v_two, unused_bias = attend_backward(
            split_heads(query_two),
            split_heads(key_two),
            split_heads(value_two),
            split_heads(grad_context_two),
            totals_two,
            cross_allowed,
            None,
        )
        grad_q_two = grad_q_two.reshape(-1, inner_local).astype(jnp.bfloat16)
        grad_k_two = grad_k_two.reshape(-1, inner_local).astype(jnp.bfloat16)
        grad_v_two = grad_v_two.reshape(-1, inner_local).astype(jnp.bfloat16)
        cross_query_grad = contract_rows(normed_two_all, grad_q_two)
        cross_key_grad = contract_rows(memory_all, grad_k_two)
        cross_value_grad = contract_rows(memory_all, grad_v_two)
        grad_memory_all = times_transpose(
            jnp.concatenate((grad_k_two, grad_v_two), axis=1), cross_pair
        )
        grad_normed_two_all = times_transpose(grad_q_two, cross_query)
        grad_normed_two, grad_memory = (
            lax.psum_scatter(
                grad_normed_two_all.astype(jnp.bfloat16), "head", scatter_dimension=0, tiled=True
            ).astype(jnp.float32),
            lax.psum_scatter(
                grad_memory_all.astype(jnp.bfloat16), "head", scatter_dimension=0, tiled=True
            ).astype(jnp.float32),
        )
        back_first, cross_gain_grad = norm_back(first_sum, cross_gain, grad_normed_two)
        grad_first = grad_second + back_first
        branch_one = grad_first.astype(jnp.bfloat16)
        self_out_grad = contract_rows(context_tok, branch_one)
        grad_context_one = times_transpose(branch_one, self_out).astype(jnp.bfloat16)
        grad_context_one = lax.all_to_all(
            grad_context_one, "head", split_axis=1, concat_axis=0, tiled=True
        )
        grad_q_one, grad_k_one, grad_v_one, bias_grad = attend_backward(
            split_heads(query_one),
            split_heads(key_one),
            split_heads(value_one),
            split_heads(grad_context_one),
            totals_one,
            self_allowed,
            position_bias,
        )
        grad_q_one = grad_q_one.reshape(-1, inner_local).astype(jnp.bfloat16)
        grad_k_one = grad_k_one.reshape(-1, inner_local).astype(jnp.bfloat16)
        grad_v_one = grad_v_one.reshape(-1, inner_local).astype(jnp.bfloat16)
        query_grad = contract_rows(normed_all, grad_q_one)
        key_grad = contract_rows(normed_all, grad_k_one)
        value_grad = contract_rows(normed_all, grad_v_one)
        grad_normed_one_all = times_transpose(
            jnp.concatenate((grad_q_one, grad_k_one, grad_v_one), axis=1), self_proj
        )
        grad_normed_one = lax.psum_scatter(
            grad_normed_one_all.astype(jnp.bfloat16), "head", scatter_dimension=0, tiled=True
        ).astype(jnp.float32)
        back_tok, self_gain_grad = norm_back(tok_wide, self_gain, grad_normed_one)
        tokens_grad = (grad_first + back_tok).astype(jnp.bfloat16)
        updates = (
            self_gain_grad,
            query_grad,
            key_grad,
            value_grad,
            self_out_grad,
            bias_grad,
            cross_gain_grad,
            cross_query_grad,
            cross_key_grad,
            cross_value_grad,
            cross_out_grad,
            ff_gain_grad,
            gate_grad,
            up_grad,
            down_grad,
        )
        return (
            jax.tree.map(jnp.add, grad_sums, updates),
            (layer_out, tokens_grad, grad_memory.astype(jnp.bfloat16)),
        )

    grad_sums, stacked = lax.scan(
        micro_step, zero_grads, (tokens, memory, cotangent, target_segments, memory_segments)
    )
    head_parts = side_by_side(
        (
            grad_sums[1].astype(jnp.bfloat16),
            grad_sums[2].astype(jnp.bfloat16),
            grad_sums[3].astype(jnp.bfloat16),
            grad_sums[7].astype(jnp.bfloat16),
            grad_sums[8].astype(jnp.bfloat16),
            grad_sums[9].astype(jnp.bfloat16),
        ),
        "batch",
        0,
        1,
    )
    shared = (
        grad_sums[4],
        grad_sums[10],
        grad_sums[12],
        grad_sums[13],
        grad_sums[14],
        grad_sums[0].reshape(1, -1),
        grad_sums[6].reshape(1, -1),
        grad_sums[11].reshape(1, -1),
    )
    summed = (
        lax.psum_scatter(shared[0], ("batch", "head"), scatter_dimension=1, tiled=True),
        lax.psum_scatter(shared[1], ("batch", "head"), scatter_dimension=1, tiled=True),
        lax.psum_scatter(shared[2], ("batch", "head"), scatter_dimension=1, tiled=True),
        lax.psum_scatter(shared[3], ("batch", "head"), scatter_dimension=1, tiled=True),
        lax.psum_scatter(shared[4], ("batch", "head"), scatter_dimension=1, tiled=True),
        lax.psum_scatter(shared[5], ("batch", "head"), scatter_dimension=1, tiled=True),
        lax.psum_scatter(shared[6], ("batch", "head"), scatter_dimension=1, tiled=True),
        lax.psum_scatter(shared[7], ("batch", "head"), scatter_dimension=1, tiled=True),
    )
    bias_total = lax.psum(grad_sums[5], "batch")
    return (
        stacked[0],
        stacked[1],
        stacked[2],
        summed[5].reshape(-1),
        head_parts[0],
        head_parts[1],
        head_parts[2],
        summed[0],
        bias_total,
        summed[6].reshape(-1),
        head_parts[3],
        head_parts[4],
        head_parts[5],
        summed[1],
        summed[7].reshape(-1),
        summed[2],
        summed[3],
        summed[4],
    )


def solution(mesh):
    return jax.shard_map(
        on_device,
        mesh=mesh,
        in_specs=(
            P("batch", "head", None),
            P("batch", "head", None),
            P("batch", "head", None),
            P("batch", None),
            P("batch", None),
            P(),
            P(None, "head"),
            P(None, "head"),
            P(None, "head"),
            P(),
            P(None, "head"),
            P(),
            P(None, "head"),
            P(None, "head"),
            P(None, "head"),
            P(),
            P(),
            P(),
            P(),
            P(),
        ),
        out_specs=(
            P("batch", "head", None),
            P("batch", "head", None),
            P("batch", "head", None),
            P(("batch", "head")),
            P("batch", "head"),
            P("batch", "head"),
            P("batch", "head"),
            P(None, ("batch", "head")),
            P(None, "head"),
            P(("batch", "head")),
            P("batch", "head"),
            P("batch", "head"),
            P("batch", "head"),
            P(None, ("batch", "head")),
            P(("batch", "head")),
            P(None, ("batch", "head")),
            P(None, ("batch", "head")),
            P(None, ("batch", "head")),
        ),
        check_vma=False,
    )
```

profile of v0, /device:TPU:0, one launch (start us, length us, event | category | flops | bytes accessed | tf_op | source)
XLA Modules:
  0.0 1601.1 jit_solution(8424553373998950626)
XLA Ops:
  14.5 997.5 %while.47 = (s32[]{:T(128)}, f32[768]{0:T(1024)}, f32[768,192]{0,1:T(8,128)}, f32[768,192]{0,1:T(8,128)}, f32[768,192]{0,1:T(8,128)}, /*index=5*/f32[768,768]{1,...) while((s32[]{:T(128)}, f32[768]{0:T(1024)}, ...), condition=%wide.region_25.26_spmd.clone, body=%wide.region_0.25_spmd.clone.sunk | while | flops 20934422528 | bytes 1386171520 | solution.py:375
  22.0 8.0 compare_select_fusion.82
  30.0 7.9 compare_select_fusion.83
  37.9 8.0 compare_select_fusion.84
  45.9 8.5 compare_select_fusion.85
  54.3 7.9 compare_select_fusion.86
  62.2 7.9 compare_select_fusion.87
  70.1 8.1 compare_select_fusion.88
  78.2 8.0 compare_select_fusion.89
  86.2 8.0 compare_select_fusion.90
  94.2 8.1 compare_select_fusion.91
  102.3 7.9 compare_select_fusion.92
  110.2 7.9 compare_select_fusion.93
  118.2 8.4 compare_select_fusion.94
  126.5 8.0 compare_select_fusion.95
  134.5 7.9 compare_select_fusion.96
  142.4 8.1 compare_select_fusion.97
  151.2 22.0 %compare_select_fusion.81 = (f32[512,1024]{1,0:T(8,128)S(1)}, f32[512,1024]{1,0:T(8,128)}, f32[512,1024]{1,0:T(8,128)}, f32[512,1024]{1,0:T(8,128)}, f32[512,102...) fusion(s32[512]{0:T(512)S(1)} %iota_add_fusion.2), kind=kLoop, calls=%fused_computation.171.clone.1 | loop fusion | flops 82313216 | bytes 67110912 | tf_op jit(solution)/shard_map/while/body/eval_jaxpr/jit(_where)/select_n | solution.py:57
  180.4 31.3 %fusion.555 = (f32[3,512]{1,0:T(4,128)S(1)}, f32[3,512,1024]{2,1,0:T(8,128)}) fusion(f32[3]{0:T(128)} %get-tuple-element.1340, f32[512,1024]{1,0:T(8,128)} %get-tuple-element.1413, f32[3]{0:T(128)} %get-tuple-element.1342, f32[512,1024]{1,0:T(8,128)} %get-tuple-element.1414, f32[3]{0:T(128)} %get-tuple-element.1344, ...), kind=kOutput, calls=%fused_computation.400.clone.1 | convolution fusion | flops 305134080 | bytes 74520960 | tf_op jit(solution)/shard_map/while/body/eval_jaxpr/qhd,khd->hqk/dot_general | solution.py:108
  219.7 30.8 %fusion.552 = (f32[3,512]{1,0:T(4,128)S(1)}, f32[3,512,1024]{2,1,0:T(8,128)}) fusion(f32[3]{0:T(128)} %get-tuple-element.1340, f32[512,1024]{1,0:T(8,128)} %get-tuple-element.1341, f32[3]{0:T(128)} %get-tuple-element.1342, f32[512,1024]{1,0:T(8,128)} %get-tuple-element.1343, f32[3]{0:T(128)} %get-tuple-element.1344, ...), kind=kOutput, calls=%fused_computation.399.clone.1 | convolution fusion | flops 305134080 | bytes 74520960 | tf_op jit(solution)/shard_map/while/body/eval_jaxpr/qhd,khd->hqk/dot_general | solution.py:108
  263.6 7.4 all-to-all-done
  273.8 7.4 convert_add_fusion.5
  284.2 7.3 convert_add_fusion.6
  320.2 7.4 all-to-all-done.1
  416.6 16.8 %reduce-scatter.26.cloned.1.call-done = bf16[256,768]{1,0:T(8,128)(2,1)} async-done(((bf16[1024,768]{1,0:T(8,128)(2,1)}), bf16[256,768]{1,0:T(8,128)(2,1)}) %reduce-scatter.26.cloned.1.call-update) | async-done | bytes 393232 | tf_op jit(solution)/shard_map/while/body/eval_jaxpr/reduce_scatter | solution.py:318
  470.9 8.0 copy.167
  483.5 10.5 fusion.584
  494.1 10.9 fusion.585
  516.6 7.9 compare_select_fusion.82
  524.5 7.9 compare_select_fusion.83
  532.4 8.0 compare_select_fusion.84
  540.4 8.2 compare_select_fusion.85
  548.6 7.9 compare_select_fusion.86
  556.5 7.9 compare_select_fusion.87
  564.4 8.4 compare_select_fusion.88
  572.7 8.0 compare_select_fusion.89
  580.8 8.0 compare_select_fusion.90
  588.7 8.1 compare_select_fusion.91
  596.8 7.9 compare_select_fusion.92
  604.7 7.9 compare_select_fusion.93
  612.6 8.2 compare_select_fusion.94
  620.8 8.0 compare_select_fusion.95
  628.8 7.9 compare_select_fusion.96
  636.7 8.3 compare_select_fusion.97
  645.8 22.0 %compare_select_fusion.81 = (f32[512,1024]{1,0:T(8,128)S(1)}, f32[512,1024]{1,0:T(8,128)}, f32[512,1024]{1,0:T(8,128)}, f32[512,1024]{1,0:T(8,128)}, f32[512,102...) fusion(s32[512]{0:T(512)S(1)} %iota_add_fusion.2), kind=kLoop, calls=%fused_computation.171.clone.1 | loop fusion | flops 82313216 | bytes 67110912 | tf_op jit(solution)/shard_map/while/body/eval_jaxpr/jit(_where)/select_n | solution.py:57
  675.0 31.3 %fusion.555 = (f32[3,512]{1,0:T(4,128)S(1)}, f32[3,512,1024]{2,1,0:T(8,128)}) fusion(f32[3]{0:T(128)} %get-tuple-element.1340, f32[512,1024]{1,0:T(8,128)} %get-tuple-element.1413, f32[3]{0:T(128)} %get-tuple-element.1342, f32[512,1024]{1,0:T(8,128)} %get-tuple-element.1414, f32[3]{0:T(128)} %get-tuple-element.1344, ...), kind=kOutput, calls=%fused_computation.400.clone.1 | convolution fusion | flops 305134080 | bytes 74520960 | tf_op jit(solution)/shard_map/while/body/eval_jaxpr/qhd,khd->hqk/dot_general | solution.py:108
  714.2 30.8 %fusion.552 = (f32[3,512]{1,0:T(4,128)S(1)}, f32[3,512,1024]{2,1,0:T(8,128)}) fusion(f32[3]{0:T(128)} %get-tuple-element.1340, f32[512,1024]{1,0:T(8,128)} %get-tuple-element.1341, f32[3]{0:T(128)} %get-tuple-element.1342, f32[512,1024]{1,0:T(8,128)} %get-tuple-element.1343, f32[3]{0:T(128)} %get-tuple-element.1344, ...), kind=kOutput, calls=%fused_computation.399.clone.1 | convolution fusion | flops 305134080 | bytes 74520960 | tf_op jit(solution)/shard_map/while/body/eval_jaxpr/qhd,khd->hqk/dot_general | solution.py:108
  757.2 7.4 all-to-all-done
  767.3 7.4 convert_add_fusion.5
  777.7 7.3 convert_add_fusion.6
  814.0 7.4 all-to-all-done.1
  871.5 7.2 select_add_fusion.23
  917.3 14.6 reduce-scatter.26.cloned.1.call-done
  970.2 7.9 copy.167
  982.9 10.5 fusion.584
  993.5 10.7 fusion.585
  1018.8 6.7 copy.136
  1025.6 6.6 copy.137
  1050.5 49.9 %psum.7 = f32[32,3]{0,1:T(4,128)} all-reduce(f32[32,3]{0,1:T(4,128)S(1)} %copy-done.135), channel_id=1, replica_groups=mesh['batch'=8,'head'=4] {'batch'}, use_global_device_ids=true, to_apply=%region_29.30 | all-reduce | flops 96 | bytes 768 | tf_op jit(solution)/shard_map/psum | solution.py:411
  1100.5 46.1 %all-reduce.3 = (f32[1,768]{1,0:T(1,128)S(1)}, f32[1,768]{1,0:T(1,128)S(1)}, f32[1,768]{1,0:T(1,128)S(1)}) all-reduce(f32[1,768]{1,0:T(1,128)S(1)} %reshape.1573, f32[1,768]{1,0:T(1,128)S(1)} %reshape.1576, f32[1,768]{1,0:T(1,128)S(1)} %reshape.1578), channel_id=6, replica_groups=mesh['batch'=8,'head'=4] {'batch','head'}, use_global_device_ids=true, to_apply=%region_26.27.clone | all-reduce | flops 2304 | bytes 18432
  1148.8 84.9 %reduce-scatter.14.cloned.1.call-done = f32[768,24]{0,1:T(8,128)} async-done(((f32[768,768]{0,1:T(8,128)}), f32[768,24]{0,1:T(8,128)}) %reduce-scatter.14.cloned.1.call-update) | async-done | bytes 73744 | tf_op jit(solution)/shard_map/reduce_scatter | solution.py:403
  1233.7 119.7 %reduce-scatter.16.cloned.1.call-done = f32[768,64]{0,1:T(8,128)} async-done(((f32[768,2048]{0,1:T(8,128)}), f32[768,64]{0,1:T(8,128)}) %reduce-scatter.16.cloned.1.call-update) | async-done | bytes 196624 | tf_op jit(solution)/shard_map/reduce_scatter | solution.py:404
  1353.3 120.4 %reduce-scatter.18.cloned.1.call-done = f32[768,64]{0,1:T(8,128)} async-done(((f32[768,2048]{0,1:T(8,128)}), f32[768,64]{0,1:T(8,128)}) %reduce-scatter.18.cloned.1.call-update) | async-done | bytes 196624 | tf_op jit(solution)/shard_map/reduce_scatter | solution.py:405
  1473.7 119.5 %reduce-scatter.20.cloned.1.call-done = f32[2048,24]{0,1:T(8,128)} async-done(((f32[2048,768]{0,1:T(8,128)}), f32[2048,24]{0,1:T(8,128)}) %reduce-scatter.20.cloned.1.call-update) | async-done | bytes 196624 | tf_op jit(solution)/shard_map/reduce_scatter | solution.py:406
  (949 shorter events, 442.1 us)
Async XLA Ops:
  14.5 15.4 copy-start.106
  14.5 161.3 %all-gather.8.cloned.1.call-start = ((), (), s32[]{:S(2)}) async-start(), calls=%async_computation.18 | async-start | bytes 1966080 | tf_op jit(solution)/shard_map/while/body/eval_jaxpr/all_gather | solution.py:231
  18.8 280.0 %all-gather.10.cloned.1.call-start = ((), (), s32[]{:S(2)}) async-start(), calls=%async_computation.19 | async-start | bytes 1966080 | tf_op jit(solution)/shard_map/while/body/eval_jaxpr/all_gather | solution.py:249
  175.8 186.4 %copy-start.11 = (pred[512,1024]{1,0:T(8,128)(4,1)}, pred[512,1024]{1,0:T(8,128)(4,1)S(1)}, u32[]{:S(2)}) copy-start(pred[512,1024]{1,0:T(8,128)(4,1)S(1)} %get-tuple-element.1457) | copy-start | bytes 1572868 | tf_op jit(solution)/shard_map/while
  179.6 40.1 %copy-start.23 = (bf16[1024,192]{0,1:T(8,128)(2,1)}, bf16[1024,192]{0,1:T(8,128)(2,1)S(1)}, u32[]{:S(2)}) copy-start(bf16[1024,192]{0,1:T(8,128)(2,1)S(1)} %get-tuple-element.1405) | copy-start | bytes 1179652 | tf_op jit(solution)/shard_map/while
  258.2 12.9 copy-start.29
  258.5 14.3 copy-start.101
  259.3 11.7 all-to-all-start
  263.6 37.6 %all-gather.12.cloned.1.call-start = ((), (), s32[]{:S(2)}) async-start(), calls=%async_computation.20 | async-start | bytes 1966080 | tf_op jit(solution)/shard_map/while/body/eval_jaxpr/all_gather | solution.py:248
  272.8 11.4 copy-start.119
  272.8 54.8 %copy-start.9 = (f32[256,768]{1,0:T(8,128)}, f32[256,768]{1,0:T(8,128)S(1)}, u32[]{:S(2)}) copy-start(f32[256,768]{1,0:T(8,128)S(1)} %get-tuple-element.1449) | copy-start | bytes 2359300 | tf_op jit(solution)/shard_map/while
  272.8 11.4 copy-start.113
  316.6 13.1 copy-start.103
  316.6 11.0 all-to-all-start.1
  342.0 10.9 all-to-all-start.2
  345.5 62.3 %reduce-scatter.22.cloned.1.call-start = ((), (), s32[]{:S(2)}) async-start(), calls=%async_computation.21 | async-start | bytes 1966080 | tf_op jit(solution)/shard_map/while/body/eval_jaxpr/reduce_scatter | solution.py:315
  373.4 60.0 %reduce-scatter.26.cloned.1.call-start = ((), (), s32[]{:S(2)}) async-start(), calls=%async_computation.23 | async-start | bytes 1966080 | tf_op jit(solution)/shard_map/while/body/eval_jaxpr/reduce_scatter | solution.py:318
  377.1 11.5 slice-start.12
  411.4 22.1 %copy-start.138 = (bf16[2,256,768]{2,1,0:T(8,128)(2,1)S(1)}, bf16[2,256,768]{2,1,0:T(8,128)(2,1)}, u32[]{:S(2)}) copy-start(bf16[2,256,768]{2,1,0:T(8,128)(2,1)} %get-tuple-element.1542) | copy-start | bytes 2359300 | tf_op jit(solution)/shard_map/while
  412.0 24.3 %copy-start.36 = (bf16[1024,192]{0,1:T(8,128)(2,1)S(1)}, bf16[1024,192]{0,1:T(8,128)(2,1)}, u32[]{:S(2)}) copy-start(bf16[1024,192]{0,1:T(8,128)(2,1)} %get-tuple-element.1339) | copy-start | bytes 1179652 | tf_op jit(solution)/shard_map/while
  413.0 21.4 %all-to-all-start.3 = ((bf16[256,4,192]{0,2,1:T(8,128)(2,1)}), bf16[256,4,192]{0,2,1:T(8,128)(2,1)S(1)}, u32[]{:S(2)}, u32[]{:S(2)}) async-start(bf16[256,4,192]{0,2,1:T(8,128)(2,1)} %bitcast.532), calls=%async_computation.4 | async-start | bytes 786432 | tf_op jit(solution)/shard_map/while/body/eval_jaxpr/all_to_all | solution.py:327
  416.5 88.6 %reduce-scatter.24.cloned.1.call-start = ((), (), s32[]{:S(2)}) async-start(), calls=%async_computation.22 | async-start | bytes 1966080 | tf_op jit(solution)/shard_map/while/body/eval_jaxpr/reduce_scatter | solution.py:348
  416.5 23.8 %copy-start.130 = (f32[768]{0:T(1024)}, f32[768]{0:T(1024)S(1)}, u32[]{:S(2)}) copy-start(f32[768]{0:T(1024)S(1)} %select_add_fusion.18) | copy-start | bytes 9220 | tf_op jit(solution)/shard_map/while
  480.7 13.3 copy-start.79
  494.0 12.5 copy-start.118
  494.1 12.5 copy-start.123
  494.1 12.5 copy-start.18
  494.1 12.5 copy-start.136
  509.1 15.4 copy-start.106
  509.1 161.3 %all-gather.8.cloned.1.call-start = ((), (), s32[]{:S(2)}) async-start(), calls=%async_computation.18 | async-start | bytes 1966080 | tf_op jit(solution)/shard_map/while/body/eval_jaxpr/all_gather | solution.py:231
  513.4 278.9 %all-gather.10.cloned.1.call-start = ((), (), s32[]{:S(2)}) async-start(), calls=%async_computation.19 | async-start | bytes 1966080 | tf_op jit(solution)/shard_map/while/body/eval_jaxpr/all_gather | solution.py:249
  670.3 185.6 %copy-start.11 = (pred[512,1024]{1,0:T(8,128)(4,1)}, pred[512,1024]{1,0:T(8,128)(4,1)S(1)}, u32[]{:S(2)}) copy-start(pred[512,1024]{1,0:T(8,128)(4,1)S(1)} %get-tuple-element.1457) | copy-start | bytes 1572868 | tf_op jit(solution)/shard_map/while
  674.2 40.0 %copy-start.23 = (bf16[1024,192]{0,1:T(8,128)(2,1)}, bf16[1024,192]{0,1:T(8,128)(2,1)S(1)}, u32[]{:S(2)}) copy-start(bf16[1024,192]{0,1:T(8,128)(2,1)S(1)} %get-tuple-element.1405) | copy-start | bytes 1179652 | tf_op jit(solution)/shard_map/while
  752.5 12.0 copy-start.29
  752.8 13.5 copy-start.101
  753.7 10.9 all-to-all-start
  757.1 37.6 %all-gather.12.cloned.1.call-start = ((), (), s32[]{:S(2)}) async-start(), calls=%async_computation.20 | async-start | bytes 1966080 | tf_op jit(solution)/shard_map/while/body/eval_jaxpr/all_gather | solution.py:248
  766.3 11.5 copy-start.119
  766.3 55.1 %copy-start.9 = (f32[256,768]{1,0:T(8,128)}, f32[256,768]{1,0:T(8,128)S(1)}, u32[]{:S(2)}) copy-start(f32[256,768]{1,0:T(8,128)S(1)} %get-tuple-element.1449) | copy-start | bytes 2359300 | tf_op jit(solution)/shard_map/while
  766.3 11.4 copy-start.113
  794.6 11.4 copy-start.43
  810.3 13.1 copy-start.103
  810.3 11.0 all-to-all-start.1
  835.8 10.9 all-to-all-start.2
  839.2 69.1 %reduce-scatter.22.cloned.1.call-start = ((), (), s32[]{:S(2)}) async-start(), calls=%async_computation.21 | async-start | bytes 1966080 | tf_op jit(solution)/shard_map/while/body/eval_jaxpr/reduce_scatter | solution.py:315
  867.1 64.8 %reduce-scatter.26.cloned.1.call-start = ((), (), s32[]{:S(2)}) async-start(), calls=%async_computation.23 | async-start | bytes 1966080 | tf_op jit(solution)/shard_map/while/body/eval_jaxpr/reduce_scatter | solution.py:318
  867.4 11.2 slice-start.14
  871.4 13.3 slice-start.12
  911.9 20.1 %copy-start.138 = (bf16[2,256,768]{2,1,0:T(8,128)(2,1)S(1)}, bf16[2,256,768]{2,1,0:T(8,128)(2,1)}, u32[]{:S(2)}) copy-start(bf16[2,256,768]{2,1,0:T(8,128)(2,1)} %get-tuple-element.1542) | copy-start | bytes 2359300 | tf_op jit(solution)/shard_map/while
  912.8 22.1 %copy-start.36 = (bf16[1024,192]{0,1:T(8,128)(2,1)S(1)}, bf16[1024,192]{0,1:T(8,128)(2,1)}, u32[]{:S(2)}) copy-start(bf16[1024,192]{0,1:T(8,128)(2,1)} %get-tuple-element.1339) | copy-start | bytes 1179652 | tf_op jit(solution)/shard_map/while
  913.8 19.2 %all-to-all-start.3 = ((bf16[256,4,192]{0,2,1:T(8,128)(2,1)}), bf16[256,4,192]{0,2,1:T(8,128)(2,1)S(1)}, u32[]{:S(2)}, u32[]{:S(2)}) async-start(bf16[256,4,192]{0,2,1:T(8,128)(2,1)} %bitcast.532), calls=%async_computation.4 | async-start | bytes 786432 | tf_op jit(solution)/shard_map/while/body/eval_jaxpr/all_to_all | solution.py:327
  917.2 87.0 %reduce-scatter.24.cloned.1.call-start = ((), (), s32[]{:S(2)}) async-start(), calls=%async_computation.22 | async-start | bytes 1966080 | tf_op jit(solution)/shard_map/while/body/eval_jaxpr/reduce_scatter | solution.py:348
  917.3 21.5 %copy-start.130 = (f32[768]{0:T(1024)}, f32[768]{0:T(1024)S(1)}, u32[]{:S(2)}) copy-start(f32[768]{0:T(1024)S(1)} %select_add_fusion.18) | copy-start | bytes 9220 | tf_op jit(solution)/shard_map/while
  979.9 13.5 copy-start.79
  993.5 12.3 copy-start.118
  993.5 12.3 copy-start.123
  993.5 12.3 copy-start.18
  993.5 12.3 copy-start.136
  1012.0 136.8 %reduce-scatter.12.cloned.1.call-start = ((), (), s32[]{:S(2)}) async-start(), calls=%async_computation.13 | async-start | bytes 2433024 | tf_op jit(solution)/shard_map/reduce_scatter | solution.py:402
  1015.1 218.6 %reduce-scatter.14.cloned.1.call-start = ((), (), s32[]{:S(2)}) async-start(), calls=%async_computation.14 | async-start | bytes 2433024 | tf_op jit(solution)/shard_map/reduce_scatter | solution.py:403
  1018.8 334.6 %reduce-scatter.16.cloned.1.call-start = ((), (), s32[]{:S(2)}) async-start(), calls=%async_computation.15 | async-start | bytes 6488064 | tf_op jit(solution)/shard_map/reduce_scatter | solution.py:404
  1025.5 448.2 %reduce-scatter.18.cloned.1.call-start = ((), (), s32[]{:S(2)}) async-start(), calls=%async_computation.16 | async-start | bytes 6488064 | tf_op jit(solution)/shard_map/reduce_scatter | solution.py:405
  1032.3 560.9 %reduce-scatter.20.cloned.1.call-start = ((), (), s32[]{:S(2)}) async-start(), calls=%async_computation.17 | async-start | bytes 6488064 | tf_op jit(solution)/shard_map/reduce_scatter | solution.py:406
  1044.8 102.9 %all-to-all-start.4 = ((bf16[8,96,1152]{2,1,0:T(8,128)(2,1)}), bf16[8,96,1152]{2,1,0:T(8,128)(2,1)S(1)}, u32[]{:S(2)}, u32[]{:S(2)}) async-start(bf16[8,96,1152]{2,1,0:T(8,128)(2,1)} %bitcast.1), calls=%async_computation.7 | async-start | bytes 3538944 | tf_op jit(solution)/shard_map/all_to_all | solution.py:19
  (264 other events, 898.0 us)
Sparse Core Ops, SparseCore 0:
  18.9 22.3 all-gather.7
  43.0 19.6 all-gather.9
  273.9 20.5 all-gather.11
  373.5 29.2 reduce-scatter.21
  405.2 28.1 reduce-scatter.25
  462.1 29.4 reduce-scatter.23
  513.5 20.9 all-gather.7
  536.1 19.6 all-gather.9
  767.4 20.9 all-gather.11
  867.3 29.5 reduce-scatter.21
  899.4 32.4 reduce-scatter.25
  960.6 28.1 reduce-scatter.23
Sparse Core Ops, SparseCore 1:
  1018.3 110.7 reduce-scatter.11
  1135.7 97.9 reduce-scatter.13
  1239.8 113.5 reduce-scatter.15
  1360.5 113.2 reduce-scatter.17
  1480.0 113.2 reduce-scatter.19
where the time goes:
time: 1610 us; the launch traced here: 1600 us
  waiting for transfers between devices  518 us (32%)
  other arithmetic  398 us (25%)
  matrix products  375 us (23%)
  local copies, waits for them, and re-layouts  154 us (10%)
  blocking collectives  96 us (6%)
  starting transfers between devices  36.1 us (2%)
  between operations  16.4 us (1%)
    select_n x34, other arithmetic, bias_from_table(): jnp.where(bucket_ids == bucket_index, 1.0, 0.0)[None]  301 us
    dot_general x8, matrix products, block_scores(): jnp.einsum('qhd,khd->hqk', query_block, key_heads, preferred_element_type...  129 us
    reduce_scatter x1, waiting for transfers between devices, on_device(): lax.psum_scatter(shared[3], ('batch', 'head'), scatter_dimension=1, tiled...  120 us
    reduce_scatter x1, waiting for transfers between devices, on_device(): lax.psum_scatter(shared[2], ('batch', 'head'), scatter_dimension=1, tiled...  120 us
    reduce_scatter x1, waiting for transfers between devices, on_device(): lax.psum_scatter(shared[4], ('batch', 'head'), scatter_dimension=1, tiled...  119 us
    reduce_scatter x1, waiting for transfers between devices, on_device(): lax.psum_scatter(shared[1], ('batch', 'head'), scatter_dimension=1, tiled...  84.9 us
    dot_general x22, matrix products, contract_rows(): lax.dot_general(left_side, right_side, (((0,), (0,)), ((), ())), preferre...  53.3 us
    psum x1, blocking collectives, on_device(): bias_total = lax.psum(grad_sums[5], 'batch')  49.9 us
  transfers between devices with their start and end apart: 26, of which 12 were waited for; matrix products, arithmetic and copies ran while one was open for 45% of the time, Pallas kernels for 0%

commit v1 on v0

v1 whole, which is shorter than its diff:
```python
import jax
import jax.numpy as jnp
import numpy as np
from jax import lax
from jax.experimental import pallas as pl
from jax.experimental.pallas import tpu as pltpu
from jax.sharding import PartitionSpec as P

NORM_EPS = 1e-06
MASKED = -1e30
BLOCK = 512
TILE = 128
F32 = jnp.float32
BF16 = jnp.bfloat16


def bucket_edges():
    distance = np.arange(1.0, 8192.0)
    far_bucket = 16.0 + np.floor(np.log(np.maximum(distance, 16.0) / 16.0) / np.log(8.0) * 16.0)
    bucket_value = np.where(distance < 16, distance, np.minimum(far_bucket, 31.0))
    return [int(distance[np.argmax(bucket_value >= bucket_level)]) for bucket_level in range(1, 32)]


def bucket_one_hot(buckets):
    ids = np.zeros(2 * TILE, np.int32)
    for edge in bucket_edges():
        ids += np.arange(2 * TILE) >= edge
    assert bucket_edges()[-1] <= TILE + 1
    return (np.arange(buckets)[:, None] == ids[None, :]).astype(np.float32)


def dot(left, right):
    return lax.dot_general(left, right, (((1,), (0,)), ((), ())), preferred_element_type=F32)


def pair_view(token_major, index, heads, size):
    first = index - index % 2
    count = min(2, heads - first)
    return token_major[:, first * size : (first + count) * size], index - first, count


def spread(head_rows, place, count):
    if count == 1:
        return head_rows
    blank = jnp.zeros_like(head_rows)
    return jnp.concatenate((head_rows, blank) if place == 0 else (blank, head_rows), axis=0)


def only_lanes(pair, place, count, size):
    if count == 1:
        return pair
    lane = lax.broadcasted_iota(jnp.int32, pair.shape, 1)
    keep = lane < size if place == 0 else lane >= size
    return jnp.where(keep, pair, jnp.zeros_like(pair))


def bias_tiles(table, index, one_hot):
    column = table[:, index : index + 1]
    by_distance = jnp.sum(column * one_hot, axis=0, keepdims=True)
    wide = jnp.broadcast_to(by_distance, (TILE, 2 * TILE))
    turned = pltpu.roll(wide, 0, 1, stride=1, stride_axis=0)
    key = lax.broadcasted_iota(jnp.int32, (TILE, TILE), 0)
    query = lax.broadcasted_iota(jnp.int32, (TILE, TILE), 1)
    near = jnp.where(key <= query, turned[:, :TILE], MASKED)
    return near, turned[:, TILE:], table[table.shape[0] - 1, index]


def self_tile(scores, key_tile, query_tile, tiles, seg_ref, base):
    near, next_one, far = tiles
    if key_tile == query_tile:
        return scores + near
    same = seg_ref[base + key_tile] == seg_ref[base + query_tile]
    shift = jnp.where(same, 0.0, MASKED)
    if key_tile == query_tile - 1:
        return scores + next_one + shift
    return scores + (far + shift)


def self_forward_kernel(heads, size, seg_ref, where_ref, q_ref, k_ref, v_ref, tab_ref, hot_ref, o_ref, lse_ref):
    base = pl.program_id(1) * (BLOCK // TILE)
    keys = jnp.transpose(k_ref[0])
    table = tab_ref[0]
    for index in range(heads):
        rows = slice(index * size, (index + 1) * size)
        pair, place, count = pair_view(keys, index, heads, size)
        query = spread(q_ref[0, rows, :], place, count)
        tiles = bias_tiles(table, index, hot_ref[...])
        for half in range(2):
            end = (half + 1) * 2 * TILE
            scores = dot(pair[:end], query[:, half * 256 : (half + 1) * 256])
            columns = []
            totals = []
            for part in range(2):
                query_tile = 2 * half + part
                parts = [
                    self_tile(
                        scores[kt * TILE : (kt + 1) * TILE, part * TILE : (part + 1) * TILE],
                        kt, query_tile, tiles, seg_ref, base,
                    )
                    for kt in range(query_tile + 1)
                ]
                top = jnp.max(parts[0], axis=0, keepdims=True)
                for piece in parts[1:]:
                    top = jnp.maximum(top, jnp.max(piece, axis=0, keepdims=True))
                probs = [jnp.exp(piece - top) for piece in parts]
                total = jnp.sum(probs[0], axis=0, keepdims=True)
                for piece in probs[1:]:
                    total = total + jnp.sum(piece, axis=0, keepdims=True)
                probs = [piece.astype(BF16) for piece in probs]
                if part == 0:
                    probs.append(jnp.zeros((TILE, TILE), BF16))
                columns.append(jnp.concatenate(probs, axis=0))
                totals.append(total)
                lse_ref[0, index : index + 1, query_tile * TILE : (query_tile + 1) * TILE] = top + jnp.log(total)
            weights = jnp.concatenate(columns, axis=1)
            context = dot(v_ref[0, rows, :end], weights)
            context = context / jnp.concatenate(totals, axis=1)
            o_ref[rows, half * 256 : (half + 1) * 256] = context.astype(BF16)


def key_mask(seg_ref, base, memseg_ref, mask_ref):
    rows = jnp.transpose(jnp.broadcast_to(memseg_ref[0].astype(F32), (TILE, BLOCK)))
    for tile in range(BLOCK // TILE):
        wanted = seg_ref[base + tile].astype(F32)
        mask_ref[:, tile * TILE : (tile + 1) * TILE] = jnp.where(rows == wanted, 0.0, MASKED)


def cross_forward_kernel(heads, size, seg_ref, where_ref, q_ref, k_ref, v_ref, memseg_ref, o_ref, lse_ref, mask_ref):
    base = pl.program_id(1) * (BLOCK // TILE)
    key_mask(seg_ref, base, memseg_ref, mask_ref)
    keys = jnp.transpose(k_ref[0])
    for index in range(heads):
        rows = slice(index * size, (index + 1) * size)
        pair, place, count = pair_view(keys, index, heads, size)
        query = spread(q_ref[0, rows, :], place, count)
        for half in range(2):
            lanes = slice(half * 256, (half + 1) * 256)
            scores = dot(pair, query[:, lanes]) + mask_ref[:, lanes]
            top = jnp.max(scores, axis=0, keepdims=True)
            probs = jnp.exp(scores - top)
            total = jnp.sum(probs, axis=0, keepdims=True)
            context = dot(v_ref[0, rows, :], probs.astype(BF16)) / total
            o_ref[rows, lanes] = context.astype(BF16)
            lse_ref[0, index : index + 1, lanes] = top + jnp.log(total)


def back_common(heads, size, q_ref, k_ref, v_ref, do_ref):
    return (
        jnp.transpose(q_ref[0]),
        jnp.transpose(k_ref[0]),
        jnp.transpose(v_ref[0]),
        jnp.transpose(do_ref[...]),
    )


def store_sums(heads, size, sums, ref, start):
    wide = jnp.concatenate([s.astype(BF16) for s in sums], axis=1)
    ref[0, start : start + heads * size, :] = jnp.transpose(wide)


def grow(old, new):
    if old is None:
        return new
    shared = old.shape[0]
    if shared == new.shape[0]:
        return old + new
    return jnp.concatenate((old + new[:shared], new[shared:]), axis=0)


def self_backward_kernel(heads, size, seg_ref, where_ref, q_ref, k_ref, v_ref, o_ref, do_ref, lse_ref, tab_ref, hot_ref, d_ref, tabgrad_ref):
    block = pl.program_id(1)
    base = block * (BLOCK // TILE)
    width = heads * size
    query_tok, keys, values, grad_tok = back_common(heads, size, q_ref, k_ref, v_ref, do_ref)
    table = tab_ref[0]
    one_hot = hot_ref[...]
    key_sums, value_sums = [], []
    buckets = one_hot.shape[0]
    lane = lax.broadcasted_iota(jnp.int32, (buckets, TILE), 1)
    bucket = lax.broadcasted_iota(jnp.int32, (buckets, TILE), 0)
    table_grad = jnp.zeros((buckets, TILE), F32)
    key = lax.broadcasted_iota(jnp.int32, (TILE, TILE), 0)
    query = lax.broadcasted_iota(jnp.int32, (TILE, TILE), 1)
    for index in range(heads):
        rows = slice(index * size, (index + 1) * size)
        key_pair, place, count = pair_view(keys, index, heads, size)
        value_pair = pair_view(values, index, heads, size)[0]
        query_pair = only_lanes(pair_view(query_tok, index, heads, size)[0], place, count, size)
        grad_pair = only_lanes(pair_view(grad_tok, index, heads, size)[0], place, count, size)
        query_rows = spread(q_ref[0, rows, :], place, count)
        grad = spread(do_ref[rows, :], place, count)
        inner = jnp.sum(do_ref[rows, :].astype(F32) * o_ref[rows, :].astype(F32), axis=0, keepdims=True)
        tiles = bias_tiles(table, index, one_hot)
        key_sum = value_sum = None
        near_sum = next_sum = far_sum = None
        for half in range(2):
            end = (half + 1) * 2 * TILE
            lanes = slice(half * 256, (half + 1) * 256)
            scores = dot(key_pair[:end], query_rows[:, lanes])
            grad_probs = dot(value_pair[:end], grad[:, lanes])
            prob_columns, grad_columns = [], []
            for part in range(2):
                query_tile = 2 * half + part
                cut = slice(query_tile * TILE, (query_tile + 1) * TILE)
                here = slice(part * TILE, (part + 1) * TILE)
                total = lse_ref[0, index : index + 1, cut]
                probs, grads = [], []
                for kt in range(query_tile + 1):
                    there = slice(kt * TILE, (kt + 1) * TILE)
                    prob = jnp.exp(self_tile(scores[there, here], kt, query_tile, tiles, seg_ref, base) - total)
                    ds = prob * (grad_probs[there, here] - inner[:, cut])
                    if kt == query_tile:
                        near_sum = ds if near_sum is None else near_sum + ds
                    elif kt == query_tile - 1:
                        next_sum = ds if next_sum is None else next_sum + ds
                    else:
                        far_sum = ds if far_sum is None else far_sum + ds
                    probs.append(prob.astype(BF16))
                    grads.append(ds.astype(BF16))
                if part == 0:
                    probs.append(jnp.zeros((TILE, TILE), BF16))
                    grads.append(jnp.zeros((TILE, TILE), BF16))
                prob_columns.append(jnp.concatenate(probs, axis=0))
                grad_columns.append(jnp.concatenate(grads, axis=0))
            probs = jnp.concatenate(prob_columns, axis=1)
            grads = jnp.concatenate(grad_columns, axis=1)
            value_sum = grow(value_sum, dot(probs, grad_pair[lanes]))
            key_sum = grow(key_sum, dot(grads, query_pair[lanes]))
            d_ref[0, rows, lanes] = dot(k_ref[0, rows, :end], grads).astype(BF16)
        if place == 0:
            key_sums.append(key_sum)
            value_sums.append(value_sum)
        else:
            key_sums[-1] = key_sums[-1] + key_sum
            value_sums[-1] = value_sums[-1] + value_sum
        both = jnp.concatenate((near_sum, next_sum), axis=1)
        flip = (key + query == TILE - 1).astype(F32)
        both = jnp.dot(flip, both, precision=lax.Precision.HIGHEST, preferred_element_type=F32)
        turned = pltpu.roll(both, 2 * TILE - (TILE - 1), 1, stride=1, stride_axis=0)
        by_distance = jnp.sum(turned, axis=0, keepdims=True)
        column = jnp.sum(by_distance * one_hot, axis=1, keepdims=True)
        far_total = jnp.sum(jnp.sum(far_sum, axis=0, keepdims=True), axis=1, keepdims=True)
        column = jnp.where(bucket == buckets - 1, column + far_total, column)
        table_grad = table_grad + jnp.where(lane == index, column, 0.0)
    store_sums(heads, size, key_sums, d_ref, width)
    store_sums(heads, size, value_sums, d_ref, 2 * width)

    @pl.when(block == 0)
    def _():
        tabgrad_ref[0] = table_grad

    @pl.when(block > 0)
    def _():
        tabgrad_ref[0] = tabgrad_ref[0] + table_grad


def cross_backward_kernel(heads, size, seg_ref, where_ref, q_ref, k_ref, v_ref, o_ref, do_ref, lse_ref, memseg_ref, dq_ref, dkv_ref, mask_ref):
    base = pl.program_id(1) * (BLOCK // TILE)
    width = heads * size
    key_mask(seg_ref, base, memseg_ref, mask_ref)
    query_tok, keys, values, grad_tok = back_common(heads, size, q_ref, k_ref, v_ref, do_ref)
    key_sums, value_sums = [], []
    for index in range(heads):
        rows = slice(index * size, (index + 1) * size)
        key_pair, place, count = pair_view(keys, index, heads, size)
        value_pair = pair_view(values, index, heads, size)[0]
        query_pair = only_lanes(pair_view(query_tok, index, heads, size)[0], place, count, size)
        grad_pair = only_lanes(pair_view(grad_tok, index, heads, size)[0], place, count, size)
        query = spread(q_ref[0, rows, :], place, count)
        grad = spread(do_ref[rows, :], place, count)
        inner = jnp.sum(do_ref[rows, :].astype(F32) * o_ref[rows, :].astype(F32), axis=0, keepdims=True)
        key_sum = value_sum = None
        for half in range(2):
            lanes = slice(half * 256, (half + 1) * 256)
            scores = dot(key_pair, query[:, lanes]) + mask_ref[:, lanes]
            probs = jnp.exp(scores - lse_ref[0, index : index + 1, lanes])
            grads = probs * (dot(value_pair, grad[:, lanes]) - inner[:, lanes])
            probs, grads = probs.astype(BF16), grads.astype(BF16)
            value_sum = grow(value_sum, dot(probs, grad_pair[lanes]))
            key_sum = grow(key_sum, dot(grads, query_pair[lanes]))
            dq_ref[0, rows, lanes] = dot(k_ref[0, rows, :], grads).astype(BF16)
        if place == 0:
            key_sums.append(key_sum)
            value_sums.append(value_sum)
        else:
            key_sums[-1] = key_sums[-1] + key_sum
            value_sums[-1] = value_sums[-1] + value_sum
    store_sums(heads, size, key_sums, dkv_ref, 0)
    store_sums(heads, size, value_sums, dkv_ref, width)


class Attention:
    def __init__(self, slots, blocks, heads, size):
        self.slots, self.blocks, self.heads, self.size = slots, blocks, heads, size
        self.width = heads * size
        self.tokens = blocks * BLOCK

    def spec(self, rows, part):
        return pl.BlockSpec((1, rows, BLOCK), lambda s, n, seg, here: (s, part, n))

    def by_group(self):
        return pl.BlockSpec((self.width, BLOCK), lambda s, n, seg, here: (jnp.bitwise_xor(here[0], s), n))

    def call(self, kernel, in_specs, out_specs, out_shape, scratch, flops, args):
        size = sum(np.prod(a.shape) * a.dtype.itemsize for a in args)
        return pl.pallas_call(
            kernel,
            grid_spec=pltpu.PrefetchScalarGridSpec(
                num_scalar_prefetch=2,
                grid=(self.slots, self.blocks),
                in_specs=in_specs,
                out_specs=out_specs,
                scratch_shapes=scratch,
            ),
            out_shape=out_shape,
            cost_estimate=pl.CostEstimate(
                flops=int(flops * self.slots * self.blocks * self.heads * BLOCK * BLOCK * self.size),
                bytes_accessed=int(size),
                transcendentals=int(self.slots * self.blocks * self.heads * BLOCK * BLOCK),
            ),
        )(*args)

    def kernel(self, body):
        def run(*refs):
            return body(self.heads, self.size, *refs)

        return run

    def lse_spec(self):
        return pl.BlockSpec((1, 8, BLOCK), lambda s, n, seg, here: (s, 0, n))

    def table_spec(self, table):
        return pl.BlockSpec((1,) + table.shape[1:], lambda s, n, seg, here: (s, 0, 0))

    def whole(self, array):
        return pl.BlockSpec(array.shape, lambda s, n, seg, here: (0,) * array.ndim)

    def memseg_spec(self):
        return pl.BlockSpec((1, 1, BLOCK), lambda s, n, seg, here: (n, 0, 0))

    def forward_shapes(self):
        return (
            jax.ShapeDtypeStruct((self.slots * self.width, self.tokens), BF16),
            jax.ShapeDtypeStruct((self.slots, 8, self.tokens), F32),
        )

    def self_forward(self, segs, here, qkv, table, one_hot):
        w = self.width
        return self.call(
            self.kernel(self_forward_kernel),
            [self.spec(w, 0), self.spec(w, 1), self.spec(w, 2), self.table_spec(table), self.whole(one_hot)],
            [self.by_group(), self.lse_spec()],
            self.forward_shapes(), [], 4, (segs, here, qkv, qkv, qkv, table, one_hot),
        )

    def cross_forward(self, segs, here, q, kv, memseg):
        w = self.width
        return self.call(
            self.kernel(cross_forward_kernel),
            [self.spec(w, 0), self.spec(w, 0), self.spec(w, 1), self.memseg_spec()],
            [self.by_group(), self.lse_spec()],
            self.forward_shapes(), [pltpu.VMEM((BLOCK, BLOCK), F32)], 4, (segs, here, q, kv, kv, memseg),
        )

    def self_backward(self, segs, here, qkv, context, grad, lse, table, one_hot):
        w = self.width
        return self.call(
            self.kernel(self_backward_kernel),
            [self.spec(w, 0), self.spec(w, 1), self.spec(w, 2), self.by_group(), self.by_group(),
             self.lse_spec(), self.table_spec(table), self.whole(one_hot)],
            [self.spec(3 * w, 0), pl.BlockSpec((1, table.shape[1], TILE), lambda s, n, seg, here: (s, 0, 0))],
            (jax.ShapeDtypeStruct((self.slots, 3 * w, self.tokens), BF16),
             jax.ShapeDtypeStruct((self.slots, table.shape[1], TILE), F32)),
            [], 10, (segs, here, qkv, qkv, qkv, context, grad, lse, table, one_hot),
        )

    def cross_backward(self, segs, here, q, kv, context, grad, lse, memseg):
        w = self.width
        return self.call(
            self.kernel(cross_backward_kernel),
            [self.spec(w, 0), self.spec(w, 0), self.spec(w, 1), self.by_group(), self.by_group(),
             self.lse_spec(), self.memseg_spec()],
            [self.spec(w, 0), self.spec(2 * w, 0)],
            (jax.ShapeDtypeStruct((self.slots, w, self.tokens), BF16),
             jax.ShapeDtypeStruct((self.slots, 2 * w, self.tokens), BF16)),
            [pltpu.VMEM((BLOCK, BLOCK), F32)], 10, (segs, here, q, kv, kv, context, grad, lse, memseg),
        )


def swap(array, axis, mask):
    size = lax.axis_size(axis)
    return lax.ppermute(array, axis, [(i, i ^ mask) for i in range(size)])


def pick(array, dim, index):
    return lax.dynamic_index_in_dim(array, index, dim, keepdims=False)


def plus(*arrays):
    total = arrays[0].astype(F32)
    for a in arrays[1:]:
        total = total + a.astype(F32)
    return total.astype(BF16)


def halve(array, axis, mask, dim, bit):
    got = swap(pick(array, dim, 1 - bit), axis, mask)
    return plus(pick(array, dim, bit), got)


def over_batch(array, low_first):
    size = lax.axis_size("batch")
    me = lax.axis_index("batch")
    done = 0
    while (1 << done) < size:
        left = size >> done
        if done == 0 and low_first and left > 1:
            array = halve(array.reshape(left // 2, 2, *array.shape[1:]), "batch", 1, 1, me & 1)
            done = 1
        elif left >= 4:
            array = array.reshape(left // 4, 4, *array.shape[1:])
            mine = (me >> done) & 3
            terms = [pick(array, 1, mine)]
            for k in (1, 2, 3):
                terms.append(swap(pick(array, 1, mine ^ k), "batch", k << done))
            array = plus(*terms) if left > 4 else sum(t.astype(F32) for t in terms)
            done += 2
        else:
            array = halve(array.reshape(left // 2, 2, *array.shape[1:]), "batch", 1 << done, 1, (me >> done) & 1)
            done += 1
    return array[0].astype(F32)


def summed_slots(parts):
    first = plus(parts[0], swap(parts[1], "head", 1))
    if len(parts) == 2:
        return first
    return plus(first, swap(plus(parts[2], swap(parts[3], "head", 1)), "head", 2))


def summed_shared(keep, send, rows_last):
    head, batch = lax.axis_size("head"), lax.axis_size("batch")
    me = lax.axis_index("head")
    core = me & 1
    total = plus(keep, swap(send, "head", 1))
    rows = total.shape[0] // (batch * head)
    total = total.reshape(batch, head // 2, 2 * rows, total.shape[1])
    if rows_last:
        total = total.reshape(batch // 2, 2, head // 2, 2 * rows, total.shape[-1])
        total = halve(total, "batch", 1, 1, lax.axis_index("batch") & 1)
        total = halve(total, "head", 2, 1, me >> 1)
        total = rest_of_batch(total)
    else:
        total = halve(total, "head", 2, 1, me >> 1)
        total = over_batch(total, True)
    total = total.reshape(2, rows, total.shape[-1])
    got = swap(pick(total, 0, 1 - core), "head", 1)
    mine = pick(total, 0, core)
    return jnp.where(core == 0, jnp.concatenate((mine, got), axis=1), jnp.concatenate((got, mine), axis=1))


def rest_of_batch(array):
    size = lax.axis_size("batch")
    me = lax.axis_index("batch")
    done = 1
    while (1 << done) < size:
        left = size >> done
        if left >= 4:
            array = array.reshape(left // 4, 4, *array.shape[1:])
            mine = (me >> done) & 3
            terms = [pick(array, 1, mine)]
            for k in (1, 2, 3):
                terms.append(swap(pick(array, 1, mine ^ k), "batch", k << done))
            array = plus(*terms) if left > 4 else sum(t.astype(F32) for t in terms)
            done += 2
        else:
            array = halve(array.reshape(left // 2, 2, *array.shape[1:]), "batch", 1 << done, 1, (me >> done) & 1)
            done += 1
    return array[0].astype(F32)


def everywhere(array, axes):
    for axis in axes:
        mask = 1
        while mask < lax.axis_size(axis):
            array = array + swap(array, axis, mask)
            mask *= 2
    return array


def norm(hidden, gain):
    scale = lax.rsqrt(jnp.mean(hidden * hidden, axis=-1, keepdims=True) + NORM_EPS)
    return (hidden * scale * gain).astype(BF16)


def norm_back(hidden, gain, grad):
    scale = lax.rsqrt(jnp.mean(hidden * hidden, axis=-1, keepdims=True) + NORM_EPS)
    weighted = grad * gain
    inner = jnp.mean(weighted * hidden, axis=-1, keepdims=True)
    return weighted * scale - hidden * (scale * scale * scale * inner), jnp.sum(grad * hidden * scale, axis=0)


def over_tokens(left, right):
    return lax.dot_general(left, right, (((0,), (0,)), ((), ())), preferred_element_type=F32)


def by_transpose(left, right):
    return lax.dot_general(left, right, (((1,), (1,)), ((), ())), preferred_element_type=F32)


def rows_first(weights, hidden):
    return lax.dot_general(weights, hidden, (((0,), (1,)), ((), ())), preferred_element_type=F32).astype(BF16)


def gelu_parts(value):
    inner = np.float32(np.sqrt(2.0 / np.pi)) * (value + 0.044715 * (value * value * value))
    bend = jnp.tanh(inner)
    slope = np.float32(np.sqrt(2.0 / np.pi)) * (1.0 + 3.0 * 0.044715 * (value * value))
    gelu = 0.5 * value * (1.0 + bend)
    return gelu, 0.5 * (1.0 + bend) + 0.5 * value * (1.0 - bend * bend) * slope


def on_device(
    tokens, memory, cotangent, target_segments, memory_segments, self_gain, self_query, self_key,
    self_value, self_out, position_bias, cross_gain, cross_query, cross_key, cross_value, cross_out,
    ff_gain, ff_gate, ff_up, ff_down,
):
    heads_axis, batch_axis = lax.axis_size("head"), lax.axis_size("batch")
    me, row = lax.axis_index("head"), lax.axis_index("batch")
    core = me & 1
    rows, part, model = tokens.shape
    assert part * 2 == BLOCK and rows % 2 == 0 and heads_axis in (2, 4)
    width = self_query.shape[1]
    heads = position_bias.shape[1]
    size = width // heads
    blocks = rows // 2
    count = blocks * BLOCK
    attention = Attention(heads_axis, blocks, heads, size)
    here = jnp.reshape(me, (1,)).astype(jnp.int32)
    one_hot = jnp.asarray(bucket_one_hot(position_bias.shape[0]))

    def to_blocks(array):
        mine = lax.dynamic_slice_in_dim(array, core * blocks, blocks, 0)
        other = swap(lax.dynamic_slice_in_dim(array, (1 - core) * blocks, blocks, 0), "head", 1)
        both = jnp.where(core == 0, jnp.concatenate((mine, other), 1), jnp.concatenate((other, mine), 1))
        return both.reshape(count, model)

    def from_blocks(array):
        halves = array.reshape(blocks, 2, part, model)
        mine = pick(halves, 1, core)
        other = swap(pick(halves, 1, 1 - core), "head", 1)
        return jnp.where(core == 0, jnp.concatenate((mine, other), 0), jnp.concatenate((other, mine), 0))

    def block_segments(segments):
        mine = lax.dynamic_slice_in_dim(segments, core * blocks, blocks, 0)
        return lax.dynamic_slice_in_dim(mine, (me >> 1) * BLOCK, BLOCK, 1)

    tile_segments = block_segments(target_segments)[:, ::TILE].reshape(-1)
    key_segments = block_segments(memory_segments).reshape(blocks, 1, BLOCK)

    def gathered(array):
        slots = [array, swap(array, "head", 1)]
        if heads_axis == 4:
            slots.append(swap(array, "head", 2))
            slots.append(swap(slots[2], "head", 1))
        return slots

    tok = to_blocks(tokens)
    self_weights = jnp.concatenate(gathered(jnp.concatenate((self_query, self_key, self_value), axis=1)), axis=1)
    table = jnp.stack(gathered(position_bias))
    mem = to_blocks(memory)
    pair_weights = jnp.concatenate(gathered(jnp.concatenate((cross_key, cross_value), axis=1)), axis=1)
    query_weights = jnp.concatenate(gathered(cross_query), axis=1)
    cot = to_blocks(cotangent)

    tok = tok.astype(F32)
    normed_one = norm(tok, self_gain)
    qkv = rows_first(self_weights, normed_one).reshape(heads_axis, 3 * width, count)
    context_one, lse_one = attention.self_forward(tile_segments, here, qkv, table, one_hot)
    kv_two = rows_first(pair_weights, mem).reshape(heads_axis, 2 * width, count)
    first_sum = tok + over_tokens(context_one, self_out)
    normed_two = norm(first_sum, cross_gain)
    q_two = rows_first(query_weights, normed_two).reshape(heads_axis, width, count)
    context_two, lse_two = attention.cross_forward(tile_segments, here, q_two, kv_two, key_segments)
    second_sum = first_sum + over_tokens(context_two, cross_out)
    normed_three = norm(second_sum, ff_gain)
    gate_value = dot(normed_three, ff_gate)
    up_value = dot(normed_three, ff_up)
    gelu, slope = gelu_parts(gate_value)
    activation = (gelu * up_value).astype(BF16)
    layer_out = from_blocks((second_sum + dot(activation, ff_down)).astype(BF16))

    def halves(array):
        lanes = array.shape[1] // 2
        return (
            lax.dynamic_slice_in_dim(array, core * lanes, lanes, 1),
            lax.dynamic_slice_in_dim(array, (1 - core) * lanes, lanes, 1),
        )

    def shared_sum(left, right, second):
        keep, send = halves(left)
        send = over_tokens(right, send).astype(BF16)
        keep = over_tokens(right, keep).astype(BF16)
        return jnp.transpose(summed_shared(keep, send, second))

    grad_act = by_transpose(cot, ff_down)
    grad_gate = (grad_act * up_value * slope).astype(BF16)
    grad_up = (grad_act * gelu).astype(BF16)
    ff_gate_grad = shared_sum(normed_three, grad_gate, False)
    ff_up_grad = shared_sum(normed_three, grad_up, True)
    ff_down_grad = shared_sum(activation, cot, False)
    grad_three = by_transpose(grad_gate, ff_gate) + by_transpose(grad_up, ff_up)
    back, ff_gain_grad = norm_back(second_sum, ff_gain, grad_three)
    grad_second = cot.astype(F32) + back
    branch_two = grad_second.astype(BF16)

    context_two_tok = jnp.transpose(context_two)
    context_one_tok = jnp.transpose(context_one)
    cross_out_grad = shared_sum(context_two_tok, branch_two, True)
    grad_context = by_transpose(cross_out, branch_two).astype(BF16)
    dq_two, dkv_two = attention.cross_backward(
        tile_segments, here, q_two, kv_two, context_two, grad_context, lse_two, key_segments
    )

    def slot_grads(hidden, grads):
        return [
            lax.dot_general(hidden, grads[s], (((0,), (1,)), ((), ())), preferred_element_type=F32).astype(BF16)
            for s in range(heads_axis)
        ]

    def head_sum(parts):
        total = summed_slots(parts)
        return over_batch(total.reshape(batch_axis, total.shape[0] // batch_axis, total.shape[1]), True)

    cross_query_grad = head_sum(slot_grads(normed_two, dq_two))
    pair_grad = head_sum(slot_grads(mem, dkv_two))
    grad_two = lax.dot_general(
        dq_two.reshape(-1, count), query_weights, (((0,), (1,)), ((), ())), preferred_element_type=F32
    )
    back, cross_gain_grad = norm_back(first_sum, cross_gain, grad_two)
    grad_first = grad_second + back
    branch_one = grad_first.astype(BF16)

    self_out_grad = shared_sum(context_one_tok, branch_one, True)
    grad_context = by_transpose(self_out, branch_one).astype(BF16)
    dqkv, table_grad = attention.self_backward(
        tile_segments, here, qkv, context_one, grad_context, lse_one, table, one_hot
    )
    self_grad = head_sum(slot_grads(normed_one, dqkv))
    memory_grad = from_blocks(
        lax.dot_general(
            dkv_two.reshape(-1, count), pair_weights, (((0,), (1,)), ((), ())), preferred_element_type=F32
        ).astype(BF16)
    )
    grad_one = lax.dot_general(
        dqkv.reshape(-1, count), self_weights, (((0,), (1,)), ((), ())), preferred_element_type=F32
    )
    back, self_gain_grad = norm_back(tok, self_gain, grad_one)
    tokens_grad = from_blocks((grad_first + back).astype(BF16))

    table_parts = [table_grad[s, :, :heads] for s in range(heads_axis)]
    bias = table_parts[0] + swap(table_parts[1], "head", 1)
    if heads_axis == 4:
        bias = bias + swap(table_parts[2] + swap(table_parts[3], "head", 1), "head", 2)
    bias_total = everywhere(bias, ("batch",))
    gains = everywhere(jnp.stack((self_gain_grad, cross_gain_grad, ff_gain_grad)), ("head", "batch"))
    share = model // (heads_axis * batch_axis)
    gains = lax.dynamic_slice_in_dim(gains, (row * heads_axis + me) * share, share, 1)

    return (
        layer_out,
        tokens_grad,
        memory_grad,
        gains[0],
        self_grad[:, :width],
        self_grad[:, width : 2 * width],
        self_grad[:, 2 * width :],
        self_out_grad,
        bias_total,
        gains[1],
        cross_query_grad,
        pair_grad[:, :width],
        pair_grad[:, width:],
        cross_out_grad,
        gains[2],
        ff_gate_grad,
        ff_up_grad,
        ff_down_grad,
    )


def solution(mesh):
    tokens = P("batch", "head", None)
    rows = P("batch", None)
    columns = P(None, "head")
    split = P("batch", "head")
    every = P(None, ("batch", "head"))
    gain = P(("batch", "head"))
    return jax.shard_map(
        on_device,
        mesh=mesh,
        in_specs=(
            tokens, tokens, tokens, rows, rows, P(), columns, columns, columns, P(), columns, P(),
            columns, columns, columns, P(), P(), P(), P(), P(),
        ),
        out_specs=(
            tokens, tokens, tokens, gain, split, split, split, every, columns, gain,
            split, split, split, every, gain, every, every, every,
        ),
        check_vma=False,
    )
```

time: 1610 us -> 398 us (0.25)
  waiting for transfers between devices: 518 us -> 96.8 us
  other arithmetic: 398 us -> 24.2 us
  matrix products: 375 us -> 93.9 us
  local copies, waits for them, and re-layouts: 154 us -> 47.6 us
  blocking collectives: 96 us -> 0 us
  Pallas kernels: 0 us -> 48.5 us
  starting transfers between devices: 36.1 us -> 78.3 us
    reduce_scatter x11 -> x0, waiting for transfers between devices: 476 us -> none  [the longest x1 120 us: on_device(): lax.psum_scatter(shared[3], ('batch', 'head'), scatter_dimension=1, tiled...]
    select_n x34 -> x3, other arithmetic: 301 us -> 3.01 us  [from_blocks(): jnp.where(core == 0, jnp.concatenate((mine, other), 0), jnp.concatenate((...]
    dot_general x106 -> x38, matrix products: 375 us -> 93.9 us  [the longest x12 27.7 us: over_tokens(): lax.dot_general(left, right, (((0,), (0,)), ((), ())), preferred_element_...]
    ppermute x0 -> x85, waiting for transfers between devices: none -> 96.8 us  [swap(): return lax.ppermute(array, axis, [(i, i ^ mask) for i in range(size)])]
    ppermute x0 -> x85, starting transfers between devices: none -> 78.3 us  [swap(): return lax.ppermute(array, axis, [(i, i ^ mask) for i in range(size)])]
    while x581 -> x0, local copies, waits for them, and re-layouts: 67.5 us -> none
    psum x1 -> x0, blocking collectives: 49.9 us -> none  [on_device(): bias_total = lax.psum(grad_sums[5], 'batch')]
    pallas_call x0 -> x4, Pallas kernels: none -> 48.5 us  [call(): pl.pallas_call(kernel, grid_spec=pltpu.PrefetchScalarGridSpec(num_scalar_...]
  transfers between devices with their start and end apart: 26 -> 85, of which waited for: 12 -> 31; matrix products, arithmetic and copies ran while one was open for 45% -> 29% of each run, Pallas kernels for 0% -> 6%
where the time goes in v1:
time: 398 us; the launch traced here: 392 us
  waiting for transfers between devices  96.8 us (24%)
  matrix products  93.9 us (24%)
  starting transfers between devices  78.3 us (20%)
  Pallas kernels  48.5 us (12%)
  local copies, waits for them, and re-layouts  47.6 us (12%)
  other arithmetic  24.2 us (6%)
    ppermute x85, waiting for transfers between devices, swap(): return lax.ppermute(array, axis, [(i, i ^ mask) for i in range(size)])  96.8 us
    ppermute x85, starting transfers between devices, swap(): return lax.ppermute(array, axis, [(i, i ^ mask) for i in range(size)])  78.3 us
    pallas_call x4, Pallas kernels, call(): pl.pallas_call(kernel, grid_spec=pltpu.PrefetchScalarGridSpec(num_scalar_...  48.5 us
    dot_general x12, matrix products, over_tokens(): lax.dot_general(left, right, (((0,), (0,)), ((), ())), preferred_element_...  27.7 us
    dot_general x12, matrix products, slot_grads(): lax.dot_general(hidden, grads[s], (((0,), (1,)), ((), ())), preferred_ele...  23.7 us
    unnamed x181, local copies, waits for them, and re-layouts  18.5 us
    dot_general x5, matrix products, by_transpose(): lax.dot_general(left, right, (((1,), (1,)), ((), ())), preferred_element_...  14.8 us
    dot_general x3, matrix products, rows_first(): lax.dot_general(weights, hidden, (((0,), (1,)), ((), ())), preferred_elem...  11.4 us
  transfers between devices with their start and end apart: 85, of which 31 were waited for; matrix products, arithmetic and copies ran while one was open for 29% of the time, Pallas kernels for 6%

profile of v1, /device:TPU:0, one launch (start us, length us, event | category | flops | bytes accessed | tf_op | source)
XLA Modules:
  0.0 391.7 jit_solution(11625908630306516891)
XLA Ops:
  0.7 3.0 collective-permute-start.5
  4.2 2.0 constant_dynamic-slice_fusion.30
  20.9 1.9 collective-permute-start.11
  31.4 6.0 %collective-permute-done.11 = bf16[768,384]{0,1:T(8,128)(2,1)} collective-permute-done((bf16[768,384]{0,1:T(8,128)(2,1)}, bf16[768,384]{0,1:T(8,128)(2,1)}, u32[]{:S(2)}, u32[]{:S(2)}) %collective-permute-start.11) | collective-permute-done | bytes 589856 | tf_op jit(solution)/shard_map/ppermute | solution.py:392
  37.4 1.9 constant_dynamic-update-slice_fusion.17
  39.3 1.9 constant_dynamic-update-slice_fusion.16
  41.8 13.9 %collective-permute-done.2 = bf16[768,576]{0,1:T(8,128)(2,1)S(1)} collective-permute-done((bf16[768,576]{0,1:T(8,128)(2,1)}, bf16[768,576]{0,1:T(8,128)(2,1)S(1)}, u32[]{:S(2)}, u32[]{:S(2)}) %collective-permute-start.2) | collective-permute-done | bytes 884768 | tf_op jit(solution)/shard_map/ppermute | solution.py:392
  57.5 4.4 %convolution_convert_fusion.1 = bf16[1536,512]{1,0:T(8,128)(2,1)} fusion(bf16[768,1536]{0,1:T(8,128)(2,1)} %constant_dynamic-update-slice_fusion.15, bf16[256,768]{1,0:T(8,128)(2,1)S(1)} %bitcast.288, bf16[256,768]{1,0:T(8,128)(2,1)S(1)} %copy-done.36, pred[]{:T(512)S(6)} %eq.2), kind=kOutput, calls=%fused_computation.25 | convolution fusion | flops 1212284928 | bytes 4718593 | tf_op jit(solution)/shard_map/dot_general | solution.py:512
  62.6 5.3 %convolution_convert_fusion = bf16[2304,512]{1,0:T(8,128)(2,1)} fusion(bf16[768,2304]{0,1:T(8,128)(2,1)S(1)} %constant_dynamic-update-slice_fusion.3, f32[768]{0:T(1024)S(1)} %copy-done.62, f32[512]{0:T(512)S(1)} %add_rsqrt_fusion.2, bf16[256,768]{1,0:T(8,128)(2,1)} %bitcast.1, bf16[256,768]{1,0:T(8,128)(2,1)S(1)} %get-tuple-element.54, pred[]{:T(512)S(6)} %eq.2), kind=kOutput, calls=%fused_computation.2 | convolution fusion | flops 1818230784 | bytes 6689793 | tf_op jit(solution)/shard_map/dot_general | solution.py:512
  67.9 10.1 %shard_map.340 = (bf16[768,512]{1,0:T(8,128)(2,1)}, f32[4,8,512]{2,1,0:T(8,128)}) custom-call(s32[4]{0:T(128)} %bitcast.283, s32[1]{0:T(128)} %bitcast.3.refs_1_, bf16[4,576,512]{2,1,0:T(8,128)(2,1)} %bitcast.247, bf16[4,576,512]{2,1,0:T(8,128)(2,1)} %bitcast.248, bf16[4,576,512]{2,1,0:T(8,128)(2,1)} %bitcast.249, ...), custom_call_target="tpu_custom_call" | custom-call | flops 805306368 | bytes 7112212 | tf_op jit(solution)/shard_map/pallas_call | solution.py:306
  78.0 2.7 multiply_reduce_fusion.5
  84.2 12.6 %shard_map.341 = (bf16[768,512]{1,0:T(8,128)(2,1)}, f32[4,8,512]{2,1,0:T(8,128)}) custom-call(s32[4]{0:T(128)} %bitcast.284, s32[1]{0:T(128)} %bitcast.3.refs_1_, bf16[4,192,512]{2,1,0:T(8,128)(2,1)} %bitcast.297, bf16[4,384,512]{2,1,0:T(8,128)(2,1)} %bitcast.293, bf16[4,384,512]{2,1,0:T(8,128)(2,1)} %bitcast.294, ...), custom_call_target="tpu_custom_call" | custom-call | flops 805306368 | bytes 3934228 | tf_op jit(solution)/shard_map/pallas_call | solution.py:306
  96.8 3.1 multiply_reduce_fusion.4
  100.2 1.8 fusion.123
  102.7 1.8 fusion.124
  104.5 6.9 %multiply_convert_fusion = (bf16[512,2048]{1,0:T(8,128)(2,1)S(1)}, bf16[512,2048]{1,0:T(8,128)(2,1)S(1)}, bf16[512,2048]{1,0:T(8,128)(2,1)}) fusion(f32[512,2048]{1,0:T(8,128)S(1)} %fusion.123, f32[512,2048]{1,0:T(8,128)S(1)} %fusion.124, bf16[2048,768]{1,0:T(8,128)(2,1)S(1)} %copy-done, bf16[256,768]{1,0:T(8,128)(2,1)} %bitcast.18, ...), kind=kOutput, calls=%fused_computation.13 | convolution fusion | flops 1639317504 | bytes 18612224 | tf_op jit(solution)/shard_map/dot_general | solution.py:508
  111.5 1.8 fusion.125
  113.3 2.5 convolution_convert_fusion.4
  115.8 2.4 convolution_convert_fusion.2
  118.3 2.6 multiply_reduce_fusion
  126.4 12.7 %shard_map.342 = (bf16[4,192,512]{2,1,0:T(8,128)(2,1)}, bf16[4,384,512]{2,1,0:T(8,128)(2,1)}) custom-call(s32[4]{0:T(128)} %bitcast.285, s32[1]{0:T(128)} %bitcast.3.refs_1_, bf16[4,192,512]{2,1,0:T(8,128)(2,1)} %bitcast.298, bf16[4,384,512]{2,1,0:T(8,128)(2,1)} %bitcast.295, bf16[4,384,512]{2,1,0:T(8,128)(2,1)} %bitcast.296, ...), custom_call_target="tpu_custom_call" | custom-call | flops 2013265920 | bytes 5572628 | tf_op jit(solution)/shard_map/pallas_call | solution.py:306
  139.1 3.0 convolution_convert_fusion.18
  142.1 2.6 convolution_convert_fusion.20
  154.0 13.1 %shard_map.343 = (bf16[4,576,512]{2,1,0:T(8,128)(2,1)}, f32[4,32,128]{2,1,0:T(8,128)}) custom-call(s32[4]{0:T(128)} %bitcast.286, s32[1]{0:T(128)} %bitcast.3.refs_1_, bf16[4,576,512]{2,1,0:T(8,128)(2,1)} %bitcast.250, bf16[4,576,512]{2,1,0:T(8,128)(2,1)} %bitcast.251, bf16[4,576,512]{2,1,0:T(8,128)(2,1)} %bitcast.252, ...), custom_call_target="tpu_custom_call" | custom-call | flops 2013265920 | bytes 8750612 | tf_op jit(solution)/shard_map/pallas_call | solution.py:306
  167.0 3.0 convolution_convert_fusion.10
  170.0 3.1 convolution_convert_fusion.8
  173.1 2.7 add_convert_fusion.6
  175.8 3.4 convolution_convert_fusion.6
  182.7 5.4 %fusion.18 = (f32[768]{0:T(1024)S(1)}, f32[512]{0:T(512)S(1)}, f32[512,768]{1,0:T(8,128)S(1)}) fusion(f32[512]{0:T(512)S(1)} %copy-done.59, bf16[256,768]{1,0:T(8,128)(2,1)S(1)} %get-tuple-element.54, bf16[256,768]{1,0:T(8,128)(2,1)} %bitcast.1, pred[]{:T(512)S(6)} %eq.2, f32[768]{0:T(1024)S(1)} %copy-done.64, bf16[2304,512]{1,0:T(8,128)(2,1)} %bitcast.287, ...), kind=kOutput, calls=%fused_computation.43 | convolution fusion | flops 1818229504 | bytes 8267777 | tf_op jit(solution)/shard_map/dot_general | solution.py:655
  188.2 3.2 convolution_convert_fusion.15
  208.2 2.7 collective-permute-start.42
  210.8 2.0 collective-permute-start.22
  213.5 2.0 collective-permute-done.22
  222.9 4.1 %collective-permute-done.45 = bf16[768,192]{0,1:T(8,128)(2,1)S(1)} collective-permute-done((bf16[768,192]{0,1:T(8,128)(2,1)S(1)}, bf16[768,192]{0,1:T(8,128)(2,1)S(1)}, u32[]{:S(2)}, u32[]{:S(2)}) %collective-permute-start.45) | collective-permute-done | bytes 294944 | tf_op jit(solution)/shard_map/ppermute | solution.py:392
  228.8 2.3 reshape_reshape.20
  231.1 2.8 constant_dynamic-slice_fusion.20
  237.2 2.0 copy.100
  239.2 1.9 add_convert_fusion.7
  243.6 1.8 fusion.25
  247.8 2.2 collective-permute-start.48
  251.1 2.8 collective-permute-done.48
  253.9 2.0 collective-permute-done.49
  258.7 6.0 %collective-permute-done.31 = bf16[4,2,48,384]{3,2,1,0:T(8,128)(2,1)S(1)} collective-permute-done((bf16[4,2,48,384]{3,2,1,0:T(8,128)(2,1)S(1)}, bf16[4,2,48,384]{3,2,1,0:T(8,128)(2,1)S(1)}, u32[]{:S(2)}, u32[]{:S(2)}) %collective-permute-start.31) | collective-permute-done | bytes 294944 | tf_op jit(solution)/shard_map/ppermute | solution.py:392
  266.9 1.9 add_convert_fusion.5
  268.8 2.0 add_convert_fusion.4
  270.9 3.5 collective-permute-done.59
  276.2 2.8 collective-permute-start.62
  279.6 2.3 collective-permute-done.62
  282.0 3.4 collective-permute-start.34
  291.9 5.8 %collective-permute-done.53 = bf16[4,96,384]{2,1,0:T(8,128)(2,1)S(1)} collective-permute-done((bf16[4,96,384]{2,1,0:T(8,128)(2,1)S(1)}, bf16[4,96,384]{2,1,0:T(8,128)(2,1)S(1)}, u32[]{:S(2)}, u32[]{:S(2)}) %collective-permute-start.53) | collective-permute-done | bytes 294944 | tf_op jit(solution)/shard_map/ppermute | solution.py:392
  297.9 3.3 collective-permute-start.55
  303.2 3.3 collective-permute-done.55
  308.3 2.3 add_convert_fusion
  314.0 15.1 %collective-permute-done.25 = bf16[768,576]{0,1:T(8,128)(2,1)S(1)} collective-permute-done((bf16[768,576]{0,1:T(8,128)(2,1)S(1)}, bf16[768,576]{0,1:T(8,128)(2,1)S(1)}, u32[]{:S(2)}, u32[]{:S(2)}) %collective-permute-start.25) | collective-permute-done | bytes 884768 | tf_op jit(solution)/shard_map/ppermute | solution.py:392
  332.5 3.3 add_convert_fusion.2
  335.8 8.5 %collective-permute-done.26 = bf16[4,96,576]{2,1,0:T(8,128)(2,1)S(1)} collective-permute-done((bf16[4,96,576]{2,1,0:T(8,128)(2,1)S(1)}, bf16[4,96,576]{2,1,0:T(8,128)(2,1)S(1)}, u32[]{:S(2)}, u32[]{:S(2)}) %collective-permute-start.26) | collective-permute-done | bytes 442400 | tf_op jit(solution)/shard_map/ppermute | solution.py:392
  344.9 2.4 collective-permute-start.28
  352.0 2.1 collective-permute-done.29
  357.3 3.0 collective-permute-done.72
  366.5 1.9 collective-permute-start.82
  375.0 2.2 collective-permute-done.82
  377.3 2.0 collective-permute-start.67
  379.2 3.3 collective-permute-start.68
  385.2 4.0 %collective-permute-done.69 = bf16[1,128,384]{2,1,0:T(8,128)(2,1)S(1)} collective-permute-done((bf16[1,128,384]{2,1,0:T(8,128)(2,1)S(1)}, bf16[1,128,384]{2,1,0:T(8,128)(2,1)S(1)}, u32[]{:S(2)}, u32[]{:S(2)}) %collective-permute-start.69) | collective-permute-done | bytes 98336 | tf_op jit(solution)/shard_map/ppermute | solution.py:392
  (442 shorter events, 135.4 us)
Async XLA Ops:
  0.7 17.1 %collective-permute-start.5 = (f32[32,3]{0,1:T(4,128)}, f32[32,3]{0,1:T(4,128)}, u32[]{:S(2)}, u32[]{:S(2)}) collective-permute-start(f32[32,3]{0,1:T(4,128)} %param.31), channel_id=1, source_target_pairs={{0,2},{1,3},{2,0},{3,1},{4,6},{5,7},{6,4},{7,5},{8,10},{9,11},{10,... | collective-permute-start | bytes 1160 | tf_op jit(solution)/shard_map/ppermute | solution.py:392
  3.7 15.7 %collective-permute-start.4 = (f32[32,3]{0,1:T(4,128)}, f32[32,3]{0,1:T(4,128)}, u32[]{:S(2)}, u32[]{:S(2)}) collective-permute-start(f32[32,3]{0,1:T(4,128)} %param.31), channel_id=1, source_target_pairs={{0,1},{1,0},{2,3},{3,2},{4,5},{5,4},{6,7},{7,6},{8,9},{9,8},{10,11... | collective-permute-start | bytes 1160 | tf_op jit(solution)/shard_map/ppermute | solution.py:392
  3.7 20.4 %collective-permute-start.8 = (bf16[768,192]{0,1:T(8,128)(2,1)}, bf16[768,192]{0,1:T(8,128)(2,1)}, u32[]{:S(2)}, u32[]{:S(2)}) collective-permute-start(bf16[768,192]{0,1:T(8,128)(2,1)} %param.33), channel_id=1, source_target_pairs={{0,2},{1,3},{2,0},{3,1},{4,6},{5,7},{6,4},{7,5},{8,10},{9,11},{10,... | collective-permute-start | bytes 884744 | tf_op jit(solution)/shard_map/ppermute | solution.py:392
  3.9 21.8 %collective-permute-start.7 = (bf16[768,192]{0,1:T(8,128)(2,1)}, bf16[768,192]{0,1:T(8,128)(2,1)}, u32[]{:S(2)}, u32[]{:S(2)}) collective-permute-start(bf16[768,192]{0,1:T(8,128)(2,1)} %param.33), channel_id=1, source_target_pairs={{0,1},{1,0},{2,3},{3,2},{4,5},{5,4},{6,7},{7,6},{8,9},{9,8},{10,11... | collective-permute-start | bytes 884744 | tf_op jit(solution)/shard_map/ppermute | solution.py:392
  6.2 22.9 %collective-permute-start = (bf16[1,256,768]{2,1,0:T(8,128)(2,1)}, bf16[1,256,768]{2,1,0:T(8,128)(2,1)}, u32[]{:S(2)}, u32[]{:S(2)}) collective-permute-start(bf16[1,256,768]{2,1,0:T(8,128)(2,1)} %get-tuple-element.53), channel_id=1, source_target_pairs={{0,1},{1,0},{2,3},{3,2},{4,5},{5,4},{6,7},{7,6},{8,9},{9,8},{10,11... | collective-permute-start | bytes 1179656 | tf_op jit(solution)/shard_map/ppermute | solution.py:392
  19.4 11.8 %collective-permute-start.10 = (bf16[768,384]{0,1:T(8,128)(2,1)}, bf16[768,384]{0,1:T(8,128)(2,1)}, u32[]{:S(2)}, u32[]{:S(2)}) collective-permute-start(bf16[768,384]{0,1:T(8,128)(2,1)} %get-tuple-element.72), channel_id=1, source_target_pairs={{0,1},{1,0},{2,3},{3,2},{4,5},{5,4},{6,7},{7,6},{8,9},{9,8},{10,11... | collective-permute-start | bytes 1769480 | tf_op jit(solution)/shard_map/ppermute | solution.py:392
  20.9 16.5 %collective-permute-start.11 = (bf16[768,384]{0,1:T(8,128)(2,1)}, bf16[768,384]{0,1:T(8,128)(2,1)}, u32[]{:S(2)}, u32[]{:S(2)}) collective-permute-start(bf16[768,384]{0,1:T(8,128)(2,1)} %get-tuple-element.72), channel_id=1, source_target_pairs={{0,2},{1,3},{2,0},{3,1},{4,6},{5,7},{6,4},{7,5},{8,10},{9,11},{10,... | collective-permute-start | bytes 1769480 | tf_op jit(solution)/shard_map/ppermute | solution.py:392
  24.2 31.5 %collective-permute-start.2 = (bf16[768,576]{0,1:T(8,128)(2,1)}, bf16[768,576]{0,1:T(8,128)(2,1)S(1)}, u32[]{:S(2)}, u32[]{:S(2)}) collective-permute-start(bf16[768,576]{0,1:T(8,128)(2,1)} %copy-done.45), channel_id=1, source_target_pairs={{0,2},{1,3},{2,0},{3,1},{4,6},{5,7},{6,4},{7,5},{8,10},{9,11},{10,... | collective-permute-start | bytes 2654216 | tf_op jit(solution)/shard_map/ppermute | solution.py:392
  25.7 30.7 %collective-permute-start.1 = (bf16[768,576]{0,1:T(8,128)(2,1)}, bf16[768,576]{0,1:T(8,128)(2,1)S(1)}, u32[]{:S(2)}, u32[]{:S(2)}) collective-permute-start(bf16[768,576]{0,1:T(8,128)(2,1)} %copy-done.45), channel_id=1, source_target_pairs={{0,1},{1,0},{2,3},{3,2},{4,5},{5,4},{6,7},{7,6},{8,9},{9,8},{10,11... | collective-permute-start | bytes 2654216 | tf_op jit(solution)/shard_map/ppermute | solution.py:392
  29.1 12.1 %collective-permute-start.9 = (bf16[768,192]{0,1:T(8,128)(2,1)}, bf16[768,192]{0,1:T(8,128)(2,1)S(1)}, u32[]{:S(2)}, u32[]{:S(2)}) collective-permute-start(bf16[768,192]{0,1:T(8,128)(2,1)} %collective-permute-done.8), channel_id=1, source_target_pairs={{0,1},{1,0},{2,3},{3,2},{4,5},{5,4},{6,7},{7,6},{8,9},{9,8},{10,11... | collective-permute-start | bytes 884744 | tf_op jit(solution)/shard_map/ppermute | solution.py:392
  31.3 26.2 %collective-permute-start.13 = (bf16[1,256,768]{2,1,0:T(8,128)(2,1)S(1)}, bf16[1,256,768]{2,1,0:T(8,128)(2,1)S(1)}, u32[]{:S(2)}, u32[]{:S(2)}) collective-permute-start(bf16[1,256,768]{2,1,0:T(8,128)(2,1)S(1)} %copy-done.39), channel_id=1, source_target_pairs={{0,1},{1,0},{2,3},{3,2},{4,5},{5,4},{6,7},{7,6},{8,9},{9,8},{10,11... | collective-permute-start | bytes 1179656 | tf_op jit(solution)/shard_map/ppermute | solution.py:392
  37.4 19.2 %collective-permute-start.12 = (bf16[768,384]{0,1:T(8,128)(2,1)}, bf16[768,384]{0,1:T(8,128)(2,1)S(1)}, u32[]{:S(2)}, u32[]{:S(2)}) collective-permute-start(bf16[768,384]{0,1:T(8,128)(2,1)} %collective-permute-done.11), channel_id=1, source_target_pairs={{0,1},{1,0},{2,3},{3,2},{4,5},{5,4},{6,7},{7,6},{8,9},{9,8},{10,11... | collective-permute-start | bytes 1769480 | tf_op jit(solution)/shard_map/ppermute | solution.py:392
  41.3 63.2 %collective-permute-start.15 = (bf16[1,256,768]{2,1,0:T(8,128)(2,1)}, bf16[1,256,768]{2,1,0:T(8,128)(2,1)}, u32[]{:S(2)}, u32[]{:S(2)}) collective-permute-start(bf16[1,256,768]{2,1,0:T(8,128)(2,1)} %get-tuple-element.48), channel_id=1, source_target_pairs={{0,1},{1,0},{2,3},{3,2},{4,5},{5,4},{6,7},{7,6},{8,9},{9,8},{10,11... | collective-permute-start | bytes 1179656 | tf_op jit(solution)/shard_map/ppermute | solution.py:392
  55.7 6.2 %collective-permute-start.3 = (bf16[768,576]{0,1:T(8,128)(2,1)S(1)}, bf16[768,576]{0,1:T(8,128)(2,1)S(1)}, u32[]{:S(2)}, u32[]{:S(2)}) collective-permute-start(bf16[768,576]{0,1:T(8,128)(2,1)S(1)} %collective-permute-done.2), channel_id=1, source_target_pairs={{0,1},{1,0},{2,3},{3,2},{4,5},{5,4},{6,7},{7,6},{8,9},{9,8},{10,11... | collective-permute-start | bytes 2654216 | tf_op jit(solution)/shard_map/ppermute | solution.py:392
  179.2 60.0 %collective-permute-start.57 = (bf16[768,384]{1,0:T(8,128)(2,1)}, bf16[768,384]{1,0:T(8,128)(2,1)}, u32[]{:S(2)}, u32[]{:S(2)}) collective-permute-start(bf16[768,384]{1,0:T(8,128)(2,1)} %convolution_convert_fusion.16), channel_id=1, source_target_pairs={{0,1},{1,0},{2,3},{3,2},{4,5},{5,4},{6,7},{7,6},{8,9},{9,8},{10,11... | collective-permute-start | bytes 1769480 | tf_op jit(solution)/shard_map/ppermute | solution.py:392
  179.7 43.2 %collective-permute-start.43 = (bf16[768,192]{0,1:T(8,128)(2,1)}, bf16[768,192]{0,1:T(8,128)(2,1)}, u32[]{:S(2)}, u32[]{:S(2)}) collective-permute-start(bf16[768,192]{0,1:T(8,128)(2,1)} %convolution_convert_fusion.26), channel_id=1, source_target_pairs={{0,1},{1,0},{2,3},{3,2},{4,5},{5,4},{6,7},{7,6},{8,9},{9,8},{10,11... | collective-permute-start | bytes 884744 | tf_op jit(solution)/shard_map/ppermute | solution.py:392
  179.7 36.4 %collective-permute-start.44 = (bf16[768,192]{0,1:T(8,128)(2,1)}, bf16[768,192]{0,1:T(8,128)(2,1)}, u32[]{:S(2)}, u32[]{:S(2)}) collective-permute-start(bf16[768,192]{0,1:T(8,128)(2,1)} %convolution_convert_fusion.24), channel_id=1, source_target_pairs={{0,1},{1,0},{2,3},{3,2},{4,5},{5,4},{6,7},{7,6},{8,9},{9,8},{10,11... | collective-permute-start | bytes 884744 | tf_op jit(solution)/shard_map/ppermute | solution.py:392
  180.9 13.5 %collective-permute-start.38 = (f32[32,3]{0,1:T(4,128)}, f32[32,3]{0,1:T(4,128)}, u32[]{:S(2)}, u32[]{:S(2)}) collective-permute-start(f32[32,3]{0,1:T(4,128)} %bitcast.51), channel_id=1, source_target_pairs={{0,1},{1,0},{2,3},{3,2},{4,5},{5,4},{6,7},{7,6},{8,9},{9,8},{10,11... | collective-permute-start | bytes 1160 | tf_op jit(solution)/shard_map/ppermute | solution.py:392
  182.2 16.0 %collective-permute-start.37 = (f32[32,3]{0,1:T(4,128)}, f32[32,3]{0,1:T(4,128)}, u32[]{:S(2)}, u32[]{:S(2)}) collective-permute-start(f32[32,3]{0,1:T(4,128)} %bitcast.49), channel_id=1, source_target_pairs={{0,1},{1,0},{2,3},{3,2},{4,5},{5,4},{6,7},{7,6},{8,9},{9,8},{10,11... | collective-permute-start | bytes 1160 | tf_op jit(solution)/shard_map/ppermute | solution.py:392
  218.0 9.0 %collective-permute-start.45 = (bf16[768,192]{0,1:T(8,128)(2,1)S(1)}, bf16[768,192]{0,1:T(8,128)(2,1)S(1)}, u32[]{:S(2)}, u32[]{:S(2)}) collective-permute-start(bf16[768,192]{0,1:T(8,128)(2,1)S(1)} %add_convert_fusion.10), channel_id=1, source_target_pairs={{0,2},{1,3},{2,0},{3,1},{4,6},{5,7},{6,4},{7,5},{8,10},{9,11},{10,... | collective-permute-start | bytes 884744 | tf_op jit(solution)/shard_map/ppermute | solution.py:392
  220.4 23.2 %collective-permute-start.51 = (bf16[768,384]{1,0:T(8,128)(2,1)}, bf16[768,384]{1,0:T(8,128)(2,1)}, u32[]{:S(2)}, u32[]{:S(2)}) collective-permute-start(bf16[768,384]{1,0:T(8,128)(2,1)} %convolution_convert_fusion.18), channel_id=1, source_target_pairs={{0,1},{1,0},{2,3},{3,2},{4,5},{5,4},{6,7},{7,6},{8,9},{9,8},{10,11... | collective-permute-start | bytes 1769480 | tf_op jit(solution)/shard_map/ppermute | solution.py:392
  221.4 60.6 %collective-permute-start.50 = (bf16[768,384]{1,0:T(8,128)(2,1)}, bf16[768,384]{1,0:T(8,128)(2,1)}, u32[]{:S(2)}, u32[]{:S(2)}) collective-permute-start(bf16[768,384]{1,0:T(8,128)(2,1)} %convolution_convert_fusion.20), channel_id=1, source_target_pairs={{0,1},{1,0},{2,3},{3,2},{4,5},{5,4},{6,7},{7,6},{8,9},{9,8},{10,11... | collective-permute-start | bytes 1769480 | tf_op jit(solution)/shard_map/ppermute | solution.py:392
  222.9 18.9 %collective-permute-start.30 = (bf16[768,384]{1,0:T(8,128)(2,1)}, bf16[768,384]{1,0:T(8,128)(2,1)}, u32[]{:S(2)}, u32[]{:S(2)}) collective-permute-start(bf16[768,384]{1,0:T(8,128)(2,1)} %convolution_convert_fusion.22), channel_id=1, source_target_pairs={{0,1},{1,0},{2,3},{3,2},{4,5},{5,4},{6,7},{7,6},{8,9},{9,8},{10,11... | collective-permute-start | bytes 1769480 | tf_op jit(solution)/shard_map/ppermute | solution.py:392
  235.7 9.8 %collective-permute-start.46 = (bf16[4,96,192]{2,1,0:T(8,128)(2,1)}, bf16[4,96,192]{2,1,0:T(8,128)(2,1)}, u32[]{:S(2)}, u32[]{:S(2)}) collective-permute-start(bf16[4,96,192]{2,1,0:T(8,128)(2,1)} %bitcast.281), channel_id=1, source_target_pairs={{0,4},{4,0},{8,12},{12,8},{16,20},{20,16},{24,28},{28,24},{1,5},{5... | collective-permute-start | bytes 442376 | tf_op jit(solution)/shard_map/ppermute | solution.py:392
  241.2 16.6 %collective-permute-start.58 = (bf16[4,2,48,384]{3,2,1,0:T(8,128)(2,1)S(1)}, bf16[4,2,48,384]{3,2,1,0:T(8,128)(2,1)S(1)}, u32[]{:S(2)}, u32[]{:S(2)}) collective-permute-start(bf16[4,2,48,384]{3,2,1,0:T(8,128)(2,1)S(1)} %dynamic-slice_bitcast_fusion.16), channel_id=1, source_target_pairs={{0,4},{4,0},{8,12},{12,8},{16,20},{20,16},{24,28},{28,24},{1,5},{5... | collective-permute-start | bytes 884744 | tf_op jit(solution)/shard_map/ppermute | solution.py:392
  247.8 6.0 %collective-permute-start.48 = (bf16[1,96,192]{2,1,0:T(8,128)(2,1)S(1)}, bf16[1,96,192]{2,1,0:T(8,128)(2,1)S(1)}, u32[]{:S(2)}, u32[]{:S(2)}) collective-permute-start(bf16[1,96,192]{2,1,0:T(8,128)(2,1)S(1)} %get-tuple-element.93), channel_id=1, source_target_pairs={{0,16},{4,20},{8,24},{12,28},{16,0},{20,4},{24,8},{28,12},{1,17},{... | collective-permute-start | bytes 110600 | tf_op jit(solution)/shard_map/ppermute | solution.py:392
  250.0 5.9 %collective-permute-start.49 = (bf16[1,96,192]{2,1,0:T(8,128)(2,1)S(1)}, bf16[1,96,192]{2,1,0:T(8,128)(2,1)S(1)}, u32[]{:S(2)}, u32[]{:S(2)}) collective-permute-start(bf16[1,96,192]{2,1,0:T(8,128)(2,1)S(1)} %get-tuple-element.92), channel_id=1, source_target_pairs={{0,24},{4,28},{8,16},{12,20},{16,8},{20,12},{24,0},{28,4},{1,25},{... | collective-permute-start | bytes 110600 | tf_op jit(solution)/shard_map/ppermute | solution.py:392
  251.0 14.9 %collective-permute-start.23 = (bf16[768,576]{0,1:T(8,128)(2,1)S(1)}, bf16[768,576]{0,1:T(8,128)(2,1)S(1)}, u32[]{:S(2)}, u32[]{:S(2)}) collective-permute-start(bf16[768,576]{0,1:T(8,128)(2,1)S(1)} %copy-done.76), channel_id=1, source_target_pairs={{0,1},{1,0},{2,3},{3,2},{4,5},{5,4},{6,7},{7,6},{8,9},{9,8},{10,11... | collective-permute-start | bytes 2654216 | tf_op jit(solution)/shard_map/ppermute | solution.py:392
  253.9 14.9 %collective-permute-start.24 = (bf16[768,576]{0,1:T(8,128)(2,1)S(1)}, bf16[768,576]{0,1:T(8,128)(2,1)S(1)}, u32[]{:S(2)}, u32[]{:S(2)}) collective-permute-start(bf16[768,576]{0,1:T(8,128)(2,1)S(1)} %copy-done.75), channel_id=1, source_target_pairs={{0,1},{1,0},{2,3},{3,2},{4,5},{5,4},{6,7},{7,6},{8,9},{9,8},{10,11... | collective-permute-start | bytes 2654216 | tf_op jit(solution)/shard_map/ppermute | solution.py:392
  255.9 29.5 %collective-permute-start.52 = (bf16[768,384]{1,0:T(8,128)(2,1)S(1)}, bf16[768,384]{1,0:T(8,128)(2,1)S(1)}, u32[]{:S(2)}, u32[]{:S(2)}) collective-permute-start(bf16[768,384]{1,0:T(8,128)(2,1)S(1)} %fusion.25), channel_id=1, source_target_pairs={{0,2},{1,3},{2,0},{3,1},{4,6},{5,7},{6,4},{7,5},{8,10},{9,11},{10,... | collective-permute-start | bytes 1769480 | tf_op jit(solution)/shard_map/ppermute | solution.py:392
  257.8 6.9 %collective-permute-start.31 = (bf16[4,2,48,384]{3,2,1,0:T(8,128)(2,1)S(1)}, bf16[4,2,48,384]{3,2,1,0:T(8,128)(2,1)S(1)}, u32[]{:S(2)}, u32[]{:S(2)}) collective-permute-start(bf16[4,2,48,384]{3,2,1,0:T(8,128)(2,1)S(1)} %dynamic-slice_bitcast_fusion.18), channel_id=1, source_target_pairs={{0,4},{4,0},{8,12},{12,8},{16,20},{20,16},{24,28},{28,24},{1,5},{5... | collective-permute-start | bytes 884744 | tf_op jit(solution)/shard_map/ppermute | solution.py:392
  264.7 9.7 %collective-permute-start.59 = (bf16[4,48,384]{2,1,0:T(8,128)(2,1)S(1)}, bf16[4,48,384]{2,1,0:T(8,128)(2,1)S(1)}, u32[]{:S(2)}, u32[]{:S(2)}) collective-permute-start(bf16[4,48,384]{2,1,0:T(8,128)(2,1)S(1)} %dynamic-slice_bitcast_fusion.19), channel_id=1, source_target_pairs={{0,2},{1,3},{2,0},{3,1},{4,6},{5,7},{6,4},{7,5},{8,10},{9,11},{10,... | collective-permute-start | bytes 442376 | tf_op jit(solution)/shard_map/ppermute | solution.py:392
  265.9 10.3 %collective-permute-start.32 = (bf16[4,48,384]{2,1,0:T(8,128)(2,1)S(1)}, bf16[4,48,384]{2,1,0:T(8,128)(2,1)S(1)}, u32[]{:S(2)}, u32[]{:S(2)}) collective-permute-start(bf16[4,48,384]{2,1,0:T(8,128)(2,1)S(1)} %dynamic-slice_bitcast_fusion.20), channel_id=1, source_target_pairs={{0,2},{1,3},{2,0},{3,1},{4,6},{5,7},{6,4},{7,5},{8,10},{9,11},{10,... | collective-permute-start | bytes 442376 | tf_op jit(solution)/shard_map/ppermute | solution.py:392
  276.2 5.8 %collective-permute-start.62 = (bf16[1,48,384]{2,1,0:T(8,128)(2,1)S(1)}, bf16[1,48,384]{2,1,0:T(8,128)(2,1)S(1)}, u32[]{:S(2)}, u32[]{:S(2)}) collective-permute-start(bf16[1,48,384]{2,1,0:T(8,128)(2,1)S(1)} %get-tuple-element.95), channel_id=1, source_target_pairs={{0,24},{4,28},{8,16},{12,20},{16,8},{20,12},{24,0},{28,4},{1,25},{... | collective-permute-start | bytes 110600 | tf_op jit(solution)/shard_map/ppermute | solution.py:392
  279.0 29.3 %collective-permute-start.78 = (bf16[768,1024]{1,0:T(8,128)(2,1)S(1)}, bf16[768,1024]{1,0:T(8,128)(2,1)S(1)}, u32[]{:S(2)}, u32[]{:S(2)}) collective-permute-start(bf16[768,1024]{1,0:T(8,128)(2,1)S(1)} %copy-done.73), channel_id=1, source_target_pairs={{0,1},{1,0},{2,3},{3,2},{4,5},{5,4},{6,7},{7,6},{8,9},{9,8},{10,11... | collective-permute-start | bytes 4718600 | tf_op jit(solution)/shard_map/ppermute | solution.py:392
  279.5 33.2 %collective-permute-start.71 = (bf16[2048,384]{1,0:T(8,128)(2,1)S(1)}, bf16[2048,384]{1,0:T(8,128)(2,1)S(1)}, u32[]{:S(2)}, u32[]{:S(2)}) collective-permute-start(bf16[2048,384]{1,0:T(8,128)(2,1)S(1)} %copy-done.72), channel_id=1, source_target_pairs={{0,1},{1,0},{2,3},{3,2},{4,5},{5,4},{6,7},{7,6},{8,9},{9,8},{10,11... | collective-permute-start | bytes 4718600 | tf_op jit(solution)/shard_map/ppermute | solution.py:392
  281.9 6.3 %collective-permute-start.33 = (bf16[1,48,384]{2,1,0:T(8,128)(2,1)S(1)}, bf16[1,48,384]{2,1,0:T(8,128)(2,1)S(1)}, u32[]{:S(2)}, u32[]{:S(2)}) collective-permute-start(bf16[1,48,384]{2,1,0:T(8,128)(2,1)S(1)} %get-tuple-element.99), channel_id=1, source_target_pairs={{0,8},{4,12},{8,0},{12,4},{16,24},{20,28},{24,16},{28,20},{1,9},{5... | collective-permute-start | bytes 110600 | tf_op jit(solution)/shard_map/ppermute | solution.py:392
  282.0 6.3 %collective-permute-start.34 = (bf16[1,48,384]{2,1,0:T(8,128)(2,1)S(1)}, bf16[1,48,384]{2,1,0:T(8,128)(2,1)S(1)}, u32[]{:S(2)}, u32[]{:S(2)}) collective-permute-start(bf16[1,48,384]{2,1,0:T(8,128)(2,1)S(1)} %get-tuple-element.101), channel_id=1, source_target_pairs={{0,16},{4,20},{8,24},{12,28},{16,0},{20,4},{24,8},{28,12},{1,17},{... | collective-permute-start | bytes 110600 | tf_op jit(solution)/shard_map/ppermute | solution.py:392
  285.4 5.8 %collective-permute-start.35 = (bf16[1,48,384]{2,1,0:T(8,128)(2,1)S(1)}, bf16[1,48,384]{2,1,0:T(8,128)(2,1)S(1)}, u32[]{:S(2)}, u32[]{:S(2)}) collective-permute-start(bf16[1,48,384]{2,1,0:T(8,128)(2,1)S(1)} %get-tuple-element.100), channel_id=1, source_target_pairs={{0,24},{4,28},{8,16},{12,20},{16,8},{20,12},{24,0},{28,4},{1,25},{... | collective-permute-start | bytes 110600 | tf_op jit(solution)/shard_map/ppermute | solution.py:392
  288.3 9.4 %collective-permute-start.53 = (bf16[4,96,384]{2,1,0:T(8,128)(2,1)S(1)}, bf16[4,96,384]{2,1,0:T(8,128)(2,1)S(1)}, u32[]{:S(2)}, u32[]{:S(2)}) collective-permute-start(bf16[4,96,384]{2,1,0:T(8,128)(2,1)S(1)} %dynamic-slice_bitcast_fusion.17), channel_id=1, source_target_pairs={{0,4},{4,0},{8,12},{12,8},{16,20},{20,16},{24,28},{28,24},{1,5},{5... | collective-permute-start | bytes 884744 | tf_op jit(solution)/shard_map/ppermute | solution.py:392
  291.2 10.1 %collective-permute-start.36 = (f32[24,384]{1,0:T(8,128)S(1)}, f32[24,384]{1,0:T(8,128)S(1)}, u32[]{:S(2)}, u32[]{:S(2)}) collective-permute-start(f32[24,384]{1,0:T(8,128)S(1)} %get-tuple-element.105), channel_id=1, source_target_pairs={{0,1},{1,0},{2,3},{3,2},{4,5},{5,4},{6,7},{7,6},{8,9},{9,8},{10,11... | collective-permute-start | bytes 110600 | tf_op jit(solution)/shard_map/ppermute | solution.py:392
  297.9 8.5 %collective-permute-start.55 = (bf16[1,96,384]{2,1,0:T(8,128)(2,1)S(1)}, bf16[1,96,384]{2,1,0:T(8,128)(2,1)S(1)}, u32[]{:S(2)}, u32[]{:S(2)}) collective-permute-start(bf16[1,96,384]{2,1,0:T(8,128)(2,1)S(1)} %get-tuple-element.71), channel_id=1, source_target_pairs={{0,16},{4,20},{8,24},{12,28},{16,0},{20,4},{24,8},{28,12},{1,17},{... | collective-permute-start | bytes 221192 | tf_op jit(solution)/shard_map/ppermute | solution.py:392
  301.3 6.3 %collective-permute-start.56 = (bf16[1,96,384]{2,1,0:T(8,128)(2,1)S(1)}, bf16[1,96,384]{2,1,0:T(8,128)(2,1)S(1)}, u32[]{:S(2)}, u32[]{:S(2)}) collective-permute-start(bf16[1,96,384]{2,1,0:T(8,128)(2,1)S(1)} %get-tuple-element.70), channel_id=1, source_target_pairs={{0,24},{4,28},{8,16},{12,20},{16,8},{20,12},{24,0},{28,4},{1,25},{... | collective-permute-start | bytes 221192 | tf_op jit(solution)/shard_map/ppermute | solution.py:392
  303.2 29.3 %collective-permute-start.64 = (bf16[2048,384]{1,0:T(8,128)(2,1)}, bf16[2048,384]{1,0:T(8,128)(2,1)}, u32[]{:S(2)}, u32[]{:S(2)}) collective-permute-start(bf16[2048,384]{1,0:T(8,128)(2,1)} %convolution_convert_fusion.4), channel_id=1, source_target_pairs={{0,1},{1,0},{2,3},{3,2},{4,5},{5,4},{6,7},{7,6},{8,9},{9,8},{10,11... | collective-permute-start | bytes 4718600 | tf_op jit(solution)/shard_map/ppermute | solution.py:392
  306.5 22.6 %collective-permute-start.25 = (bf16[768,576]{0,1:T(8,128)(2,1)S(1)}, bf16[768,576]{0,1:T(8,128)(2,1)S(1)}, u32[]{:S(2)}, u32[]{:S(2)}) collective-permute-start(bf16[768,576]{0,1:T(8,128)(2,1)S(1)} %add_convert_fusion.4), channel_id=1, source_target_pairs={{0,2},{1,3},{2,0},{3,1},{4,6},{5,7},{6,4},{7,5},{8,10},{9,11},{10,... | collective-permute-start | bytes 2654216 | tf_op jit(solution)/shard_map/ppermute | solution.py:392
  311.6 43.3 %collective-permute-start.79 = (bf16[8,48,1024]{2,1,0:T(8,128)(2,1)}, bf16[8,48,1024]{2,1,0:T(8,128)(2,1)}, u32[]{:S(2)}, u32[]{:S(2)}) collective-permute-start(bf16[8,48,1024]{2,1,0:T(8,128)(2,1)} %dynamic-slice_bitcast_fusion), channel_id=1, source_target_pairs={{0,2},{1,3},{2,0},{3,1},{4,6},{5,7},{6,4},{7,5},{8,10},{9,11},{10,... | collective-permute-start | bytes 2359304 | tf_op jit(solution)/shard_map/ppermute | solution.py:392
  330.2 14.1 %collective-permute-start.26 = (bf16[4,96,576]{2,1,0:T(8,128)(2,1)S(1)}, bf16[4,96,576]{2,1,0:T(8,128)(2,1)S(1)}, u32[]{:S(2)}, u32[]{:S(2)}) collective-permute-start(bf16[4,96,576]{2,1,0:T(8,128)(2,1)S(1)} %dynamic-slice_bitcast_fusion.3), channel_id=1, source_target_pairs={{0,4},{4,0},{8,12},{12,8},{16,20},{20,16},{24,28},{28,24},{1,5},{5... | collective-permute-start | bytes 1327112 | tf_op jit(solution)/shard_map/ppermute | solution.py:392
  332.0 28.3 %collective-permute-start.72 = (bf16[4,2,128,384]{3,2,1,0:T(8,128)(2,1)S(1)}, bf16[4,2,128,384]{3,2,1,0:T(8,128)(2,1)S(1)}, u32[]{:S(2)}, u32[]{:S(2)}) collective-permute-start(bf16[4,2,128,384]{3,2,1,0:T(8,128)(2,1)S(1)} %dynamic-slice_bitcast_fusion.1), channel_id=1, source_target_pairs={{0,4},{4,0},{8,12},{12,8},{16,20},{20,16},{24,28},{28,24},{1,5},{5... | collective-permute-start | bytes 2359304 | tf_op jit(solution)/shard_map/ppermute | solution.py:392
  344.9 7.1 %collective-permute-start.28 = (bf16[1,96,576]{2,1,0:T(8,128)(2,1)S(1)}, bf16[1,96,576]{2,1,0:T(8,128)(2,1)S(1)}, u32[]{:S(2)}, u32[]{:S(2)}) collective-permute-start(bf16[1,96,576]{2,1,0:T(8,128)(2,1)S(1)} %get-tuple-element.57), channel_id=1, source_target_pairs={{0,16},{4,20},{8,24},{12,28},{16,0},{20,4},{24,8},{28,12},{1,17},{... | collective-permute-start | bytes 331784 | tf_op jit(solution)/shard_map/ppermute | solution.py:392
  347.3 6.8 %collective-permute-start.29 = (bf16[1,96,576]{2,1,0:T(8,128)(2,1)S(1)}, bf16[1,96,576]{2,1,0:T(8,128)(2,1)S(1)}, u32[]{:S(2)}, u32[]{:S(2)}) collective-permute-start(bf16[1,96,576]{2,1,0:T(8,128)(2,1)S(1)} %get-tuple-element.56), channel_id=1, source_target_pairs={{0,24},{4,28},{8,16},{12,20},{16,8},{20,12},{24,0},{28,4},{1,25},{... | collective-permute-start | bytes 331784 | tf_op jit(solution)/shard_map/ppermute | solution.py:392
  349.5 13.7 %collective-permute-start.65 = (bf16[8,128,384]{2,1,0:T(8,128)(2,1)S(1)}, bf16[8,128,384]{2,1,0:T(8,128)(2,1)S(1)}, u32[]{:S(2)}, u32[]{:S(2)}) collective-permute-start(bf16[8,128,384]{2,1,0:T(8,128)(2,1)S(1)} %dynamic-slice_bitcast_fusion.2), channel_id=1, source_target_pairs={{0,2},{1,3},{2,0},{3,1},{4,6},{5,7},{6,4},{7,5},{8,10},{9,11},{10,... | collective-permute-start | bytes 2359304 | tf_op jit(solution)/shard_map/ppermute | solution.py:392
  356.6 8.8 %collective-permute-start.80 = (bf16[4,48,1024]{2,1,0:T(8,128)(2,1)S(1)}, bf16[4,48,1024]{2,1,0:T(8,128)(2,1)S(1)}, u32[]{:S(2)}, u32[]{:S(2)}) collective-permute-start(bf16[4,48,1024]{2,1,0:T(8,128)(2,1)S(1)} %dynamic-slice_bitcast_fusion.4), channel_id=1, source_target_pairs={{0,4},{4,0},{8,12},{12,8},{16,20},{20,16},{24,28},{28,24},{1,5},{5... | collective-permute-start | bytes 1179656 | tf_op jit(solution)/shard_map/ppermute | solution.py:392
  360.6 9.4 %collective-permute-start.73 = (bf16[4,128,384]{2,1,0:T(8,128)(2,1)S(1)}, bf16[4,128,384]{2,1,0:T(8,128)(2,1)S(1)}, u32[]{:S(2)}, u32[]{:S(2)}) collective-permute-start(bf16[4,128,384]{2,1,0:T(8,128)(2,1)S(1)} %dynamic-slice_bitcast_fusion.5), channel_id=1, source_target_pairs={{0,2},{1,3},{2,0},{3,1},{4,6},{5,7},{6,4},{7,5},{8,10},{9,11},{10,... | collective-permute-start | bytes 1179656 | tf_op jit(solution)/shard_map/ppermute | solution.py:392
  363.4 7.8 %collective-permute-start.66 = (bf16[4,128,384]{2,1,0:T(8,128)(2,1)S(1)}, bf16[4,128,384]{2,1,0:T(8,128)(2,1)S(1)}, u32[]{:S(2)}, u32[]{:S(2)}) collective-permute-start(bf16[4,128,384]{2,1,0:T(8,128)(2,1)S(1)} %dynamic-slice_bitcast_fusion.6), channel_id=1, source_target_pairs={{0,4},{4,0},{8,12},{12,8},{16,20},{20,16},{24,28},{28,24},{1,5},{5... | collective-permute-start | bytes 1179656 | tf_op jit(solution)/shard_map/ppermute | solution.py:392
  365.6 7.7 %collective-permute-start.81 = (bf16[1,48,1024]{2,1,0:T(8,128)(2,1)S(1)}, bf16[1,48,1024]{2,1,0:T(8,128)(2,1)S(1)}, u32[]{:S(2)}, u32[]{:S(2)}) collective-permute-start(bf16[1,48,1024]{2,1,0:T(8,128)(2,1)S(1)} %get-tuple-element.58), channel_id=1, source_target_pairs={{0,8},{4,12},{8,0},{12,4},{16,24},{20,28},{24,16},{28,20},{1,9},{5... | collective-permute-start | bytes 294920 | tf_op jit(solution)/shard_map/ppermute | solution.py:392
  366.5 10.8 %collective-permute-start.82 = (bf16[1,48,1024]{2,1,0:T(8,128)(2,1)S(1)}, bf16[1,48,1024]{2,1,0:T(8,128)(2,1)S(1)}, u32[]{:S(2)}, u32[]{:S(2)}) collective-permute-start(bf16[1,48,1024]{2,1,0:T(8,128)(2,1)S(1)} %get-tuple-element.60), channel_id=1, source_target_pairs={{0,16},{4,20},{8,24},{12,28},{16,0},{20,4},{24,8},{28,12},{1,17},{... | collective-permute-start | bytes 294920 | tf_op jit(solution)/shard_map/ppermute | solution.py:392
  368.4 10.9 %collective-permute-start.83 = (bf16[1,48,1024]{2,1,0:T(8,128)(2,1)S(1)}, bf16[1,48,1024]{2,1,0:T(8,128)(2,1)S(1)}, u32[]{:S(2)}, u32[]{:S(2)}) collective-permute-start(bf16[1,48,1024]{2,1,0:T(8,128)(2,1)S(1)} %get-tuple-element.59), channel_id=1, source_target_pairs={{0,24},{4,28},{8,16},{12,20},{16,8},{20,12},{24,0},{28,4},{1,25},{... | collective-permute-start | bytes 294920 | tf_op jit(solution)/shard_map/ppermute | solution.py:392
  370.2 12.5 %collective-permute-start.74 = (bf16[1,128,384]{2,1,0:T(8,128)(2,1)S(1)}, bf16[1,128,384]{2,1,0:T(8,128)(2,1)S(1)}, u32[]{:S(2)}, u32[]{:S(2)}) collective-permute-start(bf16[1,128,384]{2,1,0:T(8,128)(2,1)S(1)} %get-tuple-element.61), channel_id=1, source_target_pairs={{0,8},{4,12},{8,0},{12,4},{16,24},{20,28},{24,16},{28,20},{1,9},{5... | collective-permute-start | bytes 294920 | tf_op jit(solution)/shard_map/ppermute | solution.py:392
  371.2 13.0 %collective-permute-start.75 = (bf16[1,128,384]{2,1,0:T(8,128)(2,1)S(1)}, bf16[1,128,384]{2,1,0:T(8,128)(2,1)S(1)}, u32[]{:S(2)}, u32[]{:S(2)}) collective-permute-start(bf16[1,128,384]{2,1,0:T(8,128)(2,1)S(1)} %get-tuple-element.63), channel_id=1, source_target_pairs={{0,16},{4,20},{8,24},{12,28},{16,0},{20,4},{24,8},{28,12},{1,17},{... | collective-permute-start | bytes 294920 | tf_op jit(solution)/shard_map/ppermute | solution.py:392
  373.3 11.0 %collective-permute-start.76 = (bf16[1,128,384]{2,1,0:T(8,128)(2,1)S(1)}, bf16[1,128,384]{2,1,0:T(8,128)(2,1)S(1)}, u32[]{:S(2)}, u32[]{:S(2)}) collective-permute-start(bf16[1,128,384]{2,1,0:T(8,128)(2,1)S(1)} %get-tuple-element.62), channel_id=1, source_target_pairs={{0,24},{4,28},{8,16},{12,20},{16,8},{20,12},{24,0},{28,4},{1,25},{... | collective-permute-start | bytes 294920 | tf_op jit(solution)/shard_map/ppermute | solution.py:392
  377.3 7.7 %collective-permute-start.67 = (bf16[1,128,384]{2,1,0:T(8,128)(2,1)S(1)}, bf16[1,128,384]{2,1,0:T(8,128)(2,1)S(1)}, u32[]{:S(2)}, u32[]{:S(2)}) collective-permute-start(bf16[1,128,384]{2,1,0:T(8,128)(2,1)S(1)} %get-tuple-element.64), channel_id=1, source_target_pairs={{0,8},{4,12},{8,0},{12,4},{16,24},{20,28},{24,16},{28,20},{1,9},{5... | collective-permute-start | bytes 294920 | tf_op jit(solution)/shard_map/ppermute | solution.py:392
  379.2 5.9 %collective-permute-start.68 = (bf16[1,128,384]{2,1,0:T(8,128)(2,1)S(1)}, bf16[1,128,384]{2,1,0:T(8,128)(2,1)S(1)}, u32[]{:S(2)}, u32[]{:S(2)}) collective-permute-start(bf16[1,128,384]{2,1,0:T(8,128)(2,1)S(1)} %get-tuple-element.66), channel_id=1, source_target_pairs={{0,16},{4,20},{8,24},{12,28},{16,0},{20,4},{24,8},{28,12},{1,17},{... | collective-permute-start | bytes 294920 | tf_op jit(solution)/shard_map/ppermute | solution.py:392
  382.7 6.5 %collective-permute-start.69 = (bf16[1,128,384]{2,1,0:T(8,128)(2,1)S(1)}, bf16[1,128,384]{2,1,0:T(8,128)(2,1)S(1)}, u32[]{:S(2)}, u32[]{:S(2)}) collective-permute-start(bf16[1,128,384]{2,1,0:T(8,128)(2,1)S(1)} %get-tuple-element.65), channel_id=1, source_target_pairs={{0,24},{4,28},{8,16},{12,20},{16,8},{20,12},{24,0},{28,4},{1,25},{... | collective-permute-start | bytes 294920 | tf_op jit(solution)/shard_map/ppermute | solution.py:392
  384.4 5.6 %collective-permute-start.77 = (f32[64,384]{1,0:T(8,128)S(1)}, f32[64,384]{1,0:T(8,128)S(1)}, u32[]{:S(2)}, u32[]{:S(2)}) collective-permute-start(f32[64,384]{1,0:T(8,128)S(1)} %get-tuple-element.88), channel_id=1, source_target_pairs={{0,1},{1,0},{2,3},{3,2},{4,5},{5,4},{6,7},{7,6},{8,9},{9,8},{10,11... | collective-permute-start | bytes 294920 | tf_op jit(solution)/shard_map/ppermute | solution.py:392
  (106 other events, 809.8 us)

commit v2 on v1

v2 whole, which is shorter than its diff:
```python
import jax
import jax.numpy as jnp
import numpy as np
from jax import lax
from jax.experimental import pallas as pl
from jax.experimental.pallas import tpu as pltpu
from jax.sharding import PartitionSpec as P

NORM_EPS = 1e-06
MASKED = -1e30
BLOCK = 512
TILE = 128
HALF = 256
SIZE = 64
HEADS = 3
GROUP = HEADS * SIZE
F32 = jnp.float32
BF16 = jnp.bfloat16
MESH = pl.DeviceIdType.MESH


def bucket_edges():
    distance = np.arange(1.0, 8192.0)
    far_bucket = 16.0 + np.floor(np.log(np.maximum(distance, 16.0) / 16.0) / np.log(8.0) * 16.0)
    bucket_value = np.where(distance < 16, distance, np.minimum(far_bucket, 31.0))
    return [int(distance[np.argmax(bucket_value >= bucket_level)]) for bucket_level in range(1, 32)]


def bucket_one_hot(buckets):
    ids = np.zeros(2 * TILE, np.int32)
    for edge in bucket_edges():
        ids += np.arange(2 * TILE) >= edge
    assert bucket_edges()[-1] <= TILE + 1
    return (np.arange(buckets)[:, None] == ids[None, :]).astype(np.float32)


def dot(left, right):
    return lax.dot_general(left, right, (((1,), (0,)), ((), ())), preferred_element_type=F32)


KEY_AT = ((0, 0), (0, 1), (2, 0))
VALUE_AT = ((1, 0), (1, 1), (2, 1))
QUERY_START = 2 * GROUP


def rows_of(at):
    tile, place = at
    return slice(tile * 128 + place * SIZE, tile * 128 + (place + 1) * SIZE)


def lanes_of(at):
    return slice(at[0] * 128, (at[0] + 1) * 128)


def spread(head_rows, place):
    blank = jnp.zeros_like(head_rows)
    return jnp.concatenate((head_rows, blank) if place == 0 else (blank, head_rows), axis=0)


def bias_tiles(table, index, one_hot):
    column = table[:, index : index + 1]
    by_distance = jnp.sum(column * one_hot, axis=0, keepdims=True)
    wide = jnp.broadcast_to(by_distance, (TILE, 2 * TILE))
    turned = pltpu.roll(wide, 0, 1, stride=1, stride_axis=0)
    key = lax.broadcasted_iota(jnp.int32, (TILE, TILE), 0)
    query = lax.broadcasted_iota(jnp.int32, (TILE, TILE), 1)
    near = jnp.where(key <= query, turned[:, :TILE], MASKED)
    return near, turned[:, TILE:], table[table.shape[0] - 1, index]


def self_tile(scores, key_tile, query_tile, tiles, seg_ref, base):
    near, next_one, far = tiles
    if key_tile == query_tile:
        return scores + near
    same = seg_ref[base + key_tile] == seg_ref[base + query_tile]
    shift = jnp.where(same, 0.0, MASKED)
    if key_tile == query_tile - 1:
        return scores + next_one + shift
    return scores + (far + shift)


def self_forward_kernel(seg_ref, where_ref, kv_ref, q_ref, tab_ref, hot_ref, o_ref, lse_ref):
    key_values = jnp.transpose(kv_ref[0])
    table = tab_ref[0]
    for index in range(HEADS):
        rows = slice(index * SIZE, (index + 1) * SIZE)
        keys = key_values[:, lanes_of(KEY_AT[index])]
        value_rows = kv_ref[0, rows_of(VALUE_AT[index]), :]
        query = spread(q_ref[0, rows, :], KEY_AT[index][1])
        tiles = bias_tiles(table, index, hot_ref[...])
        for half in range(2):
            end = (half + 1) * HALF
            scores = dot(keys[:end], query[:, half * HALF : (half + 1) * HALF])
            columns, totals = [], []
            for part in range(2):
                query_tile = 2 * half + part
                parts = [
                    self_tile(
                        scores[kt * TILE : (kt + 1) * TILE, part * TILE : (part + 1) * TILE],
                        kt, query_tile, tiles, seg_ref, 0,
                    )
                    for kt in range(query_tile + 1)
                ]
                top = jnp.max(parts[0], axis=0, keepdims=True)
                for piece in parts[1:]:
                    top = jnp.maximum(top, jnp.max(piece, axis=0, keepdims=True))
                probs = [jnp.exp(piece - top) for piece in parts]
                total = jnp.sum(probs[0], axis=0, keepdims=True)
                for piece in probs[1:]:
                    total = total + jnp.sum(piece, axis=0, keepdims=True)
                probs = [piece.astype(BF16) for piece in probs]
                if part == 0:
                    probs.append(jnp.zeros((TILE, TILE), BF16))
                columns.append(jnp.concatenate(probs, axis=0))
                totals.append(total)
                lse_ref[0, index : index + 1, query_tile * TILE : (query_tile + 1) * TILE] = top + jnp.log(total)
            weights = jnp.concatenate(columns, axis=1)
            context = dot(value_rows[:, :end], weights)
            context = context / jnp.concatenate(totals, axis=1)
            o_ref[rows, half * HALF : (half + 1) * HALF] = context.astype(BF16)


def key_mask(seg_ref, memseg, mask_ref):
    rows = jnp.transpose(jnp.broadcast_to(memseg.astype(F32), (TILE, BLOCK)))
    for tile in range(BLOCK // TILE):
        wanted = seg_ref[tile].astype(F32)
        mask_ref[:, tile * TILE : (tile + 1) * TILE] = jnp.where(rows == wanted, 0.0, MASKED).astype(mask_ref.dtype)


def cross_forward_kernel(seg_ref, where_ref, kv_ref, q_ref, memseg_ref, o_ref, lse_ref, mask_ref):
    @pl.when(pl.program_id(0) == 0)
    def _():
        key_mask(seg_ref, memseg_ref[...], mask_ref)

    key_values = jnp.transpose(kv_ref[0])
    for index in range(HEADS):
        rows = slice(index * SIZE, (index + 1) * SIZE)
        keys = key_values[:, lanes_of(KEY_AT[index])]
        value_rows = kv_ref[0, rows_of(VALUE_AT[index]), :]
        query = spread(q_ref[0, rows, :], KEY_AT[index][1])
        for half in range(2):
            lanes = slice(half * HALF, (half + 1) * HALF)
            scores = dot(keys, query[:, lanes]) + mask_ref[:, lanes]
            top = jnp.max(scores, axis=0, keepdims=True)
            probs = jnp.exp(scores - top)
            total = jnp.sum(probs, axis=0, keepdims=True)
            context = dot(value_rows, probs.astype(BF16)) / total
            o_ref[rows, lanes] = context.astype(BF16)
            lse_ref[0, index : index + 1, lanes] = top + jnp.log(total)


def attention_forward(kernel, segs, here, kv, kv_part, q, q_part, extra, extra_specs, scratch):
    slots = kv.shape[0]
    return pl.pallas_call(
        kernel,
        grid_spec=pltpu.PrefetchScalarGridSpec(
            num_scalar_prefetch=2,
            grid=(slots,),
            in_specs=[
                pl.BlockSpec((1, 2 * GROUP, BLOCK), lambda s, seg, at: (s, kv_part, 0)),
                pl.BlockSpec((1, GROUP, BLOCK), lambda s, seg, at: (s, q_part, 0)),
            ]
            + extra_specs,
            out_specs=[
                pl.BlockSpec((GROUP, BLOCK), lambda s, seg, at: (jnp.bitwise_xor(at[0], s), 0)),
                pl.BlockSpec((1, 8, BLOCK), lambda s, seg, at: (s, 0, 0)),
            ],
            scratch_shapes=scratch,
        ),
        out_shape=(
            jax.ShapeDtypeStruct((slots * GROUP, BLOCK), BF16),
            jax.ShapeDtypeStruct((slots, 8, BLOCK), F32),
        ),
        cost_estimate=pl.CostEstimate(
            flops=4 * slots * GROUP * BLOCK * BLOCK,
            bytes_accessed=8 * slots * GROUP * BLOCK,
            transcendentals=slots * HEADS * BLOCK * BLOCK,
        ),
    )(segs, here, kv, q, *extra)


def grow(old, new):
    if old is None:
        return new
    shared = old.shape[0]
    if shared == new.shape[0]:
        return old + new
    return jnp.concatenate((old + new[:shared], new[shared:]), axis=0)


def only_lanes(wide, at):
    pair = wide[:, lanes_of(at)]
    lane = lax.broadcasted_iota(jnp.int32, pair.shape, 1)
    keep = lane < SIZE if at[1] == 0 else lane >= SIZE
    return jnp.where(keep, pair, jnp.zeros_like(pair))


def moved(wide, index, place):
    if index < 2:
        assert place == index
        return only_lanes(wide, (0, index))
    part = wide[:, 128:192]
    blank = jnp.zeros_like(part)
    return jnp.concatenate((part, blank) if place == 0 else (blank, part), axis=1)


def attention_back(read, tile_of, skip, note, dq_ref, sums_ref, tick):
    key_values = jnp.transpose(read.kv())
    query_tok = jnp.transpose(read.q(slice(0, GROUP)))
    grad_tok = jnp.transpose(read.do(slice(0, GROUP)))
    sums = [None, None, None]
    for index in range(HEADS):
        rows = slice(index * SIZE, (index + 1) * SIZE)
        k_at, v_at = KEY_AT[index], VALUE_AT[index]
        key_pair, value_pair = key_values[:, lanes_of(k_at)], key_values[:, lanes_of(v_at)]
        query_pair = moved(query_tok, index, k_at[1])
        grad_pair = moved(grad_tok, index, v_at[1])
        query_rows = spread(read.q(rows), k_at[1])
        grad_rows = spread(read.do(rows), v_at[1])
        inner = jnp.sum(read.do(rows).astype(F32) * read.o(rows).astype(F32), axis=0, keepdims=True)
        key_sum = value_sum = None
        for half in range(2):
            end = (half + 1) * HALF if skip else BLOCK
            lanes = slice(half * HALF, (half + 1) * HALF)
            scores = dot(key_pair[:end], query_rows[:, lanes])
            grad_probs = dot(value_pair[:end], grad_rows[:, lanes])
            prob_columns, grad_columns = [], []
            for part in range(2):
                query_tile = 2 * half + part
                cut = slice(query_tile * TILE, (query_tile + 1) * TILE)
                here = slice(part * TILE, (part + 1) * TILE)
                total = read.lse(index, cut)
                probs, grads = [], []
                for kt in range(query_tile + 1 if skip else BLOCK // TILE):
                    there = slice(kt * TILE, (kt + 1) * TILE)
                    prob = jnp.exp(tile_of(scores[there, here], index, kt, query_tile) - total)
                    ds = prob * (grad_probs[there, here] - inner[:, cut])
                    note(index, kt, query_tile, ds)
                    probs.append(prob.astype(BF16))
                    grads.append(ds.astype(BF16))
                if skip and part == 0:
                    probs.append(jnp.zeros((TILE, TILE), BF16))
                    grads.append(jnp.zeros((TILE, TILE), BF16))
                prob_columns.append(jnp.concatenate(probs, axis=0))
                grad_columns.append(jnp.concatenate(grads, axis=0))
            probs = jnp.concatenate(prob_columns, axis=1)
            grads = jnp.concatenate(grad_columns, axis=1)
            value_sum = grow(value_sum, dot(probs, grad_pair[lanes]))
            key_sum = grow(key_sum, dot(grads, query_pair[lanes]))
            dq_ref[rows, lanes] = dot(read.k(index, end), grads).astype(BF16)
        for at, total in ((k_at, key_sum), (v_at, value_sum)):
            sums[at[0]] = total if sums[at[0]] is None else sums[at[0]] + total
        tick(index)
    for tile in range(3):
        sums_ref[:, tile * 128 : (tile + 1) * 128] = sums[tile].astype(BF16)
    sums_ref[:, QUERY_START : QUERY_START + GROUP] = jnp.transpose(dq_ref[...])


class Read:
    def __init__(self, kv, k, q, do, o, lse):
        self.kv, self.k, self.q, self.do, self.o, self.lse = kv, k, q, do, o, lse


class Named:
    def __init__(self, tree):
        for key, value in tree.items():
            setattr(self, key, Named(value) if isinstance(value, dict) else value)


class Copies:
    def __init__(self, send, recv):
        self.send, self.recv, self.count, self.sent = send, recv, 0, []

    def new(self, source, target, device):
        at = self.count
        self.count += 1
        return Copy(self, at, source, target, device)


class Copy:
    def __init__(self, owner, at, source, target, device):
        self.owner, self.at, self.source, self.target, self.device = owner, at, source, target, device

    def make(self):
        return pltpu.make_async_remote_copy(
            src_ref=self.source(), dst_ref=self.target(), send_sem=self.owner.send.at[self.at],
            recv_sem=self.owner.recv.at[self.at], device_id=self.device, device_id_type=MESH,
        )

    def start(self):
        self.make().start()

    def got(self):
        self.make().wait_recv()

    def sent(self):
        self.make().wait_send()

    def done(self):
        self.make().wait()


class Place:
    def __init__(self, depth):
        b, h = lax.axis_index("batch"), lax.axis_index("head")
        self.depth = depth
        self.core, self.y, self.x, self.z = h % 2, h // 2, b % 2, b // 2
        self.to_core = (b, h + 1 - 2 * self.core)
        self.to_y = (b, h + 2 - 4 * self.y)
        self.to_x = (b + 1 - 2 * self.x, h)
        self.to_z = [(lax.rem(self.z + k, depth) * 2 + self.x, h) for k in range(1, depth)]

    def group(self, slot):
        low, high = slot % 2, slot // 2
        return (self.core + low - 2 * self.core * low) + 2 * (self.y + high - 2 * self.y * high)

    def everyone(self):
        return [self.to_core, self.to_y, self.to_x] + self.to_z


Z, X, Y = range(3)


class Sum:
    def __init__(self, place, copies, total, got, order):
        self.place, self.total, self.got, self.order = place, total, got, order
        self.dims = len(total.shape) - 2
        self.stages = []
        for at, axis in enumerate(order):
            room = got[at]
            if axis == Z:
                stage = [
                    copies.new(self.source(at, k), (lambda room, k: lambda: room.at[k - 1])(room, k), place.to_z[k - 1])
                    for k in range(1, place.depth)
                ]
            else:
                device = place.to_x if axis == X else place.to_y
                stage = [copies.new(self.source(at, 1), (lambda room: lambda: room)(room), device)]
            self.stages.append(stage)

    @staticmethod
    def rooms(depth, dims, order, rows, lanes):
        sizes = {Z: depth, X: 2, Y: 2}
        free = list(range(dims))
        shapes = []
        for axis in order:
            free.remove(axis)
            lead = (depth - 1,) if axis == Z else ()
            shapes.append(lead + tuple(sizes[d] for d in free) + (rows, lanes))
        return shapes

    def mine(self, axis):
        return (self.place.z, self.place.x, self.place.y)[axis]

    def source(self, at, k):
        def view():
            index = [slice(None)] * self.dims
            for axis in self.order[:at]:
                index[axis] = self.mine(axis)
            axis = self.order[at]
            index[axis] = lax.rem(self.place.z + k, self.place.depth) if axis == Z else 1 - self.mine(axis)
            return self.total.at[tuple(index)]

        return view

    def start(self, at):
        for copy in self.stages[at]:
            copy.start()

    def value(self, at, free):
        axis = self.order[at]
        later = sorted(self.order[at + 1 :])
        index = [None] * self.dims
        for done in self.order[: at + 1]:
            index[done] = self.mine(done)
        for d, i in zip(later, free):
            index[d] = i
        got = [self.got[at].at[k] for k in range(self.place.depth - 1)] if axis == Z else [self.got[at]]
        return tuple(index), [g[tuple(free)] if free else g[...] for g in got]

    def add(self, at):
        for copy in self.stages[at]:
            copy.got()
        later = sorted(self.order[at + 1 :])

        def one(free):
            index, got = self.value(at, free)
            if len(got) == 1:
                self.total[index] = self.total[index] + got[0]
            else:
                total = self.total[index].astype(F32)
                for g in got:
                    total = total + g.astype(F32)
                self.total[index] = total.astype(BF16)

        def over(dims, free):
            if not dims:
                one(free)
            elif dims[0] == Z:

                @pl.loop(0, self.place.depth)
                def _(z):
                    over(dims[1:], free + [z])

            else:
                for i in range(2):
                    over(dims[1:], free + [i])

        over(later, [])
        self.start(at + 1)

    def finish(self):
        at = len(self.order) - 1
        for copy in self.stages[at]:
            copy.got()
        index, got = self.value(at, [])
        total = self.total[index].astype(F32)
        for g in got:
            total = total + g.astype(F32)
        return total

    def sent(self):
        for stage in self.stages:
            for copy in stage:
                copy.sent()


def add_loop(depth, target, other, inner):
    @pl.loop(0, depth)
    def _(z):
        for index in np.ndindex(*inner):
            target[(z, *index)] = target[(z, *index)] + other[(z, *index)]


class Shared:
    def __init__(self, place, copies, room, order, send, pair):
        self.place, self.room, self.from_pair = place, room, pair
        self.sum = Sum(place, copies, room.total, room.got, order)
        self.pair = copies.new(lambda: send, lambda: pair, place.to_core)
        self.swap = copies.new(lambda: room.last.at[1 - place.core], lambda: room.other, place.to_core)

    def enter(self, keep=None):
        self.pair.got()
        if keep is not None:
            keep.wait()
        add_loop(self.place.depth, self.room.total, self.from_pair, (2, 2))
        self.sum.start(0)

    def last(self):
        total = self.sum.finish()
        rows = total.shape[0] // 2
        self.room.last[0] = total[:rows]
        self.room.last[1] = total[rows:]
        self.swap.start()

    def store(self, out, offset, half):
        self.swap.got()
        lanes = self.room.other.shape[1]
        core = self.place.core
        for which, value in ((core, self.room.last[core]), (1 - core, self.room.other[...])):
            at = pl.ds(pl.multiple_of(which * half + offset, 8), lanes)
            out[at, :] = jnp.transpose(value)

    def sent(self):
        self.swap.sent()
        self.sum.sent()


class Slots:
    def __init__(self, place, copies, room, sends, y_first, order):
        self.place, self.room, self.y_first = place, room, y_first
        self.pair = [copies.new((lambda j: lambda: sends.at[j])(j), (lambda j: lambda: room.pair.at[j])(j), place.to_core) for j in range(2)]
        self.own = Sum(place, copies, room.total.at[0], room.got, order)
        if y_first:
            self.across = copies.new(lambda: room.total.at[1], lambda: room.across, place.to_y)
        else:
            self.far = Sum(place, copies, room.total.at[1], room.far, order)
            self.across = copies.new(lambda: room.chunk, lambda: room.across, place.to_y)

    def enter(self, j):
        self.pair[j].got()
        add_loop(self.place.depth, self.room.total.at[j], self.room.pair.at[j], (2,))
        if j == 1:
            if self.y_first:
                self.across.start()
            else:
                self.far.start(0)
        elif not self.y_first:
            self.own.start(0)

    def take(self):
        self.across.got()
        add_loop(self.place.depth, self.room.total.at[0], self.room.across, (2,))
        self.own.start(0)

    def give(self):
        self.room.chunk[...] = self.far.finish().astype(BF16)
        self.across.start()

    def finish(self):
        total = self.own.finish()
        if not self.y_first:
            self.across.got()
            total = total + self.room.across[...].astype(F32)
        return total

    def sent(self):
        self.own.sent()
        self.across.sent()
        if not self.y_first:
            self.far.sent()


SHARED_ORDER = dict(
    gate=(Z, X, Y), up=(Y, X, Z), down_a=(X, Y, Z), down_b=(X, Y, Z), out_two=(X, Y, Z), out_one=(X, Y, Z)
)
SLOT_ORDER = dict(kv_two=(True, (X, Z)), q_two=(False, (X, Z)), kv_one=(True, (X, Z)), q_one=(True, (X, Z)))
KV = slice(0, 2 * GROUP)
QS = slice(2 * GROUP, 3 * GROUP)


def put_heads(ref, kv):
    key_out, value_out = ref
    key_out[:, :128] = kv[:, :128]
    key_out[:, 128:] = kv[:, 256:320]
    value_out[:, :128] = kv[:, 128:256]
    value_out[:, 128:] = kv[:, 320:384]


def backward_kernel(depth, ins, outs, r):
    place = Place(depth)
    step = pl.program_id(0)
    core = place.core
    copies = Copies(r.send, r.recv)

    shared = Named({
        name: Shared(
            place, copies, getattr(r, name), order, getattr(ins.sends, name, r.out_send), getattr(r.pairs, name, r.out_pair)
        )
        for name, order in SHARED_ORDER.items()
    })
    slots = Named({
        name: Slots(place, copies, getattr(r, name), r.kv_send if order_at < 1 else r.q_send, y_first, order)
        for name, (y_first, order), order_at in (
            (n, o, int(getattr(r, n).total.shape[-1] == GROUP)) for n, o in SLOT_ORDER.items()
        )
    })
    layer_swap = copies.new(lambda: r.block.at[1 - core], lambda: outs.layer.at[core], place.to_core)
    memory_swap = copies.new(lambda: r.block.at[1 - core], lambda: outs.memory.at[core], place.to_core)
    tokens_swap = copies.new(lambda: r.block.at[1 - core], lambda: outs.tokens.at[core], place.to_core)
    gain_copies = [
        copies.new(lambda: r.gains, (lambda k: lambda: r.gains_got.at[k])(k), d)
        for k, d in enumerate([place.to_core, place.to_y, place.to_x] + place.to_z)
    ]
    bias_copies = [
        copies.new((lambda s: lambda: r.bias.at[s])(s), (lambda k: lambda: r.bias_got.at[k])(k), d)
        for k, (s, d) in enumerate(
            zip([1, 3, 2, 0] + [0] * (depth - 1), [place.to_core, place.to_core, place.to_y, place.to_x] + place.to_z)
        )
    ]
    assert copies.count == r.send.shape[0], copies.count

    loads = []

    def load(source, target):
        loads.append(pltpu.make_async_copy(source, target, r.load.at[len(loads)]))
        return loads[-1]

    i = ins.loaded
    after, wo_two, ctx_two = load(i.after, r.after), load(i.wo_two, r.wo), load(i.ctx_two, r.ctx)
    n_two, mem, first, tok = load(i.n_two, r.n), load(i.mem, r.mem), load(i.first, r.hidden), load(i.tok, r.hidden)
    wo_one, ctx_one, n_one = load(i.wo_one, r.wo), load(i.ctx_one, r.ctx), load(i.n_one, r.n)
    keeps = Named({
        name: load(getattr(ins.keeps, name), getattr(r, name).total) for name in SHARED_ORDER if hasattr(ins.keeps, name)
    })
    layer_in = load(ins.layer, r.block)
    layer_put = load(r.block.at[core], outs.layer.at[core])
    memory_put = load(r.block.at[core], outs.memory.at[core])
    tokens_put = load(r.block.at[core], outs.tokens.at[core])

    def out_products(unit, context, branch):
        lanes = context.shape[0] // 2
        for which, target in ((1 - core, r.out_send), (core, unit.room.total)):
            side = jnp.transpose(context[pl.ds(pl.multiple_of(which * lanes, 16), lanes), :])
            per = branch.shape[0] // 2
            for part in range(2):
                product = dot(branch[part * per : (part + 1) * per, :], side).astype(BF16)
                rows = target.shape[3]
                for piece in range(per // rows):
                    at = part * (per // rows) + piece
                    target[at // 4, (at // 2) % 2, at % 2] = product[piece * rows : (piece + 1) * rows]
            if which is not core:
                unit.pair.start()

    def weight_products(target, left, lanes):
        rows = target.shape[2]
        per = left.shape[0] // 2
        for part in range(2):
            product = dot(left[part * per : (part + 1) * per, :], r.dqkv[:, lanes]).astype(BF16)
            for piece in range(per // rows):
                at = part * (per // rows) + piece
                target[at // 2, at % 2] = product[piece * rows : (piece + 1) * rows]

    def add_rows(target, lanes, weights, fresh):
        for part in range(2):
            rows = slice(part * HALF, (part + 1) * HALF)
            product = dot(r.dqkv[rows, lanes], weights)

            @pl.when(fresh)
            def _():
                target[rows, :] = product

            @pl.when(jnp.logical_not(fresh))
            def _():
                target[rows, :] = target[rows, :] + product

    def norm_back(hidden, gain, incoming, onto, gain_row, branch):
        total = jnp.zeros((1, hidden.shape[1]), F32)
        for part in range(4):
            rows = slice(part * TILE, (part + 1) * TILE)
            h = hidden[rows, :].astype(F32)
            e = incoming[rows, :]
            scale = lax.rsqrt(jnp.mean(h * h, axis=-1, keepdims=True) + NORM_EPS)
            weighted = e * gain[...]
            inner = jnp.mean(weighted * h, axis=-1, keepdims=True)
            result = onto[rows, :] + weighted * scale - h * (scale * scale * scale * inner)
            total = total + jnp.sum(e * h * scale, axis=0, keepdims=True)
            if branch is None:
                r.block[part // 2, (part % 2) * TILE : (part % 2 + 1) * TILE, :] = result.astype(BF16)
            else:
                onto[rows, :] = result
                branch[:, rows] = jnp.transpose(result.astype(BF16))
        r.gains[gain_row : gain_row + 1, :] = total

    plan = {}

    def at(point, *tasks):
        plan.setdefault(point, []).extend(tasks)

    sh, sl = shared, slots
    at((0, 0), lambda: sh.up.enter(keeps.up), sh.out_two.enter)
    at((0, 1), lambda: sh.down_a.enter(keeps.down_a))
    at((0, 2), lambda: sh.down_b.enter(keeps.down_b))
    at((0, 3), sl.kv_two.pair[1].start, sl.q_two.pair[1].start)
    at((1, 0), lambda: sh.out_two.sum.add(0))
    at((1, 3), lambda: sl.kv_two.enter(1), lambda: sl.q_two.enter(1))
    at((2, 3), sl.kv_two.pair[0].start, sl.q_two.pair[0].start)
    at((3, 0), lambda: sh.up.sum.add(0), lambda: sh.down_a.sum.add(0))
    at((3, 3), lambda: sl.kv_two.enter(0), lambda: sl.q_two.enter(0))
    at((4, 0), lambda: sh.down_b.sum.add(0), sh.out_one.enter, lambda: sl.q_two.far.add(0))
    at((4, 2), sl.kv_two.take)
    at((4, 3), sl.kv_one.pair[1].start, sl.q_one.pair[1].start, lambda: sh.gate.sum.add(0), lambda: sl.q_two.own.add(0))
    at((5, 0), lambda: sh.out_two.sum.add(1))
    at((5, 2), lambda: sh.down_a.sum.add(1))
    at((5, 3), lambda: sl.kv_one.enter(1), lambda: sl.q_one.enter(1), sl.q_two.give)
    at((6, 0), lambda: sh.up.sum.add(1), lambda: sh.down_b.sum.add(1))
    at((6, 2), lambda: sh.out_one.sum.add(0))
    at((6, 3), sl.kv_one.pair[0].start, sl.q_one.pair[0].start)
    at((7, 2), lambda: sl.kv_two.own.add(0))

    def tick(steps, index):
        for k in steps:
            if (k, index) in plan:

                def run(tasks=plan[k, index]):
                    for task in tasks:
                        task()

                pl.when(step == k)(run)

    @pl.when(step == 0)
    def _():
        barrier = pltpu.get_barrier_semaphore()
        for device in place.everyone():
            pl.semaphore_signal(barrier, inc=1, device_id=device, device_id_type=MESH)
        for copy in (after, wo_two, ctx_two, layer_in):
            copy.start()
        pl.semaphore_wait(barrier, len(place.everyone()))
        for name in SHARED_ORDER:
            if hasattr(keeps, name):
                getattr(shared, name).pair.start()
                getattr(keeps, name).start()
        for copy in (n_two, mem, first):
            copy.start()
        after.wait()
        for part in range(4):
            rows = slice(part * TILE, (part + 1) * TILE)
            r.branch[:, rows] = jnp.transpose(r.after[rows, :].astype(BF16))
        key_mask(ins.segs, ins.memsegs[...], r.mask)
        wo_two.wait()
        ctx_two.wait()
        layer_in.wait()
        layer_swap.start()
        layer_put.start()
        sh.gate.enter(keeps.gate)
        out_products(sh.out_two, r.ctx, r.branch)
        n_two.wait()
        mem.wait()
        r.gains[...] = jnp.zeros_like(r.gains)
        r.gains[2:3, :] = ins.ff_gain_grad[...]

    slot = 3 - step % 4
    odd = slot % 2 == 1
    rows_at = pl.ds(pl.multiple_of(place.group(slot) * GROUP, 16), GROUP)

    def slot_products(kv, q, kv_left, q_left):
        @pl.when(odd)
        def _():
            weight_products(r.kv_send.at[slot // 2], kv_left, KV)
            weight_products(r.q_send.at[slot // 2], q_left, QS)

        @pl.when(jnp.logical_not(odd))
        def _():
            weight_products(kv.room.total.at[slot // 2], kv_left, KV)
            weight_products(q.room.total.at[slot // 2], q_left, QS)

    @pl.when(step < 4)
    def _():
        r.do[...] = dot(r.wo[rows_at, :], r.branch[...]).astype(BF16)
        kv, q, lse = ins.kv_two, ins.q_two, ins.lse_two
        context = r.ctx.at[rows_at, :]
        read = Read(
            lambda: kv[0], lambda h, end: kv[0, rows_of(KEY_AT[h]), :end], lambda rows: q[0, rows, :],
            lambda rows: r.do[rows, :], lambda rows: context[rows, :], lambda h, cut: lse[0, h : h + 1, cut],
        )

        def tile_of(scores, index, kt, qt):
            return scores + r.mask[kt * TILE : (kt + 1) * TILE, qt * TILE : (qt + 1) * TILE].astype(F32)

        attention_back(read, tile_of, False, lambda *a: None, r.dq, r.dqkv, lambda h: tick(range(4), h))
        slot_products(sl.kv_two, sl.q_two, r.mem, r.n)
        tick(range(4), 3)
        add_rows(r.acc_b, KV, ins.wt_two[0, KV, :], step == 0)
        add_rows(r.acc_a, QS, ins.wt_two[0, QS, :], step == 0)

    @pl.when(step == 3)
    def _():
        for copy in (wo_one, ctx_one, n_one):
            copy.start()
        first.wait()
        layer_swap.sent()
        layer_put.wait()
        norm_back(r.hidden, ins.cross_gain, r.acc_a, r.after, 1, r.branch)
        tok.start()
        for part in range(4):
            rows = slice(part * TILE, (part + 1) * TILE)
            r.block[part // 2, (part % 2) * TILE : (part % 2 + 1) * TILE, :] = r.acc_b[rows, :].astype(BF16)
        memory_swap.start()
        memory_put.start()
        for copy in (wo_one, ctx_one, n_one):
            copy.wait()
        sh.out_two.pair.sent()
        out_products(sh.out_one, r.ctx, r.branch)

    @pl.when(step >= 4)
    def _():
        r.do[...] = dot(r.wo[rows_at, :], r.branch[...]).astype(BF16)
        qkv, lse = ins.qkv_one, ins.lse_one
        context = r.ctx.at[rows_at, :]
        read = Read(
            lambda: qkv[0, KV, :], lambda h, end: qkv[0, rows_of(KEY_AT[h]), :end],
            lambda rows: qkv[0, QUERY_START + rows.start : QUERY_START + rows.stop, :],
            lambda rows: r.do[rows, :], lambda rows: context[rows, :], lambda h, cut: lse[0, h : h + 1, cut],
        )
        table, one_hot = ins.table[0], ins.hot[...]
        tiles = [bias_tiles(table, index, one_hot) for index in range(HEADS)]
        kept = {}

        def note(index, kt, qt, ds):
            key = (index, min(qt - kt, 2))
            kept[key] = kept[key] + ds if key in kept else ds

        attention_back(
            read, lambda scores, index, kt, qt: self_tile(scores, kt, qt, tiles[index], ins.segs, 0), True, note,
            r.dq, r.dqkv, lambda h: tick(range(4, 8), h),
        )
        buckets = one_hot.shape[0]
        lane = lax.broadcasted_iota(jnp.int32, (buckets, TILE), 1)
        bucket = lax.broadcasted_iota(jnp.int32, (buckets, TILE), 0)
        key = lax.broadcasted_iota(jnp.int32, (TILE, TILE), 0)
        query = lax.broadcasted_iota(jnp.int32, (TILE, TILE), 1)
        flip = (key + query == TILE - 1).astype(F32)
        table_grad = jnp.zeros((buckets, TILE), F32)
        for index in range(HEADS):
            both = jnp.concatenate((kept[index, 0], kept[index, 1]), axis=1)
            both = jnp.dot(flip, both, precision=lax.Precision.HIGHEST, preferred_element_type=F32)
            turned = pltpu.roll(both, TILE + 1, 1, stride=1, stride_axis=0)
            by_distance = jnp.sum(turned, axis=0, keepdims=True)
            column = jnp.sum(by_distance * one_hot, axis=1, keepdims=True)
            far_total = jnp.sum(jnp.sum(kept[index, 2], axis=0, keepdims=True), axis=1, keepdims=True)
            column = jnp.where(bucket == buckets - 1, column + far_total, column)
            table_grad = table_grad + jnp.where(lane == index, column, 0.0)
        r.bias[slot] = table_grad

        for k, j in ((4, 1), (6, 0)):

            @pl.when(step == k)
            def _(j=j):
                sl.kv_two.pair[j].sent()
                sl.q_two.pair[j].sent()

        slot_products(sl.kv_one, sl.q_one, r.n, r.n)
        tick(range(4, 8), 3)
        add_rows(r.acc_a, slice(0, 3 * GROUP), ins.wt_one[0], step == 4)

    @pl.when(step == 7)
    def _():
        sl.kv_one.enter(0)
        sl.q_one.enter(0)
        gains, bias = r.gains, r.bias
        memory_swap.sent()
        memory_put.wait()
        tok.wait()
        norm_back(r.hidden, ins.self_gain, r.acc_a, r.after, 0, None)
        tokens_swap.start()
        tokens_put.start()
        gain_copies[0].start()
        bias_copies[0].start()
        bias_copies[1].start()
        sl.kv_one.take()
        sh.gate.sum.add(1)
        sh.up.last()
        sh.down_a.last()
        gain_copies[0].done()
        gains[...] = gains[...] + r.gains_got[0]
        bias_copies[0].done()
        bias_copies[1].done()
        bias[0] = bias[0] + r.bias_got[0]
        bias[2] = bias[2] + r.bias_got[1]
        gain_copies[1].start()
        bias_copies[2].start()
        sh.down_b.last()
        sl.q_one.take()
        sl.kv_one.own.add(0)
        gain_copies[1].done()
        gains[...] = gains[...] + r.gains_got[1]
        bias_copies[2].done()
        bias[0] = bias[0] + r.bias_got[2]
        gain_copies[2].start()
        bias_copies[3].start()
        sh.out_one.sum.add(1)
        sl.q_one.own.add(0)
        sh.gate.last()
        sh.out_two.last()
        gain_copies[2].done()
        gains[...] = gains[...] + r.gains_got[2]
        bias_copies[3].done()
        bias[0] = bias[0] + r.bias_got[3]
        for k in range(depth - 1):
            gain_copies[3 + k].start()
            bias_copies[4 + k].start()
        outs.wq_two[...] = sl.q_two.finish()
        put_heads((outs.wk_two, outs.wv_two), sl.kv_two.finish())
        put_heads((outs.wk_one, outs.wv_one), sl.kv_one.finish())
        gain_total, bias_total = gains[...], bias[0]
        for k in range(depth - 1):
            gain_copies[3 + k].done()
            bias_copies[4 + k].done()
            gain_total = gain_total + r.gains_got[3 + k]
            bias_total = bias_total + r.bias_got[4 + k]
        outs.gains[...] = gain_total
        outs.bias[...] = bias_total
        sh.up.store(outs.up, 0, outs.up.shape[0] // 2)
        sh.down_a.store(outs.down, 0, outs.down.shape[0] // 2)
        sh.down_b.store(outs.down, outs.down.shape[0] // 4, outs.down.shape[0] // 2)
        sh.gate.store(outs.gate, 0, outs.gate.shape[0] // 2)
        sh.out_two.store(outs.out_two, 0, outs.out_two.shape[0] // 2)
        sh.out_one.last()
        outs.wq_one[...] = sl.q_one.finish()
        sh.out_one.store(outs.out_one, 0, outs.out_one.shape[0] // 2)
        for name in SHARED_ORDER:
            unit = getattr(shared, name)
            unit.sent()
            if unit is not sh.out_two:
                unit.pair.sent()
        for name in SLOT_ORDER:
            getattr(slots, name).sent()
        for j in range(2):
            sl.kv_one.pair[j].sent()
            sl.q_one.pair[j].sent()
        layer_swap.got()
        memory_swap.got()
        tokens_swap.done()
        tokens_put.wait()


def backward_call(batch_size, operands):
    depth = batch_size // 2
    tok = operands["loaded"]["tok"]
    model = tok.shape[1]
    share = model // batch_size
    anywhere = pl.BlockSpec(memory_space=pl.ANY)

    def fixed(shape):
        return pl.BlockSpec(shape, lambda t: (0,) * len(shape))

    def early(array):
        return pl.BlockSpec((1,) + array.shape[1:], lambda t: (3 - t + (t // 4) * (t - 3), 0, 0))

    def late(array):
        return pl.BlockSpec((1,) + array.shape[1:], lambda t: (3 - (t // 4) * (t - 4), 0, 0))

    kinds = dict(
        segs=lambda a: pl.BlockSpec(memory_space=pltpu.SMEM), kv_two=early, q_two=early, lse_two=early, wt_two=early,
        qkv_one=late, lse_one=late, wt_one=late, table=late, loaded=lambda a: anywhere, sends=lambda a: anywhere,
        keeps=lambda a: anywhere, layer=lambda a: anywhere,
    )
    in_specs = {
        name: jax.tree.map(kinds.get(name, lambda a: fixed(a.shape)), value) for name, value in operands.items()
    }
    keeps = operands["keeps"]
    shapes = {name: keeps[name].shape[3:] for name in keeps}
    shapes.update(out_two=(model // (4 * depth), model // 2), out_one=(model // (4 * depth), model // 2))
    block = jax.ShapeDtypeStruct((2, HALF, model), BF16)

    def wide(rows, columns):
        return jax.ShapeDtypeStruct((rows, columns), F32)

    head = wide(share, GROUP)
    buckets = operands["hot"].shape[0]
    outs = dict(
        layer=block, memory=block, tokens=block,
        gate=wide(2 * shapes["gate"][1], shapes["gate"][0] // 2), up=wide(2 * shapes["up"][1], shapes["up"][0] // 2),
        down=wide(4 * shapes["down_a"][1], shapes["down_a"][0] // 2),
        out_two=wide(model, shapes["out_two"][0] // 2), out_one=wide(model, shapes["out_one"][0] // 2),
        wq_two=head, wk_two=head, wv_two=head, wq_one=head, wk_one=head, wv_one=head,
        gains=wide(8, model), bias=wide(buckets, TILE),
    )
    out_specs = {name: anywhere if s is block else fixed(s.shape) for name, s in outs.items()}

    def room(*shape, kind=BF16):
        return pltpu.VMEM(shape, kind)

    scratch = {}
    for name, order in SHARED_ORDER.items():
        rows, lanes = shapes[name]
        scratch[name] = dict(
            total=room(depth, 2, 2, rows, lanes),
            got=[room(*s) for s in Sum.rooms(depth, 3, order, rows, lanes)],
            last=room(2, rows // 2, lanes, kind=F32), other=room(rows // 2, lanes, kind=F32),
        )
    for name, (y_first, order) in SLOT_ORDER.items():
        lanes = 2 * GROUP if name.startswith("kv") else GROUP
        got = [room(*s) for s in Sum.rooms(depth, 2, order, share, lanes)]
        both = room(2, depth, 2, share, lanes)
        scratch[name] = dict(total=both, pair=both, got=got)
        if y_first:
            scratch[name].update(across=room(depth, 2, share, lanes))
        else:
            scratch[name].update(across=room(share, lanes), chunk=room(share, lanes), far=list(got))
    scratch.update(
        pairs={name: room(depth, 2, 2, *shapes[name]) for name in keeps},
        out_send=room(depth, 2, 2, *shapes["out_one"]), out_pair=room(depth, 2, 2, *shapes["out_one"]), kv_send=room(2, depth, 2, share, 2 * GROUP),
        q_send=room(2, depth, 2, share, GROUP), block=room(2, HALF, model), branch=room(model, BLOCK),
        acc_a=room(BLOCK, model, kind=F32), acc_b=room(BLOCK, model, kind=F32), dqkv=room(BLOCK, 3 * GROUP),
        dq=room(GROUP, BLOCK), do=room(GROUP, BLOCK), mask=room(BLOCK, BLOCK), gains=room(8, model, kind=F32),
        gains_got=room(depth + 2, 8, model, kind=F32), bias=room(4, buckets, TILE, kind=F32),
        bias_got=room(depth + 3, buckets, TILE, kind=F32),
        after=room(BLOCK, model, kind=F32), hidden=room(BLOCK, model, kind=F32),
        wo=room(model, model), ctx=room(model, BLOCK), n=room(model, BLOCK), mem=room(model, BLOCK),
    )
    z = depth - 1
    copies = sum(2 + 2 + z for _ in SHARED_ORDER) + 3 + (3 + z) + (4 + z)
    copies += sum(2 + (1 + z) + 1 + (0 if y_first else 1 + z) for y_first, _ in SLOT_ORDER.values())
    scratch.update(send=pltpu.SemaphoreType.DMA((copies,)), recv=pltpu.SemaphoreType.DMA((copies,)))
    scratch.update(load=pltpu.SemaphoreType.DMA((18,)))

    arrays, in_tree = jax.tree.flatten(operands)
    out_shapes, out_tree = jax.tree.flatten(outs)
    rooms, room_tree = jax.tree.flatten(scratch)

    def kernel(*refs):
        a, b = len(arrays), len(arrays) + len(out_shapes)
        backward_kernel(
            depth, Named(jax.tree.unflatten(in_tree, refs[:a])), Named(jax.tree.unflatten(out_tree, refs[a:b])),
            Named(jax.tree.unflatten(room_tree, refs[b:])),
        )

    results = pl.pallas_call(
        kernel,
        grid=(8,),
        in_specs=jax.tree.leaves(in_specs),
        out_specs=jax.tree.leaves(out_specs),
        out_shape=out_shapes,
        scratch_shapes=rooms,
        compiler_params=pltpu.CompilerParams(
            collective_id=0, has_side_effects=True, vmem_limit_bytes=66_000_000, dimension_semantics=("arbitrary",)
        ),
        cost_estimate=pl.CostEstimate(flops=20_000_000_000, bytes_accessed=40_000_000, transcendentals=6_000_000),
    )(*arrays)
    return Named(jax.tree.unflatten(out_tree, results))


def swap(array, axis, mask):
    size = lax.axis_size(axis)
    return lax.ppermute(array, axis, [(i, i ^ mask) for i in range(size)])


def norm(hidden, gain):
    scale = lax.rsqrt(jnp.mean(hidden * hidden, axis=-1, keepdims=True) + NORM_EPS)
    return (hidden * scale * gain).astype(BF16)


def norm_back(hidden, gain, grad):
    scale = lax.rsqrt(jnp.mean(hidden * hidden, axis=-1, keepdims=True) + NORM_EPS)
    weighted = grad * gain
    inner = jnp.mean(weighted * hidden, axis=-1, keepdims=True)
    return weighted * scale - hidden * (scale * scale * scale * inner), jnp.sum(grad * hidden * scale, axis=0)


def over_tokens(left, right):
    return lax.dot_general(left, right, (((0,), (0,)), ((), ())), preferred_element_type=F32)


def by_transpose(left, right):
    return lax.dot_general(left, right, (((1,), (1,)), ((), ())), preferred_element_type=F32)


def gelu_parts(value):
    inner = np.float32(np.sqrt(2.0 / np.pi)) * (value + 0.044715 * (value * value * value))
    bend = jnp.tanh(inner)
    slope = np.float32(np.sqrt(2.0 / np.pi)) * (1.0 + 3.0 * 0.044715 * (value * value))
    gelu = 0.5 * value * (1.0 + bend)
    return gelu, 0.5 * (1.0 + bend) + 0.5 * value * (1.0 - bend * bend) * slope


def group_rows(query, key, value):
    q, k, v = query.T, key.T, value.T
    return jnp.concatenate((k[:128], v[:128], k[128:], v[128:], q), axis=0)


def on_device(
    tokens, memory, cotangent, target_segments, memory_segments, self_gain, self_query, self_key,
    self_value, self_out, position_bias, cross_gain, cross_query, cross_key, cross_value, cross_out,
    ff_gain, ff_gate, ff_up, ff_down,
):
    heads_axis, batch_axis = lax.axis_size("head"), lax.axis_size("batch")
    me, row = lax.axis_index("head"), lax.axis_index("batch")
    core = me & 1
    rows, part, model = tokens.shape
    assert part * 2 == BLOCK and rows == 2 and heads_axis == 4
    assert position_bias.shape[1] == HEADS and self_query.shape[1] == GROUP
    here = jnp.reshape(me, (1,)).astype(jnp.int32)
    one_hot = jnp.asarray(bucket_one_hot(position_bias.shape[0]))

    def to_block(array):
        mine = lax.dynamic_index_in_dim(array, core, 0, keepdims=False)
        other = swap(lax.dynamic_index_in_dim(array, 1 - core, 0, keepdims=False), "head", 1)
        return jnp.where(core == 0, jnp.concatenate((mine, other), 0), jnp.concatenate((other, mine), 0))

    def block_segments(segments):
        mine = lax.dynamic_index_in_dim(segments, core, 0, keepdims=False)
        return lax.dynamic_slice_in_dim(mine, (me >> 1) * BLOCK, BLOCK, 0)

    tile_segments = block_segments(target_segments)[::TILE]
    key_segments = block_segments(memory_segments).reshape(1, BLOCK)

    def gathered(array):
        slots = [array, swap(array, "head", 1), swap(array, "head", 2)]
        slots.append(swap(slots[2], "head", 1))
        return jnp.stack(slots)

    tok = to_block(tokens)
    wt_one = gathered(group_rows(self_query, self_key, self_value))
    table = gathered(position_bias)
    mem = to_block(memory)
    wt_two = gathered(group_rows(cross_query, cross_key, cross_value))
    cot = to_block(cotangent)

    wide = tok.astype(F32)
    normed_one = jnp.transpose(norm(wide, self_gain))
    qkv = dot(wt_one.reshape(-1, model), normed_one).astype(BF16).reshape(4, 3 * GROUP, BLOCK)
    hot_spec = pl.BlockSpec(one_hot.shape, lambda s, seg, at: (0, 0))
    context_one, lse_one = attention_forward(
        self_forward_kernel, tile_segments, here, qkv, 0, qkv, 2, (table, one_hot),
        [pl.BlockSpec((1,) + table.shape[1:], lambda s, seg, at: (s, 0, 0)), hot_spec], [],
    )
    mem_rows = jnp.transpose(mem)
    kv_two = jnp.einsum("sad,dt->sat", wt_two[:, :QUERY_START], mem_rows, preferred_element_type=F32).astype(BF16)
    first_sum = wide + over_tokens(context_one, self_out)
    normed_two = jnp.transpose(norm(first_sum, cross_gain))
    q_two = jnp.einsum("sad,dt->sat", wt_two[:, QUERY_START:], normed_two, preferred_element_type=F32).astype(BF16)
    context_two, lse_two = attention_forward(
        cross_forward_kernel, tile_segments, here, kv_two, 0, q_two, 0, (key_segments,),
        [pl.BlockSpec((1, BLOCK), lambda s, seg, at: (0, 0))], [pltpu.VMEM((BLOCK, BLOCK), F32)],
    )
    second_sum = first_sum + over_tokens(context_two, cross_out)
    normed_three = norm(second_sum, ff_gain)
    gate_value = dot(normed_three, ff_gate)
    up_value = dot(normed_three, ff_up)
    gelu, slope = gelu_parts(gate_value)
    activation = (gelu * up_value).astype(BF16)
    layer = (second_sum + dot(activation, ff_down)).astype(BF16)

    grad_act = by_transpose(cot, ff_down)
    grad_gate = (grad_act * up_value * slope).astype(BF16)
    grad_up = (grad_act * gelu).astype(BF16)
    grad_three = by_transpose(grad_gate, ff_gate) + by_transpose(grad_up, ff_up)
    back, ff_gain_grad = norm_back(second_sum, ff_gain, grad_three)
    grad_second = cot.astype(F32) + back

    def halves(left, right, pieces):
        lanes = left.shape[1] // (2 * pieces)
        chunks = batch_axis // 2, 2, 2, right.shape[1] // (2 * batch_axis), lanes
        found = []
        for piece in range(pieces):
            found.append([
                over_tokens(
                    right, lax.dynamic_slice_in_dim(left, (which * pieces + piece) * lanes, lanes, 1)
                ).astype(BF16).reshape(chunks)
                for which in (1 - core, core)
            ])
        return found

    (gate,) = halves(normed_three, grad_gate, 1)
    (up,) = halves(normed_three, grad_up, 1)
    down_a, down_b = halves(activation, cot, 2)
    done = backward_call(
        batch_axis,
        dict(
            segs=tile_segments, memsegs=key_segments, hot=one_hot, self_gain=self_gain.reshape(1, -1),
            cross_gain=cross_gain.reshape(1, -1), ff_gain_grad=ff_gain_grad.reshape(1, -1),
            kv_two=kv_two, q_two=q_two, lse_two=lse_two, wt_two=wt_two,
            qkv_one=qkv, lse_one=lse_one, wt_one=wt_one, table=table,
            loaded=dict(
                after=grad_second, wo_two=cross_out, ctx_two=context_two, n_two=normed_two, mem=mem_rows,
                first=first_sum, wo_one=self_out, ctx_one=context_one, n_one=normed_one, tok=wide,
            ),
            sends=dict(gate=gate[0], up=up[0], down_a=down_a[0], down_b=down_b[0]),
            keeps=dict(gate=gate[1], up=up[1], down_a=down_a[1], down_b=down_b[1]),
            layer=layer.reshape(2, part, model),
        ),
    )
    share = model // (heads_axis * batch_axis)
    gain_sums = lax.dynamic_slice_in_dim(done.gains, (row * heads_axis + me) * share, share, 1)
    return (
        done.layer, done.tokens, done.memory, gain_sums[0], done.wq_one, done.wk_one, done.wv_one, done.out_one,
        done.bias[:, :HEADS], gain_sums[1], done.wq_two, done.wk_two, done.wv_two, done.out_two, gain_sums[2],
        done.gate, done.up, done.down,
    )


def solution(mesh):
    tokens = P("batch", "head", None)
    rows = P("batch", None)
    columns = P(None, "head")
    split = P("batch", "head")
    every = P(None, ("batch", "head"))
    gain = P(("batch", "head"))
    return jax.shard_map(
        on_device,
        mesh=mesh,
        in_specs=(
            tokens, tokens, tokens, rows, rows, P(), columns, columns, columns, P(), columns, P(),
            columns, columns, columns, P(), P(), P(), P(), P(),
        ),
        out_specs=(
            tokens, tokens, tokens, gain, split, split, split, every, columns, gain,
            split, split, split, every, gain, every, every, every,
        ),
        check_vma=False,
    )
```

time: 398 us -> 267 us (0.67)
  Pallas kernels: 48.5 us -> 133 us
  waiting for transfers between devices: 96.8 us -> 19.7 us
  starting transfers between devices: 78.3 us -> 6.43 us
  matrix products: 93.9 us -> 52.8 us
  other arithmetic: 24.2 us -> 12.8 us
  local copies, waits for them, and re-layouts: 47.6 us -> 36.7 us
    pallas_call x4 -> x3, Pallas kernels: 48.5 us -> 133 us  [the longest x1 110 us: backward_call(): pl.pallas_call(kernel, grid=(8,), in_specs=jax.tree.leaves(in_specs), out...]
    ppermute x85 -> x12, waiting for transfers between devices: 96.8 us -> 19.7 us  [swap(): return lax.ppermute(array, axis, [(i, i ^ mask) for i in range(size)])]
    ppermute x85 -> x12, starting transfers between devices: 78.3 us -> 6.43 us  [swap(): return lax.ppermute(array, axis, [(i, i ^ mask) for i in range(size)])]
    dot_general x18 -> x2, matrix products: 45.1 us -> 5.75 us  [the longest x1 3.73 us: on_device(): jnp.einsum('sad,dt->sat', wt_two[:, :QUERY_START], mem_rows, preferred_el...]
    another operation x8 -> x4, local copies, waits for them, and re-layouts: 7.04 us -> 1.01 us  [gathered(): return jnp.stack(slots)]
    convert_element_type x16 -> x1, other arithmetic: 7.32 us -> 1.41 us  [on_device(): wide = tok.astype(F32)]
    dynamic_slice x4 -> x3, local copies, waits for them, and re-layouts: 7.38 us -> 2.87 us  [the longest x2 2.1 us: block_segments(): return lax.dynamic_slice_in_dim(mine, (me >> 1) * BLOCK, BLOCK, 0)]
    slice x8 -> x1, local copies, waits for them, and re-layouts: 4.72 us -> 0.6 us  [on_device(): tile_segments = block_segments(target_segments)[::TILE]]
  transfers between devices with their start and end apart: 85 -> 12, of which waited for: 31 -> 3; matrix products, arithmetic and copies ran while one was open for 29% -> 16% of each run, Pallas kernels for 6% -> 9%
where the time goes in v2:
time: 267 us; the launch traced here: 263 us
  Pallas kernels  133 us (50%)
  matrix products  52.8 us (20%)
  local copies, waits for them, and re-layouts  36.7 us (14%)
  waiting for transfers between devices  19.7 us (7%)
  other arithmetic  12.8 us (5%)
  starting transfers between devices  6.43 us (2%)
    pallas_call x1, Pallas kernels, backward_call(): pl.pallas_call(kernel, grid=(8,), in_specs=jax.tree.leaves(in_specs), out...  110 us
    dot_general x10, matrix products, over_tokens(): lax.dot_general(left, right, (((0,), (0,)), ((), ())), preferred_element_...  25.9 us
    pallas_call x2, Pallas kernels, attention_forward(): pl.pallas_call(kernel, grid_spec=pltpu.PrefetchScalarGridSpec(num_scalar_...  22.7 us
    unnamed x89, local copies, waits for them, and re-layouts  20.2 us
    ppermute x12, waiting for transfers between devices, swap(): return lax.ppermute(array, axis, [(i, i ^ mask) for i in range(size)])  19.7 us
    dot_general x3, matrix products, by_transpose(): lax.dot_general(left, right, (((1,), (1,)), ((), ())), preferred_element_...  11.1 us
    dot_general x4, matrix products, dot(): lax.dot_general(left, right, (((1,), (0,)), ((), ())), preferred_element_...  10 us
    ppermute x12, starting transfers between devices, swap(): return lax.ppermute(array, axis, [(i, i ^ mask) for i in range(size)])  6.43 us
  transfers between devices with their start and end apart: 12, of which 3 were waited for; matrix products, arithmetic and copies ran while one was open for 16% of the time, Pallas kernels for 9%

profile of v2, /device:TPU:0, one launch (start us, length us, event | category | flops | bytes accessed | tf_op | source)
XLA Modules:
  0.0 262.6 jit_solution(12427278227217081428)
XLA Ops:
  0.7 1.0 slice_dynamic-update-slice_fusion.3
  1.7 1.0 slice_dynamic-update-slice_fusion.2
  2.7 0.9 slice_dynamic-update-slice_fusion.7
  3.7 0.9 slice_dynamic-update-slice_fusion.6
  4.6 1.0 bitcast_dynamic-update-slice_fusion.1
  5.5 3.0 %collective-permute-start.3 = (bf16[576,768]{1,0:T(8,128)(2,1)S(1)}, bf16[576,768]{1,0:T(8,128)(2,1)}, u32[]{:S(2)}, u32[]{:S(2)}) collective-permute-start(bf16[576,768]{1,0:T(8,128)(2,1)S(1)} %bitcast_dynamic-update-slice_fusion.1), channel_id=1, source_target_pairs={{0,2},{1,3},{2,0},{3,1},{4,6},{5,7},{6,4},{7,5},{8,10},{9,11},{10,... | collective-permute-start | bytes 2654216 | tf_op jit(solution)/shard_map/ppermute | solution.py:996
  9.1 0.8 dynamic-slice_bitcast_fusion.2
  10.1 0.7 slice_dynamic-update-slice_fusion.1
  10.8 0.7 slice_dynamic-update-slice_fusion
  11.4 1.9 dynamic-slice_bitcast_fusion.1
  13.4 0.6 slice_dynamic-update-slice_fusion.5
  14.6 0.8 dynamic-slice_bitcast_fusion.5
  15.5 0.8 dynamic_slice.57
  16.9 1.3 dynamic_slice.61.memseg_ref.refs_21_
  18.8 1.7 bitcast_dynamic-update-slice_fusion
  21.1 7.2 %collective-permute-done.6 = f32[32,3]{0,1:T(4,128)S(1)} collective-permute-done((f32[32,3]{0,1:T(4,128)S(1)}, f32[32,3]{0,1:T(4,128)S(1)}, u32[]{:S(2)}, u32[]{:S(2)}) %collective-permute-start.6) | collective-permute-done | bytes 416 | tf_op jit(solution)/shard_map/ppermute | solution.py:996
  28.4 1.7 collective-permute-start.9
  30.2 0.8 copy.68
  33.1 1.2 copy.72.refs_14_
  34.2 1.3 collective-permute-done.11
  35.8 1.3 fusion.27
  37.1 1.2 copy.71.refs_13_
  38.3 1.4 fusion.39.refs_16_
  39.7 11.1 %collective-permute-done.9 = bf16[576,768]{1,0:T(8,128)(2,1)} collective-permute-done((bf16[576,768]{1,0:T(8,128)(2,1)}, bf16[576,768]{1,0:T(8,128)(2,1)}, u32[]{:S(2)}, u32[]{:S(2)}) %collective-permute-start.9) | collective-permute-done | bytes 884768 | tf_op jit(solution)/shard_map/ppermute | solution.py:996
  50.8 2.1 pad_maximum_fusion.refs_31_
  53.0 3.7 %convolution_convert_fusion = bf16[2304,512]{1,0:T(8,128)(2,1)} fusion(bf16[2304,768]{1,0:T(8,128)(2,1)S(1)} %bitcast.84, f32[768]{0:T(1024)S(1)} %copy-done.23, f32[512]{0:T(512)S(1)} %add_rsqrt_fusion.2, bf16[256,768]{1,0:T(8,128)(2,1)S(1)} %collective-permute-done.1, bf16[256,768]{1,0:T(8,128)(2,1)S(1)} %get-tuple-element.122, pred[]{:T(512)S(6)} %eq.2), kind=kOutput, calls=%fused_computation.2 | convolution fusion | flops 1818230784 | bytes 6689793 | tf_op jit(solution)/shard_map/dot_general | solution.py:38
  56.6 9.9 %shard_map.340 = (bf16[768,512]{1,0:T(8,128)(2,1)}, f32[4,8,512]{2,1,0:T(8,128)}) custom-call(s32[4]{0:T(128)} %slice.45.seg_ref.refs_24_, s32[1]{0:T(128)} %bitcast.5.where_ref, bf16[4,576,512]{2,1,0:T(8,128)(2,1)} %bitcast.99, bf16[4,576,512]{2,1,0:T(8,128)(2,1)} %bitcast.100, f32[4,32,3]{2,1,0:T(8,128)} %pad_maximum_fusion.2.tab_ref.refs_30_, ...), custom_call_target="tpu_custom_call" | custom-call | flops 805306368 | bytes 3145728 | tf_op jit(solution)/shard_map/pallas_call | solution.py:154
  66.5 2.5 multiply_reduce_fusion.3
  69.0 2.7 %pad_maximum_fusion.1.refs_32_ = bf16[4,576,768]{2,1,0:T(8,128)(2,1)S(1)} fusion(bf16[1,576,768]{2,1,0:T(8,128)(2,1)} %bitcast.25, bf16[1,576,768]{2,1,0:T(8,128)(2,1)} %bitcast.24, bf16[1,576,768]{2,1,0:T(8,128)(2,1)} %bitcast.23, bf16[1,576,768]{2,1,0:T(8,128)(2,1)} %bitcast.22), kind=kLoop, calls=%fused_computation.17 | loop fusion | flops 5308416 | bytes 7077888 | tf_op jit(solution)/shard_map/stack | solution.py:1061
  71.8 2.0 convolution_convert_fusion.5.q_ref.refs_22_
  73.8 3.7 %fusion.12.kv_ref.refs_7_ = bf16[4,384,512]{2,1,0:T(8,128)(2,1)} fusion(bf16[4,576,768]{2,1,0:T(8,128)(2,1)S(1)} %pad_maximum_fusion.1.refs_32_, bf16[256,768]{1,0:T(8,128)(2,1)} %collective-permute-done.11, bf16[256,768]{1,0:T(8,128)(2,1)S(1)} %copy-done.6, pred[]{:T(512)S(6)} %eq.2), kind=kOutput, calls=%fused_computation.24 | convolution fusion | flops 1212284928 | bytes 4718593 | tf_op jit(solution)/shard_map/sad,dt->sat/dot_general | solution.py:1079
  77.5 12.8 %shard_map.341 = (bf16[768,512]{1,0:T(8,128)(2,1)}, f32[4,8,512]{2,1,0:T(8,128)}) custom-call(s32[4]{0:T(128)} %slice.45.seg_ref.refs_24_, s32[1]{0:T(128)} %bitcast.5.where_ref, bf16[4,384,512]{2,1,0:T(8,128)(2,1)} %fusion.12.kv_ref.refs_7_, bf16[4,192,512]{2,1,0:T(8,128)(2,1)} %convolution_convert_fusion.5.q_ref.refs_22_, ...), custom_call_target="tpu_custom_call" | custom-call | flops 805306368 | bytes 3145728 | tf_op jit(solution)/shard_map/pallas_call | solution.py:154
  90.4 2.6 multiply_reduce_fusion.2
  93.2 1.8 fusion.41
  95.0 1.8 fusion.42
  96.9 6.1 %multiply_convert_fusion = (bf16[512,2048]{1,0:T(8,128)(2,1)S(1)}, bf16[512,2048]{1,0:T(8,128)(2,1)S(1)}, bf16[512,2048]{1,0:T(8,128)(2,1)S(1)}) fusion(f32[512,2048]{1,0:T(8,128)S(1)} %fusion.41, f32[512,2048]{1,0:T(8,128)S(1)} %fusion.42, bf16[2048,768]{1,0:T(8,128)(2,1)S(1)} %copy-done.30, bf16[256,768]{1,0:T(8,128)(2,1)} %collective-permute-done, ...), kind=kOutput, calls=%fused_computation.13 | convolution fusion | flops 1639317504 | bytes 18612224 | tf_op jit(solution)/shard_map/dot_general | solution.py:1016
  103.0 1.8 fusion.43
  104.9 2.5 convolution_convert_fusion.2
  107.3 2.5 convolution_convert_fusion.1
  109.8 2.5 convolution_convert_fusion.3
  112.3 2.4 convolution_convert_fusion.4
  114.7 1.1 fusion.38
  115.8 3.2 %multiply_reduce_fusion = (f32[512]{0:T(512)S(1)}, f32[768]{0:T(1024)S(1)}, f32[512,768]{1,0:T(8,128)}) fusion(f32[512,768]{1,0:T(8,128)S(1)} %get-tuple-element.129, f32[768]{0:T(1024)S(1)} %copy-done.26, f32[512]{0:T(512)S(1)} %add_rsqrt_fusion, f32[512,768]{1,0:T(8,128)S(1)} %fusion.43, bf16[512,2048]{1,0:T(8,128)(2,1)S(1)} %get-tuple-element.116, ...), kind=kOutput, calls=%fused_computation.26 | convolution fusion | flops 1613363968 | bytes 9971712 | tf_op jit(solution)/shard_map/dot_general | solution.py:1016
  119.0 2.7 %add_convert_fusion = bf16[512,768]{1,0:T(8,128)(2,1)} fusion(f32[512,768]{1,0:T(8,128)S(1)} %get-tuple-element.129, bf16[512,2048]{1,0:T(8,128)(2,1)S(1)} %get-tuple-element.114, bf16[2048,768]{1,0:T(8,128)(2,1)S(1)} %copy-done.30), kind=kOutput, calls=%fused_computation.27 | convolution fusion | flops 1611399168 | bytes 7602176 | tf_op jit(solution)/shard_map/dot_general | solution.py:38
  122.3 1.2 copy.73.refs_15_
  123.5 2.9 %convolution_convert_fusion.6 = bf16[768,512]{1,0:T(8,128)(2,1)} fusion(bf16[512,2048]{1,0:T(8,128)(2,1)} %copy-done.31, s32[]{:T(128)S(6)} %select_n.74, bf16[256,768]{1,0:T(8,128)(2,1)} %collective-permute-done, bf16[256,768]{1,0:T(8,128)(2,1)S(1)} %get-tuple-element.117, pred[]{:T(512)S(6)} %eq.2), kind=kOutput, calls=%fused_computation.39 | convolution fusion | flops 406585344 | bytes 2097157 | tf_op jit(solution)/shard_map/dot_general | solution.py:1012
  126.4 2.7 %convolution_convert_fusion.8 = bf16[768,512]{1,0:T(8,128)(2,1)} fusion(bf16[512,2048]{1,0:T(8,128)(2,1)S(1)} %copy-done.32, s32[]{:T(128)S(6)} %select_n.71, bf16[256,768]{1,0:T(8,128)(2,1)} %collective-permute-done, bf16[256,768]{1,0:T(8,128)(2,1)S(1)} %get-tuple-element.117, pred[]{:T(512)S(6)} %eq.2), kind=kOutput, calls=%fused_computation.41 | convolution fusion | flops 406585344 | bytes 2097157 | tf_op jit(solution)/shard_map/dot_general | solution.py:1012
  129.1 2.6 convolution_convert_fusion.7
  131.7 2.8 %convolution_convert_fusion.9 = bf16[768,512]{1,0:T(8,128)(2,1)} fusion(bf16[512,2048]{1,0:T(8,128)(2,1)S(1)} %copy-done.32, s32[]{:T(128)S(6)} %select_n.70, bf16[256,768]{1,0:T(8,128)(2,1)} %collective-permute-done, bf16[256,768]{1,0:T(8,128)(2,1)S(1)} %get-tuple-element.117, pred[]{:T(512)S(6)} %eq.2), kind=kOutput, calls=%fused_computation.42 | convolution fusion | flops 406585344 | bytes 2097157 | tf_op jit(solution)/shard_map/dot_general | solution.py:1012
  134.6 2.7 %subtract_add_fusion.refs_9_ = f32[512,768]{1,0:T(8,128)} fusion(f32[512,768]{1,0:T(8,128)S(1)} %get-tuple-element.129, f32[512,768]{1,0:T(8,128)S(1)} %copy-done.4, f32[512]{0:T(512)S(1)} %fusion.36, f32[768]{0:T(1024)S(1)} %copy-done.26, f32[512]{0:T(512)S(1)} %add_rsqrt_fusion, bf16[256,768]{1,0:T(8,128)(2,1)S(1)} %get-tuple-element.117, ...), kind=kLoop, calls=%fused_computation.25 | loop fusion | flops 5898240 | bytes 5512193 | tf_op jit(solution)/shard_map/add | solution.py:1100
  137.2 110.3 %shard_map.342 = (f32[32,128]{1,0:T(8,128)}, f32[2048,24]{1,0:T(8,128)}, f32[8,768]{1,0:T(8,128)}, f32[768,64]{1,0:T(8,128)}, bf16[2,256,768]{2,1,0:T(8,128)(2,1...) custom-call(f32[1,768]{1,0:T(1,128)} %reshape.122.refs_0_, ...), custom_call_target="tpu_custom_call" | custom-call | flops 20000000000 | bytes 40000000 | tf_op jit(solution)/shard_map/pallas_call | solution.py:979
  247.6 2.0 copy.77
  249.6 1.8 copy.78
  251.4 1.0 copy.79
  252.4 0.8 copy.74
  253.2 0.8 copy.76
  253.9 0.8 constant_dynamic-slice_fusion
  255.2 0.7 copy.75
  255.9 0.9 copy.97
  256.8 0.9 copy.98
  257.7 0.9 copy.99
  258.5 0.6 copy.100
  261.1 0.6 copy.104
  261.8 0.6 copy.105
  (105 shorter events, 9.1 us)
Async XLA Ops:
  0.7 7.9 %copy-start.27 = (f32[32,3]{0,1:T(4,128)S(1)}, f32[32,3]{0,1:T(4,128)}, u32[]{:S(2)}) copy-start(f32[32,3]{0,1:T(4,128)} %param.31) | copy-start | bytes 1156
  0.7 8.4 %copy-start.11 = (bf16[2,256,768]{2,1,0:T(8,128)(2,1)S(1)}, bf16[2,256,768]{2,1,0:T(8,128)(2,1)}, u32[]{:S(2)}) copy-start(bf16[2,256,768]{2,1,0:T(8,128)(2,1)} %param.21) | copy-start | bytes 2359300
  1.7 8.4 %copy-start.15 = (bf16[768,192]{0,1:T(8,128)(2,1)S(1)}, bf16[768,192]{0,1:T(8,128)(2,1)}, u32[]{:S(2)}) copy-start(bf16[768,192]{0,1:T(8,128)(2,1)} %param.34) | copy-start | bytes 884740
  2.7 8.1 %copy-start.16 = (bf16[768,192]{0,1:T(8,128)(2,1)S(1)}, bf16[768,192]{0,1:T(8,128)(2,1)}, u32[]{:S(2)}) copy-start(bf16[768,192]{0,1:T(8,128)(2,1)} %param.35) | copy-start | bytes 884740
  5.5 25.7 %collective-permute-start.3 = (bf16[576,768]{1,0:T(8,128)(2,1)S(1)}, bf16[576,768]{1,0:T(8,128)(2,1)}, u32[]{:S(2)}, u32[]{:S(2)}) collective-permute-start(bf16[576,768]{1,0:T(8,128)(2,1)S(1)} %bitcast_dynamic-update-slice_fusion.1), channel_id=1, source_target_pairs={{0,2},{1,3},{2,0},{3,1},{4,6},{5,7},{6,4},{7,5},{8,10},{9,11},{10,... | collective-permute-start | bytes 2654216 | tf_op jit(solution)/shard_map/ppermute | solution.py:996
  8.6 42.3 %collective-permute-start.2 = (bf16[576,768]{1,0:T(8,128)(2,1)S(1)}, bf16[576,768]{1,0:T(8,128)(2,1)}, u32[]{:S(2)}, u32[]{:S(2)}) collective-permute-start(bf16[576,768]{1,0:T(8,128)(2,1)S(1)} %bitcast_dynamic-update-slice_fusion.1), channel_id=1, source_target_pairs={{0,1},{1,0},{2,3},{3,2},{4,5},{5,4},{6,7},{7,6},{8,9},{9,8},{10,11... | collective-permute-start | bytes 2654216 | tf_op jit(solution)/shard_map/ppermute | solution.py:996
  8.6 19.8 %collective-permute-start.6 = (f32[32,3]{0,1:T(4,128)S(1)}, f32[32,3]{0,1:T(4,128)S(1)}, u32[]{:S(2)}, u32[]{:S(2)}) collective-permute-start(f32[32,3]{0,1:T(4,128)S(1)} %copy-done.27), channel_id=1, source_target_pairs={{0,2},{1,3},{2,0},{3,1},{4,6},{5,7},{6,4},{7,5},{8,10},{9,11},{10,... | collective-permute-start | bytes 1160 | tf_op jit(solution)/shard_map/ppermute | solution.py:996
  8.7 19.7 %collective-permute-start.5 = (f32[32,3]{0,1:T(4,128)S(1)}, f32[32,3]{0,1:T(4,128)}, u32[]{:S(2)}, u32[]{:S(2)}) collective-permute-start(f32[32,3]{0,1:T(4,128)S(1)} %copy-done.27), channel_id=1, source_target_pairs={{0,1},{1,0},{2,3},{3,2},{4,5},{5,4},{6,7},{7,6},{8,9},{9,8},{10,11... | collective-permute-start | bytes 1160 | tf_op jit(solution)/shard_map/ppermute | solution.py:996
  9.9 4.8 %copy-start.12 = (bf16[2,256,768]{2,1,0:T(8,128)(2,1)S(1)}, bf16[2,256,768]{2,1,0:T(8,128)(2,1)}, u32[]{:S(2)}) copy-start(bf16[2,256,768]{2,1,0:T(8,128)(2,1)} %param.23) | copy-start | bytes 2359300
  9.9 22.3 %collective-permute-start.1 = (bf16[256,768]{1,0:T(8,128)(2,1)}, bf16[256,768]{1,0:T(8,128)(2,1)S(1)}, u32[]{:S(2)}, u32[]{:S(2)}) collective-permute-start(bf16[256,768]{1,0:T(8,128)(2,1)} %get-tuple-element.121), channel_id=1, source_target_pairs={{0,1},{1,0},{2,3},{3,2},{4,5},{5,4},{6,7},{7,6},{8,9},{9,8},{10,11... | collective-permute-start | bytes 1179656 | tf_op jit(solution)/shard_map/ppermute | solution.py:996
  11.4 6.8 %copy-start.23 = (f32[768]{0:T(1024)S(1)}, f32[768]{0:T(1024)}, u32[]{:S(2)}) copy-start(f32[768]{0:T(1024)} %param.26) | copy-start | bytes 9220
  13.4 22.4 %copy-start.5 = (bf16[256,768]{1,0:T(8,128)(2,1)}, bf16[256,768]{1,0:T(8,128)(2,1)S(1)}, u32[]{:S(2)}) copy-start(bf16[256,768]{1,0:T(8,128)(2,1)S(1)} %get-tuple-element.119) | copy-start | bytes 1179652
  13.4 7.2 %copy-start.24 = (f32[768]{0:T(1024)S(1)}, f32[768]{0:T(1024)}, u32[]{:S(2)}) copy-start(f32[768]{0:T(1024)} %param.32) | copy-start | bytes 9220
  28.3 2.6 collective-permute-start.7
  28.4 22.4 %collective-permute-start.9 = (bf16[576,768]{1,0:T(8,128)(2,1)}, bf16[576,768]{1,0:T(8,128)(2,1)}, u32[]{:S(2)}, u32[]{:S(2)}) collective-permute-start(bf16[576,768]{1,0:T(8,128)(2,1)} %bitcast_dynamic-update-slice_fusion), channel_id=1, source_target_pairs={{0,2},{1,3},{2,0},{3,1},{4,6},{5,7},{6,4},{7,5},{8,10},{9,11},{10,... | collective-permute-start | bytes 2654216 | tf_op jit(solution)/shard_map/ppermute | solution.py:996
  30.9 38.0 %collective-permute-start.8 = (bf16[576,768]{1,0:T(8,128)(2,1)}, bf16[576,768]{1,0:T(8,128)(2,1)}, u32[]{:S(2)}, u32[]{:S(2)}) collective-permute-start(bf16[576,768]{1,0:T(8,128)(2,1)} %bitcast_dynamic-update-slice_fusion), channel_id=1, source_target_pairs={{0,1},{1,0},{2,3},{3,2},{4,5},{5,4},{6,7},{7,6},{8,9},{9,8},{10,11... | collective-permute-start | bytes 2654216 | tf_op jit(solution)/shard_map/ppermute | solution.py:996
  31.3 19.6 %collective-permute-start.4 = (bf16[576,768]{1,0:T(8,128)(2,1)}, bf16[576,768]{1,0:T(8,128)(2,1)}, u32[]{:S(2)}, u32[]{:S(2)}) collective-permute-start(bf16[576,768]{1,0:T(8,128)(2,1)} %collective-permute-done.3), channel_id=1, source_target_pairs={{0,1},{1,0},{2,3},{3,2},{4,5},{5,4},{6,7},{7,6},{8,9},{9,8},{10,11... | collective-permute-start | bytes 2654216 | tf_op jit(solution)/shard_map/ppermute | solution.py:996
  32.2 3.4 %collective-permute-start.11 = (bf16[256,768]{1,0:T(8,128)(2,1)}, bf16[256,768]{1,0:T(8,128)(2,1)}, u32[]{:S(2)}, u32[]{:S(2)}) collective-permute-start(bf16[256,768]{1,0:T(8,128)(2,1)} %get-tuple-element.120), channel_id=1, source_target_pairs={{0,1},{1,0},{2,3},{3,2},{4,5},{5,4},{6,7},{7,6},{8,9},{9,8},{10,11... | collective-permute-start | bytes 1179656 | tf_op jit(solution)/shard_map/ppermute | solution.py:996
  35.5 61.3 %collective-permute-start = (bf16[256,768]{1,0:T(8,128)(2,1)}, bf16[256,768]{1,0:T(8,128)(2,1)}, u32[]{:S(2)}, u32[]{:S(2)}) collective-permute-start(bf16[256,768]{1,0:T(8,128)(2,1)} %get-tuple-element.118), channel_id=1, source_target_pairs={{0,1},{1,0},{2,3},{3,2},{4,5},{5,4},{6,7},{7,6},{8,9},{9,8},{10,11... | collective-permute-start | bytes 1179656 | tf_op jit(solution)/shard_map/ppermute | solution.py:996
  50.8 18.2 %collective-permute-start.10 = (bf16[576,768]{1,0:T(8,128)(2,1)}, bf16[576,768]{1,0:T(8,128)(2,1)}, u32[]{:S(2)}, u32[]{:S(2)}) collective-permute-start(bf16[576,768]{1,0:T(8,128)(2,1)} %collective-permute-done.9), channel_id=1, source_target_pairs={{0,1},{1,0},{2,3},{3,2},{4,5},{5,4},{6,7},{7,6},{8,9},{9,8},{10,11... | collective-permute-start | bytes 2654216 | tf_op jit(solution)/shard_map/ppermute | solution.py:996
  52.9 3.7 %copy-start.1 = (bf16[4,576,768]{2,1,0:T(8,128)(2,1)}, bf16[4,576,768]{2,1,0:T(8,128)(2,1)S(1)}, u32[]{:S(2)}) copy-start(bf16[4,576,768]{2,1,0:T(8,128)(2,1)S(1)} %pad_maximum_fusion.refs_31_) | copy-start | bytes 10616836
  69.0 45.8 %copy-start = (f32[512,768]{1,0:T(8,128)}, f32[512,768]{1,0:T(8,128)S(1)}, u32[]{:S(2)}) copy-start(f32[512,768]{1,0:T(8,128)S(1)} %get-tuple-element.127.refs_12_) | copy-start | bytes 4718596
  71.7 2.0 copy-start.2
  71.7 2.0 copy-start.6
  90.3 2.6 copy-start.26
  90.3 2.8 %copy-start.29 = (bf16[768,2048]{1,0:T(8,128)(2,1)S(1)}, bf16[768,2048]{1,0:T(8,128)(2,1)}, u32[]{:S(2)}) copy-start(bf16[768,2048]{1,0:T(8,128)(2,1)} %param.39) | copy-start | bytes 9437188
  93.2 1.9 copy-start.28
  95.0 1.9 copy-start.30
  103.0 16.0 %copy-start.31 = (bf16[512,2048]{1,0:T(8,128)(2,1)}, bf16[512,2048]{1,0:T(8,128)(2,1)S(1)}, u32[]{:S(2)}) copy-start(bf16[512,2048]{1,0:T(8,128)(2,1)S(1)} %get-tuple-element.114) | copy-start | bytes 6291460
  119.0 3.3 %copy-start.3 = (bf16[768,512]{0,1:T(8,128)(2,1)S(1)}, bf16[768,512]{0,1:T(8,128)(2,1)}, u32[]{:S(2)}) copy-start(bf16[768,512]{0,1:T(8,128)(2,1)} %fusion.38) | copy-start | bytes 2359300
  123.5 2.9 %copy-start.32 = (bf16[512,2048]{1,0:T(8,128)(2,1)S(1)}, bf16[512,2048]{1,0:T(8,128)(2,1)}, u32[]{:S(2)}) copy-start(bf16[512,2048]{1,0:T(8,128)(2,1)} %copy-done.31) | copy-start | bytes 6291460
  131.7 2.8 %copy-start.4 = (f32[512,768]{1,0:T(8,128)S(1)}, f32[512,768]{1,0:T(8,128)}, u32[]{:S(2)}) copy-start(f32[512,768]{1,0:T(8,128)} %get-tuple-element.130) | copy-start | bytes 4718596
  247.5 3.8 %copy-start.7 = (f32[2048,24]{1,0:T(8,128)S(1)}, f32[2048,24]{1,0:T(8,128)}, u32[]{:S(2)}) copy-start(f32[2048,24]{1,0:T(8,128)} %get-tuple-element.111) | copy-start | bytes 589828
  247.5 4.8 %copy-start.14 = (f32[768,24]{1,0:T(8,128)S(1)}, f32[768,24]{1,0:T(8,128)}, u32[]{:S(2)}) copy-start(f32[768,24]{1,0:T(8,128)} %get-tuple-element.101) | copy-start | bytes 221188
  247.6 5.6 %copy-start.13 = (f32[768,24]{1,0:T(8,128)S(1)}, f32[768,24]{1,0:T(8,128)}, u32[]{:S(2)}) copy-start(f32[768,24]{1,0:T(8,128)} %get-tuple-element.107) | copy-start | bytes 221188
  247.6 7.7 %copy-start.25 = (f32[32,128]{1,0:T(8,128)S(1)}, f32[32,128]{1,0:T(8,128)}, u32[]{:S(2)}) copy-start(f32[32,128]{1,0:T(8,128)} %get-tuple-element.50) | copy-start | bytes 49156
  247.6 8.3 %copy-start.10 = (bf16[2,256,768]{2,1,0:T(8,128)(2,1)S(1)}, bf16[2,256,768]{2,1,0:T(8,128)(2,1)}, u32[]{:S(2)}) copy-start(bf16[2,256,768]{2,1,0:T(8,128)(2,1)} %get-tuple-element.149) | copy-start | bytes 2359300
  252.4 4.4 %copy-start.9 = (bf16[2,256,768]{2,1,0:T(8,128)(2,1)S(1)}, bf16[2,256,768]{2,1,0:T(8,128)(2,1)}, u32[]{:S(2)}) copy-start(bf16[2,256,768]{2,1,0:T(8,128)(2,1)} %get-tuple-element.150) | copy-start | bytes 2359300
  255.9 1.8 copy-start.8
  256.8 1.8 copy-start.22
  256.8 2.4 copy-start.21
  256.8 3.1 %copy-start.20 = (f32[96,192]{1,0:T(8,128)S(1)}, f32[96,192]{1,0:T(8,128)}, u32[]{:S(2)}) copy-start(f32[96,192]{1,0:T(8,128)} %get-tuple-element.155) | copy-start | bytes 221188
  256.8 3.7 %copy-start.19 = (f32[96,192]{1,0:T(8,128)S(1)}, f32[96,192]{1,0:T(8,128)}, u32[]{:S(2)}) copy-start(f32[96,192]{1,0:T(8,128)} %get-tuple-element.159) | copy-start | bytes 221188
  257.7 3.5 %copy-start.18 = (f32[96,192]{1,0:T(8,128)S(1)}, f32[96,192]{1,0:T(8,128)}, u32[]{:S(2)}) copy-start(f32[96,192]{1,0:T(8,128)} %get-tuple-element.160) | copy-start | bytes 221188
  257.7 4.1 %copy-start.17 = (f32[96,192]{1,0:T(8,128)S(1)}, f32[96,192]{1,0:T(8,128)}, u32[]{:S(2)}) copy-start(f32[96,192]{1,0:T(8,128)} %get-tuple-element.161) | copy-start | bytes 221188

commit v3 on v2

--- a/solution.py
+++ b/solution.py
@@ -31,7 +31,8 @@
     for edge in bucket_edges():
         ids += np.arange(2 * TILE) >= edge
     assert bucket_edges()[-1] <= TILE + 1
-    return (np.arange(buckets)[:, None] == ids[None, :]).astype(np.float32)
+    assert buckets <= TILE and ids[-1] == buckets - 1
+    return (np.arange(TILE)[:, None] == ids[None, :]).astype(np.float32)
 
 
 def dot(left, right):
@@ -58,14 +59,15 @@
 
 
 def bias_tiles(table, index, one_hot):
-    column = table[:, index : index + 1]
-    by_distance = jnp.sum(column * one_hot, axis=0, keepdims=True)
+    by_distance = jnp.dot(
+        table, one_hot, precision=lax.Precision.HIGHEST, preferred_element_type=F32
+    )[index : index + 1]
     wide = jnp.broadcast_to(by_distance, (TILE, 2 * TILE))
     turned = pltpu.roll(wide, 0, 1, stride=1, stride_axis=0)
     key = lax.broadcasted_iota(jnp.int32, (TILE, TILE), 0)
     query = lax.broadcasted_iota(jnp.int32, (TILE, TILE), 1)
     near = jnp.where(key <= query, turned[:, :TILE], MASKED)
-    return near, turned[:, TILE:], table[table.shape[0] - 1, index]
+    return near, turned[:, TILE:], by_distance[0, 2 * TILE - 1]
 
 
 def self_tile(scores, key_tile, query_tile, tiles, seg_ref, base):
@@ -79,15 +81,13 @@
     return scores + (far + shift)
 
 
-def self_forward_kernel(seg_ref, where_ref, kv_ref, q_ref, tab_ref, hot_ref, o_ref, lse_ref):
-    key_values = jnp.transpose(kv_ref[0])
-    table = tab_ref[0]
+def self_forward(kv, q, table, one_hot, seg_ref, out, lse, tick):
+    key_values = jnp.transpose(kv[...])
     for index in range(HEADS):
         rows = slice(index * SIZE, (index + 1) * SIZE)
         keys = key_values[:, lanes_of(KEY_AT[index])]
-        value_rows = kv_ref[0, rows_of(VALUE_AT[index]), :]
-        query = spread(q_ref[0, rows, :], KEY_AT[index][1])
-        tiles = bias_tiles(table, index, hot_ref[...])
+        query = spread(q[rows, :], KEY_AT[index][1])
+        tiles = bias_tiles(table, index, one_hot)
         for half in range(2):
             end = (half + 1) * HALF
             scores = dot(keys[:end], query[:, half * HALF : (half + 1) * HALF])
@@ -113,70 +113,38 @@
                     probs.append(jnp.zeros((TILE, TILE), BF16))
                 columns.append(jnp.concatenate(probs, axis=0))
                 totals.append(total)
-                lse_ref[0, index : index + 1, query_tile * TILE : (query_tile + 1) * TILE] = top + jnp.log(total)
+                lse[index : index + 1, query_tile * TILE : (query_tile + 1) * TILE] = top + jnp.log(total)
             weights = jnp.concatenate(columns, axis=1)
-            context = dot(value_rows[:, :end], weights)
+            context = dot(kv[rows_of(VALUE_AT[index]), :end], weights)
             context = context / jnp.concatenate(totals, axis=1)
-            o_ref[rows, half * HALF : (half + 1) * HALF] = context.astype(BF16)
+            out[rows, half * HALF : (half + 1) * HALF] = context.astype(BF16)
+        tick(index)
 
 
 def key_mask(seg_ref, memseg, mask_ref):
     rows = jnp.transpose(jnp.broadcast_to(memseg.astype(F32), (TILE, BLOCK)))
     for tile in range(BLOCK // TILE):
         wanted = seg_ref[tile].astype(F32)
-        mask_ref[:, tile * TILE : (tile + 1) * TILE] = jnp.where(rows == wanted, 0.0, MASKED).astype(mask_ref.dtype)
-
-
-def cross_forward_kernel(seg_ref, where_ref, kv_ref, q_ref, memseg_ref, o_ref, lse_ref, mask_ref):
-    @pl.when(pl.program_id(0) == 0)
-    def _():
-        key_mask(seg_ref, memseg_ref[...], mask_ref)
-
-    key_values = jnp.transpose(kv_ref[0])
+        shift = jnp.where(rows == wanted, 0.0, MASKED)
+        mask_ref[:, tile * TILE : (tile + 1) * TILE] = shift.astype(mask_ref.dtype)
+
+
+def cross_forward(kv, q, mask, out, lse, tick):
+    key_values = jnp.transpose(kv[...])
     for index in range(HEADS):
         rows = slice(index * SIZE, (index + 1) * SIZE)
         keys = key_values[:, lanes_of(KEY_AT[index])]
-        value_rows = kv_ref[0, rows_of(VALUE_AT[index]), :]
-        query = spread(q_ref[0, rows, :], KEY_AT[index][1])
+        query = spread(q[rows, :], KEY_AT[index][1])
         for half in range(2):
             lanes = slice(half * HALF, (half + 1) * HALF)
-            scores = dot(keys, query[:, lanes]) + mask_ref[:, lanes]
+            scores = dot(keys, query[:, lanes]) + mask[:, lanes]
             top = jnp.max(scores, axis=0, keepdims=True)
             probs = jnp.exp(scores - top)
             total = jnp.sum(probs, axis=0, keepdims=True)
-            context = dot(value_rows, probs.astype(BF16)) / total
-            o_ref[rows, lanes] = context.astype(BF16)
-            lse_ref[0, index : index + 1, lanes] = top + jnp.log(total)
-
-
-def attention_forward(kernel, segs, here, kv, kv_part, q, q_part, extra, extra_specs, scratch):
-    slots = kv.shape[0]
-    return pl.pallas_call(
-        kernel,
-        grid_spec=pltpu.PrefetchScalarGridSpec(
-            num_scalar_prefetch=2,
-            grid=(slots,),
-            in_specs=[
-                pl.BlockSpec((1, 2 * GROUP, BLOCK), lambda s, seg, at: (s, kv_part, 0)),
-                pl.BlockSpec((1, GROUP, BLOCK), lambda s, seg, at: (s, q_part, 0)),
-            ]
-            + extra_specs,
-            out_specs=[
-                pl.BlockSpec((GROUP, BLOCK), lambda s, seg, at: (jnp.bitwise_xor(at[0], s), 0)),
-                pl.BlockSpec((1, 8, BLOCK), lambda s, seg, at: (s, 0, 0)),
-            ],
-            scratch_shapes=scratch,
-        ),
-        out_shape=(
-            jax.ShapeDtypeStruct((slots * GROUP, BLOCK), BF16),
-            jax.ShapeDtypeStruct((slots, 8, BLOCK), F32),
-        ),
-        cost_estimate=pl.CostEstimate(
-            flops=4 * slots * GROUP * BLOCK * BLOCK,
-            bytes_accessed=8 * slots * GROUP * BLOCK,
-            transcendentals=slots * HEADS * BLOCK * BLOCK,
-        ),
-    )(segs, here, kv, q, *extra)
+            context = dot(kv[rows_of(VALUE_AT[index]), :], probs.astype(BF16)) / total
+            out[rows, lanes] = context.astype(BF16)
+            lse[index : index + 1, lanes] = top + jnp.log(total)
+        tick(index)
 
 
 def grow(old, new):
@@ -256,6 +224,23 @@
     sums_ref[:, QUERY_START : QUERY_START + GROUP] = jnp.transpose(dq_ref[...])
 
 
+def row_of(ref):
+    return jnp.reshape(ref[...], (1, ref.shape[0]))
+
+
+class Tiles:
+    def __init__(self, place, ref):
+        self.place, self.ref = place, ref
+
+    def __getitem__(self, tile):
+        return self.ref[self.place.core, self.place.y * BLOCK + tile * TILE]
+
+
+def key_segments(place, ref):
+    lanes = pl.ds(pl.multiple_of(place.y * BLOCK, BLOCK), BLOCK)
+    return jnp.where(place.core == 0, ref[0:1, lanes], ref[1:2, lanes])
+
+
 class Read:
     def __init__(self, kv, k, q, do, o, lse):
         self.kv, self.k, self.q, self.do, self.o, self.lse = kv, k, q, do, o, lse
@@ -456,10 +441,10 @@
     def store(self, out, offset, half):
         self.swap.got()
         lanes = self.room.other.shape[1]
-        core = self.place.core
-        for which, value in ((core, self.room.last[core]), (1 - core, self.room.other[...])):
-            at = pl.ds(pl.multiple_of(which * half + offset, 8), lanes)
-            out[at, :] = jnp.transpose(value)
+        mine, other = self.room.last[self.place.core], self.room.other[...]
+        for which in range(2):
+            at = slice(which * half + offset, which * half + offset + lanes)
+            out[:, at] = jnp.where(self.place.core == which, mine, other)
 
     def sent(self):
         self.swap.sent()
@@ -532,6 +517,7 @@
     step = pl.program_id(0)
     core = place.core
     copies = Copies(r.send, r.recv)
+    segs = Tiles(place, ins.segs)
 
     shared = Named({
         name: Shared(
@@ -621,7 +607,7 @@
             h = hidden[rows, :].astype(F32)
             e = incoming[rows, :]
             scale = lax.rsqrt(jnp.mean(h * h, axis=-1, keepdims=True) + NORM_EPS)
-            weighted = e * gain[...]
+            weighted = e * row_of(gain)
             inner = jnp.mean(weighted * h, axis=-1, keepdims=True)
             result = onto[rows, :] + weighted * scale - h * (scale * scale * scale * inner)
             total = total + jnp.sum(e * h * scale, axis=0, keepdims=True)
@@ -686,7 +672,7 @@
         for part in range(4):
             rows = slice(part * TILE, (part + 1) * TILE)
             r.branch[:, rows] = jnp.transpose(r.after[rows, :].astype(BF16))
-        key_mask(ins.segs, ins.memsegs[...], r.mask)
+        key_mask(segs, key_segments(place, ins.memsegs), r.mask)
         wo_two.wait()
         ctx_two.wait()
         layer_in.wait()
@@ -697,7 +683,7 @@
         n_two.wait()
         mem.wait()
         r.gains[...] = jnp.zeros_like(r.gains)
-        r.gains[2:3, :] = ins.ff_gain_grad[...]
+        r.gains[2:3, :] = row_of(ins.ff_gain_grad)
 
     slot = 3 - step % 4
     odd = slot % 2 == 1
@@ -771,27 +757,25 @@
             kept[key] = kept[key] + ds if key in kept else ds
 
         attention_back(
-            read, lambda scores, index, kt, qt: self_tile(scores, kt, qt, tiles[index], ins.segs, 0), True, note,
+            read, lambda scores, index, kt, qt: self_tile(scores, kt, qt, tiles[index], segs, 0), True, note,
             r.dq, r.dqkv, lambda h: tick(range(4, 8), h),
         )
-        buckets = one_hot.shape[0]
-        lane = lax.broadcasted_iota(jnp.int32, (buckets, TILE), 1)
-        bucket = lax.broadcasted_iota(jnp.int32, (buckets, TILE), 0)
         key = lax.broadcasted_iota(jnp.int32, (TILE, TILE), 0)
         query = lax.broadcasted_iota(jnp.int32, (TILE, TILE), 1)
         flip = (key + query == TILE - 1).astype(F32)
-        table_grad = jnp.zeros((buckets, TILE), F32)
+        row = lax.broadcasted_iota(jnp.int32, (8, 2 * TILE), 0)
+        lane = lax.broadcasted_iota(jnp.int32, (8, 2 * TILE), 1)
+        by_distance = jnp.zeros((8, 2 * TILE), F32)
         for index in range(HEADS):
             both = jnp.concatenate((kept[index, 0], kept[index, 1]), axis=1)
             both = jnp.dot(flip, both, precision=lax.Precision.HIGHEST, preferred_element_type=F32)
-            turned = pltpu.roll(both, TILE + 1, 1, stride=1, stride_axis=0)
-            by_distance = jnp.sum(turned, axis=0, keepdims=True)
-            column = jnp.sum(by_distance * one_hot, axis=1, keepdims=True)
+            turned = jnp.sum(pltpu.roll(both, TILE + 1, 1, stride=1, stride_axis=0), axis=0, keepdims=True)
             far_total = jnp.sum(jnp.sum(kept[index, 2], axis=0, keepdims=True), axis=1, keepdims=True)
-            column = jnp.where(bucket == buckets - 1, column + far_total, column)
-            table_grad = table_grad + jnp.where(lane == index, column, 0.0)
-        r.bias[slot] = table_grad
-
+            turned = turned + jnp.where(lane[:1] == 2 * TILE - 1, far_total, 0.0)
+            by_distance = by_distance + jnp.where(row == index, turned, 0.0)
+        r.bias[slot] = lax.dot_general(
+            by_distance, one_hot, (((1,), (1,)), ((), ())), precision=lax.Precision.HIGHEST, preferred_element_type=F32
+        )
         for k, j in ((4, 1), (6, 0)):
 
             @pl.when(step == k)
@@ -860,14 +844,14 @@
             bias_total = bias_total + r.bias_got[4 + k]
         outs.gains[...] = gain_total
         outs.bias[...] = bias_total
-        sh.up.store(outs.up, 0, outs.up.shape[0] // 2)
-        sh.down_a.store(outs.down, 0, outs.down.shape[0] // 2)
-        sh.down_b.store(outs.down, outs.down.shape[0] // 4, outs.down.shape[0] // 2)
-        sh.gate.store(outs.gate, 0, outs.gate.shape[0] // 2)
-        sh.out_two.store(outs.out_two, 0, outs.out_two.shape[0] // 2)
+        sh.up.store(outs.up, 0, outs.up.shape[1] // 2)
+        sh.down_a.store(outs.down, 0, outs.down.shape[1] // 2)
+        sh.down_b.store(outs.down, outs.down.shape[1] // 4, outs.down.shape[1] // 2)
+        sh.gate.store(outs.gate, 0, outs.gate.shape[1] // 2)
+        sh.out_two.store(outs.out_two, 0, outs.out_two.shape[1] // 2)
         sh.out_one.last()
         outs.wq_one[...] = sl.q_one.finish()
-        sh.out_one.store(outs.out_one, 0, outs.out_one.shape[0] // 2)
+        sh.out_one.store(outs.out_one, 0, outs.out_one.shape[1] // 2)
         for name in SHARED_ORDER:
             unit = getattr(shared, name)
             unit.sent()
@@ -917,14 +901,13 @@
         return jax.ShapeDtypeStruct((rows, columns), F32)
 
     head = wide(share, GROUP)
-    buckets = operands["hot"].shape[0]
     outs = dict(
         layer=block, memory=block, tokens=block,
-        gate=wide(2 * shapes["gate"][1], shapes["gate"][0] // 2), up=wide(2 * shapes["up"][1], shapes["up"][0] // 2),
-        down=wide(4 * shapes["down_a"][1], shapes["down_a"][0] // 2),
-        out_two=wide(model, shapes["out_two"][0] // 2), out_one=wide(model, shapes["out_one"][0] // 2),
+        gate=wide(shapes["gate"][0] // 2, 2 * shapes["gate"][1]), up=wide(shapes["up"][0] // 2, 2 * shapes["up"][1]),
+        down=wide(shapes["down_a"][0] // 2, 4 * shapes["down_a"][1]),
+        out_two=wide(shapes["out_two"][0] // 2, model), out_one=wide(shapes["out_one"][0] // 2, model),
         wq_two=head, wk_two=head, wv_two=head, wq_one=head, wk_one=head, wv_one=head,
-        gains=wide(8, model), bias=wide(buckets, TILE),
+        gains=wide(8, model), bias=wide(8, TILE),
     )
     out_specs = {name: anywhere if s is block else fixed(s.shape) for name, s in outs.items()}
 
@@ -954,8 +937,8 @@
         q_send=room(2, depth, 2, share, GROUP), block=room(2, HALF, model), branch=room(model, BLOCK),
         acc_a=room(BLOCK, model, kind=F32), acc_b=room(BLOCK, model, kind=F32), dqkv=room(BLOCK, 3 * GROUP),
         dq=room(GROUP, BLOCK), do=room(GROUP, BLOCK), mask=room(BLOCK, BLOCK), gains=room(8, model, kind=F32),
-        gains_got=room(depth + 2, 8, model, kind=F32), bias=room(4, buckets, TILE, kind=F32),
-        bias_got=room(depth + 3, buckets, TILE, kind=F32),
+        gains_got=room(depth + 2, 8, model, kind=F32), bias=room(4, 8, TILE, kind=F32),
+        bias_got=room(depth + 3, 8, TILE, kind=F32),
         after=room(BLOCK, model, kind=F32), hidden=room(BLOCK, model, kind=F32),
         wo=room(model, model), ctx=room(model, BLOCK), n=room(model, BLOCK), mem=room(model, BLOCK),
     )
@@ -991,9 +974,342 @@
     return Named(jax.tree.unflatten(out_tree, results))
 
 
-def swap(array, axis, mask):
-    size = lax.axis_size(axis)
-    return lax.ppermute(array, axis, [(i, i ^ mask) for i in range(size)])
+PIECES = 3
+
+
+class Gather:
+    def __init__(self, place, copies, slots):
+        self.slots = slots
+        half = slots.shape[1] // 2
+        size = half // PIECES
+        self.core = copies.new(lambda: slots.at[0], lambda: slots.at[1], place.to_core)
+
+        def rows(side, j):
+            return pl.ds(pl.multiple_of(side * half + j * size, 32), size)
+
+        def make(source, target, side, device):
+            return [
+                copies.new(
+                    (lambda j: lambda: slots.at[source, rows(side, j)])(j),
+                    (lambda j: lambda: slots.at[target, rows(side, j)])(j), device,
+                )
+                for j in range(PIECES)
+            ]
+
+        self.over_y = make(0, 2, place.x, place.to_y)
+        self.over_x = make(2, 2, place.x, place.to_x)
+        self.near = make(2, 3, place.x, place.to_core)
+        self.far = make(2, 3, 1 - place.x, place.to_core)
+
+    def start(self):
+        for copy in self.over_y:
+            copy.start()
+        self.core.start()
+
+    def pass_y(self, j):
+        self.over_y[j].got()
+        self.over_x[j].start()
+        self.near[j].start()
+
+    def pass_x(self, j):
+        self.over_x[j].got()
+        self.far[j].start()
+
+    def ready(self):
+        for copy in self.near + self.far:
+            copy.got()
+
+    def sent(self):
+        for copy in [self.core] + self.over_y + self.over_x + self.near + self.far:
+            copy.sent()
+
+
+def forward_kernel(ins, outs, r):
+    place = Place(1)
+    step = pl.program_id(0)
+    core = place.core
+    copies = Copies(r.send, r.recv)
+    segs = Tiles(place, ins.segs)
+    gather_one = Gather(place, copies, r.wt_one)
+    gather_two = Gather(place, copies, r.wt_two)
+    tables = [
+        copies.new((lambda a: lambda: r.table.at[a])(a), (lambda b: lambda: r.table.at[b])(b), d)
+        for a, b, d in ((0, 1, place.to_core), (0, 2, place.to_y), (2, 3, place.to_core))
+    ]
+    swaps = {}
+    tok_swap = copies.new(lambda: ins.tokens.at[1 - core], lambda: r.tok_in.at[core], place.to_core)
+    mem_swap = copies.new(lambda: ins.memory.at[1 - core], lambda: r.mem_in.at[core], place.to_core)
+    cot_swap = copies.new(lambda: ins.cotangent.at[1 - core], lambda: r.cot_in.at[core], place.to_core)
+    assert copies.count == r.send.shape[0], copies.count
+    count = [0]
+
+    def load(source, target):
+        count[0] += 1
+        return pltpu.make_async_copy(source, target, r.load.at[count[0] - 1])
+
+    tok_own = load(ins.tokens.at[core], r.tok_in.at[core])
+    mem_own = load(ins.memory.at[core], r.mem_in.at[core])
+    cot_own = load(ins.cotangent.at[core], r.cot_in.at[core])
+
+    def load_group(key, value, query, slots):
+        return [
+            load(source.at[pl.ds(at, size)], slots.at[0, pl.ds(to, size)])
+            for source, at, to, size in (
+                (key, 0, 0, 128), (value, 0, 128, 128), (key, 128, 256, 64), (value, 128, 320, 64), (query, 0, 384, GROUP)
+            )
+        ]
+
+    raw_one = load_group(ins.self_key, ins.self_value, ins.self_query, r.wt_one)
+    raw_two = load_group(ins.cross_key, ins.cross_value, ins.cross_query, r.wt_two)
+    out_one, out_two = load(ins.self_out, r.wo_one), load(ins.cross_out, r.wo_two)
+    puts = Named({name: load(getattr(r, name), getattr(outs, name)) for name in vars(outs)})
+
+
+    def normed(hidden, gain, target):
+        for part in range(4):
+            rows = slice(part * TILE, (part + 1) * TILE)
+            h = hidden[rows, :]
+            scale = lax.rsqrt(jnp.mean(h * h, axis=-1, keepdims=True) + NORM_EPS)
+            target[:, rows] = jnp.transpose((h * scale * row_of(gain)).astype(BF16))
+
+    def project_out(context, weights, base, target):
+        for part in range(2):
+            rows = slice(part * HALF, (part + 1) * HALF)
+            target[rows, :] = base[rows, :] + dot(jnp.transpose(context[:, rows]), weights[...])
+
+    def cross_keys(slot):
+        r.kv_two[slot] = dot(r.wt_two[slot, KV, :], r.mem[...]).astype(BF16)
+
+    plan = {}
+
+    def at(point, *tasks):
+        plan.setdefault(point, []).extend(tasks)
+
+    one, two = gather_one, gather_two
+    at((0, 1), lambda: one.pass_y(0))
+    at((1, 0), lambda: one.pass_y(1))
+    at((1, 1), lambda: one.pass_x(0), tables[1].got, tables[2].start)
+    at((2, 1), lambda: two.pass_y(0))
+    at((2, 2), lambda: two.pass_y(1), lambda: two.pass_x(0))
+    at((3, 1), lambda: two.pass_y(2), lambda: two.pass_x(1))
+    at((4, 0), lambda: two.pass_x(2))
+
+    def tick(steps, index):
+        for k in steps:
+            if (k, index) in plan:
+
+                def run(tasks=plan[k, index]):
+                    for task in tasks:
+                        task()
+
+                pl.when(step == k)(run)
+
+    @pl.when(step == 0)
+    def _():
+        barrier = pltpu.get_barrier_semaphore()
+        for device in (place.to_core, place.to_y, place.to_x):
+            pl.semaphore_signal(barrier, inc=1, device_id=device, device_id_type=MESH)
+        for copy in raw_one + [tok_own] + raw_two + [mem_own, out_one, out_two, cot_own]:
+            copy.start()
+        r.table[0] = jnp.zeros_like(r.table[0])
+        r.table[0, :HEADS, : ins.table.shape[1]] = ins.table[...]
+        for copy in raw_one:
+            copy.wait()
+        pl.semaphore_wait(barrier, 3)
+        tok_swap.start()
+        gather_one.start()
+        tables[0].start()
+        tables[1].start()
+        mem_swap.start()
+        cot_swap.start()
+        tok_own.wait()
+        tok_swap.got()
+        for half in range(2):
+            r.tok[half * HALF : (half + 1) * HALF, :] = r.tok_in[half].astype(F32)
+        puts.tok.start()
+        normed(r.tok, ins.self_gain, r.n_one)
+        puts.n_one.start()
+        for copy in raw_two:
+            copy.wait()
+        gather_two.start()
+
+    @pl.when(step == 1)
+    def _():
+        gather_one.core.got()
+        tables[0].got()
+
+    @pl.when(step == 2)
+    def _():
+        mem_own.wait()
+        mem_swap.got()
+        for half in range(2):
+            r.mem[:, half * HALF : (half + 1) * HALF] = jnp.transpose(r.mem_in[half])
+        puts.mem.start()
+        cot_own.wait()
+        cot_swap.got()
+        for half in range(2):
+            r.cot[half * HALF : (half + 1) * HALF, :] = r.cot_in[half]
+        puts.cot.start()
+        one.pass_y(2)
+        one.pass_x(1)
+        gather_two.core.got()
+        cross_keys(0)
+        cross_keys(1)
+        one.pass_x(2)
+        one.ready()
+        puts.wt_one.start()
+        tables[2].got()
+        puts.table.start()
+
+    slot = step % 4
+    rows_at = pl.ds(pl.multiple_of(place.group(slot) * GROUP, 16), GROUP)
+
+    @pl.when(step < 4)
+    def _():
+        r.qkv_one[slot] = dot(r.wt_one[slot], r.n_one[...]).astype(BF16)
+        self_forward(
+            r.qkv_one.at[slot, KV], r.qkv_one.at[slot, QS], r.table[slot], ins.hot[...], segs,
+            r.ctx_one.at[rows_at], r.lse_one.at[slot], lambda h: tick(range(4), h),
+        )
+
+    @pl.when(step == 4)
+    def _():
+        puts.qkv_one.start()
+        puts.ctx_one.start()
+        puts.lse_one.start()
+        out_one.wait()
+        project_out(r.ctx_one, r.wo_one, r.tok, r.first)
+        puts.first.start()
+        normed(r.first, ins.cross_gain, r.n_two)
+        puts.n_two.start()
+        key_mask(segs, key_segments(place, ins.memsegs), r.mask)
+
+    @pl.when(step == 6)
+    def _():
+        two.ready()
+        puts.wt_two.start()
+
+    @pl.when(step >= 4)
+    def _():
+        @pl.when(step >= 6)
+        def _():
+            cross_keys(slot)
+
+        r.q_two[slot] = dot(r.wt_two[slot, QS, :], r.n_two[...]).astype(BF16)
+        cross_forward(
+            r.kv_two.at[slot], r.q_two.at[slot], r.mask, r.ctx_two.at[rows_at], r.lse_two.at[slot],
+            lambda h: tick(range(4, 8), h),
+        )
+
+    @pl.when(step == 7)
+    def _():
+        out_two.wait()
+        project_out(r.ctx_two, r.wo_two, r.first, r.second)
+        for put in (puts.second, puts.ctx_two, puts.q_two, puts.kv_two, puts.lse_two):
+            put.start()
+        gather_one.sent()
+        gather_two.sent()
+        for copy in tables + [tok_swap, mem_swap, cot_swap]:
+            copy.sent()
+        for name in vars(outs):
+            getattr(puts, name).wait()
+
+
+def forward_call(operands):
+    tokens = operands["tokens"]
+    model = tokens.shape[2]
+    anywhere = pl.BlockSpec(memory_space=pl.ANY)
+
+    def fixed(array):
+        return pl.BlockSpec(array.shape, lambda t: (0,) * array.ndim)
+
+    small = dict(self_gain=fixed, cross_gain=fixed, table=fixed, hot=fixed, memsegs=fixed)
+    small.update(segs=lambda a: pl.BlockSpec(memory_space=pltpu.SMEM))
+    in_specs = {name: small.get(name, lambda a: anywhere)(a) for name, a in operands.items()}
+
+    def room(*shape, kind=BF16):
+        return pltpu.VMEM(shape, kind)
+
+    kept = dict(
+        tok=room(BLOCK, model, kind=F32), mem=room(model, BLOCK), cot=room(BLOCK, model), n_one=room(model, BLOCK),
+        n_two=room(model, BLOCK), qkv_one=room(4, 3 * GROUP, BLOCK), kv_two=room(4, 2 * GROUP, BLOCK),
+        q_two=room(4, GROUP, BLOCK), ctx_one=room(model, BLOCK), ctx_two=room(model, BLOCK),
+        lse_one=room(4, 8, BLOCK, kind=F32), lse_two=room(4, 8, BLOCK, kind=F32),
+        first=room(BLOCK, model, kind=F32), second=room(BLOCK, model, kind=F32),
+        wt_one=room(4, 3 * GROUP, model), wt_two=room(4, 3 * GROUP, model), table=room(4, 8, TILE, kind=F32),
+    )
+    block = tokens.shape[1:]
+    copies = 2 * (1 + 4 * PIECES) + 3 + 3
+    scratch = dict(
+        kept, tok_in=room(2, *block), mem_in=room(2, *block), cot_in=room(2, *block),
+        wo_one=room(model, model), wo_two=room(model, model), mask=room(BLOCK, BLOCK, kind=F32),
+        send=pltpu.SemaphoreType.DMA((copies,)), recv=pltpu.SemaphoreType.DMA((copies,)),
+        load=pltpu.SemaphoreType.DMA((15 + len(kept),)),
+    )
+    outs = {name: jax.ShapeDtypeStruct(m.shape, m.dtype) for name, m in kept.items()}
+    arrays, in_tree = jax.tree.flatten(operands)
+    out_shapes, out_tree = jax.tree.flatten(outs)
+    rooms, room_tree = jax.tree.flatten(scratch)
+
+    def kernel(*refs):
+        a, b = len(arrays), len(arrays) + len(out_shapes)
+        forward_kernel(
+            Named(jax.tree.unflatten(in_tree, refs[:a])), Named(jax.tree.unflatten(out_tree, refs[a:b])),
+            Named(jax.tree.unflatten(room_tree, refs[b:])),
+        )
+
+    results = pl.pallas_call(
+        kernel,
+        grid=(8,),
+        in_specs=jax.tree.leaves(in_specs),
+        out_specs=[anywhere] * len(out_shapes),
+        out_shape=out_shapes,
+        scratch_shapes=rooms,
+        compiler_params=pltpu.CompilerParams(
+            collective_id=1, has_side_effects=True, vmem_limit_bytes=60_000_000, dimension_semantics=("arbitrary",)
+        ),
+        cost_estimate=pl.CostEstimate(flops=10_000_000_000, bytes_accessed=40_000_000, transcendentals=6_000_000),
+    )(*arrays)
+    return Named(jax.tree.unflatten(out_tree, results))
+
+
+def finish_call(results, devices, buckets):
+    plain = {name: a for name, a in results.items() if name not in ("gains", "bias")}
+    share = results["gains"].shape[1] // devices
+    outs = {name: jax.ShapeDtypeStruct(a.shape, a.dtype) for name, a in plain.items()}
+    anywhere = pl.BlockSpec(memory_space=pl.ANY)
+    count = len(plain)
+
+    def kernel(gains, bias, *refs):
+        sources, (bias_out, *gain_outs), targets = refs[:count], refs[count : count + 4], refs[count + 4 : 2 * count + 4]
+        rooms, semaphores = refs[2 * count + 4 : 3 * count + 4], refs[3 * count + 4]
+        takes = [pltpu.make_async_copy(s, r, semaphores.at[k]) for k, (s, r) in enumerate(zip(sources, rooms))]
+        puts = [pltpu.make_async_copy(r, t, semaphores.at[count + k]) for k, (r, t) in enumerate(zip(rooms, targets))]
+        for take in takes:
+            take.start()
+        bias_out[...] = bias[:HEADS, :buckets]
+        first = (lax.axis_index("batch") * lax.axis_size("head") + lax.axis_index("head")) * share
+        turned = pltpu.roll(gains[...], gains.shape[1] - first, 1)
+        for k, out in enumerate(gain_outs):
+            out[...] = jnp.reshape(turned[k : k + 1, :share], (share,))
+        for take, put in zip(takes, puts):
+            take.wait()
+            put.start()
+        for put in puts:
+            put.wait()
+
+    def fixed(shape):
+        return pl.BlockSpec(shape, lambda: (0,) * len(shape))
+
+    small = [jax.ShapeDtypeStruct((HEADS, buckets), F32)] + [jax.ShapeDtypeStruct((share,), F32)] * 3
+    bias, *rest = pl.pallas_call(
+        kernel,
+        in_specs=[fixed(results["gains"].shape), fixed(results["bias"].shape)] + [anywhere] * count,
+        out_specs=[fixed(a.shape) for a in small] + [anywhere] * count,
+        out_shape=small + list(outs.values()),
+        scratch_shapes=[pltpu.VMEM(a.shape, a.dtype) for a in plain.values()] + [pltpu.SemaphoreType.DMA((2 * count,))],
+    )(results["gains"], results["bias"], *plain.values())
+    return dict(zip(plain, rest[3:]), bias=bias, gain_0=rest[0], gain_1=rest[1], gain_2=rest[2])
 
 
 def norm(hidden, gain):
@@ -1024,67 +1340,27 @@
     return gelu, 0.5 * (1.0 + bend) + 0.5 * value * (1.0 - bend * bend) * slope
 
 
-def group_rows(query, key, value):
-    q, k, v = query.T, key.T, value.T
-    return jnp.concatenate((k[:128], v[:128], k[128:], v[128:], q), axis=0)
-
-
 def on_device(
     tokens, memory, cotangent, target_segments, memory_segments, self_gain, self_query, self_key,
     self_value, self_out, position_bias, cross_gain, cross_query, cross_key, cross_value, cross_out,
     ff_gain, ff_gate, ff_up, ff_down,
 ):
     heads_axis, batch_axis = lax.axis_size("head"), lax.axis_size("batch")
-    me, row = lax.axis_index("head"), lax.axis_index("batch")
-    core = me & 1
+    core = lax.axis_index("head") & 1
     rows, part, model = tokens.shape
     assert part * 2 == BLOCK and rows == 2 and heads_axis == 4
     assert position_bias.shape[1] == HEADS and self_query.shape[1] == GROUP
-    here = jnp.reshape(me, (1,)).astype(jnp.int32)
     one_hot = jnp.asarray(bucket_one_hot(position_bias.shape[0]))
 
-    def to_block(array):
-        mine = lax.dynamic_index_in_dim(array, core, 0, keepdims=False)
-        other = swap(lax.dynamic_index_in_dim(array, 1 - core, 0, keepdims=False), "head", 1)
-        return jnp.where(core == 0, jnp.concatenate((mine, other), 0), jnp.concatenate((other, mine), 0))
-
-    def block_segments(segments):
-        mine = lax.dynamic_index_in_dim(segments, core, 0, keepdims=False)
-        return lax.dynamic_slice_in_dim(mine, (me >> 1) * BLOCK, BLOCK, 0)
-
-    tile_segments = block_segments(target_segments)[::TILE]
-    key_segments = block_segments(memory_segments).reshape(1, BLOCK)
-
-    def gathered(array):
-        slots = [array, swap(array, "head", 1), swap(array, "head", 2)]
-        slots.append(swap(slots[2], "head", 1))
-        return jnp.stack(slots)
-
-    tok = to_block(tokens)
-    wt_one = gathered(group_rows(self_query, self_key, self_value))
-    table = gathered(position_bias)
-    mem = to_block(memory)
-    wt_two = gathered(group_rows(cross_query, cross_key, cross_value))
-    cot = to_block(cotangent)
-
-    wide = tok.astype(F32)
-    normed_one = jnp.transpose(norm(wide, self_gain))
-    qkv = dot(wt_one.reshape(-1, model), normed_one).astype(BF16).reshape(4, 3 * GROUP, BLOCK)
-    hot_spec = pl.BlockSpec(one_hot.shape, lambda s, seg, at: (0, 0))
-    context_one, lse_one = attention_forward(
-        self_forward_kernel, tile_segments, here, qkv, 0, qkv, 2, (table, one_hot),
-        [pl.BlockSpec((1,) + table.shape[1:], lambda s, seg, at: (s, 0, 0)), hot_spec], [],
+    fwd = forward_call(
+        dict(
+            tokens=tokens, memory=memory, cotangent=cotangent, segs=target_segments, memsegs=memory_segments, hot=one_hot,
+            self_gain=self_gain, cross_gain=cross_gain, table=position_bias.T,
+            self_query=self_query.T, self_key=self_key.T, self_value=self_value.T, self_out=self_out,
+            cross_query=cross_query.T, cross_key=cross_key.T, cross_value=cross_value.T, cross_out=cross_out,
+        )
     )
-    mem_rows = jnp.transpose(mem)
-    kv_two = jnp.einsum("sad,dt->sat", wt_two[:, :QUERY_START], mem_rows, preferred_element_type=F32).astype(BF16)
-    first_sum = wide + over_tokens(context_one, self_out)
-    normed_two = jnp.transpose(norm(first_sum, cross_gain))
-    q_two = jnp.einsum("sad,dt->sat", wt_two[:, QUERY_START:], normed_two, preferred_element_type=F32).astype(BF16)
-    context_two, lse_two = attention_forward(
-        cross_forward_kernel, tile_segments, here, kv_two, 0, q_two, 0, (key_segments,),
-        [pl.BlockSpec((1, BLOCK), lambda s, seg, at: (0, 0))], [pltpu.VMEM((BLOCK, BLOCK), F32)],
-    )
-    second_sum = first_sum + over_tokens(context_two, cross_out)
+    second_sum, cot = fwd.second, fwd.cot
     normed_three = norm(second_sum, ff_gain)
     gate_value = dot(normed_three, ff_gate)
     up_value = dot(normed_three, ff_up)
@@ -1118,25 +1394,24 @@
     done = backward_call(
         batch_axis,
         dict(
-            segs=tile_segments, memsegs=key_segments, hot=one_hot, self_gain=self_gain.reshape(1, -1),
-            cross_gain=cross_gain.reshape(1, -1), ff_gain_grad=ff_gain_grad.reshape(1, -1),
-            kv_two=kv_two, q_two=q_two, lse_two=lse_two, wt_two=wt_two,
-            qkv_one=qkv, lse_one=lse_one, wt_one=wt_one, table=table,
+            segs=target_segments, memsegs=memory_segments, hot=one_hot, self_gain=self_gain, cross_gain=cross_gain,
+            ff_gain_grad=ff_gain_grad,
+            kv_two=fwd.kv_two, q_two=fwd.q_two, lse_two=fwd.lse_two, wt_two=fwd.wt_two,
+            qkv_one=fwd.qkv_one, lse_one=fwd.lse_one, wt_one=fwd.wt_one, table=fwd.table,
             loaded=dict(
-                after=grad_second, wo_two=cross_out, ctx_two=context_two, n_two=normed_two, mem=mem_rows,
-                first=first_sum, wo_one=self_out, ctx_one=context_one, n_one=normed_one, tok=wide,
+                after=grad_second, wo_two=cross_out, ctx_two=fwd.ctx_two, n_two=fwd.n_two, mem=fwd.mem,
+                first=fwd.first, wo_one=self_out, ctx_one=fwd.ctx_one, n_one=fwd.n_one, tok=fwd.tok,
             ),
             sends=dict(gate=gate[0], up=up[0], down_a=down_a[0], down_b=down_b[0]),
             keeps=dict(gate=gate[1], up=up[1], down_a=down_a[1], down_b=down_b[1]),
             layer=layer.reshape(2, part, model),
         ),
     )
-    share = model // (heads_axis * batch_axis)
-    gain_sums = lax.dynamic_slice_in_dim(done.gains, (row * heads_axis + me) * share, share, 1)
+    done = Named(finish_call(vars(done), heads_axis * batch_axis, position_bias.shape[0]))
     return (
-        done.layer, done.tokens, done.memory, gain_sums[0], done.wq_one, done.wk_one, done.wv_one, done.out_one,
-        done.bias[:, :HEADS], gain_sums[1], done.wq_two, done.wk_two, done.wv_two, done.out_two, gain_sums[2],
-        done.gate, done.up, done.down,
+        done.layer, done.tokens, done.memory, done.gain_0, done.wq_one, done.wk_one, done.wv_one, done.out_one.T,
+        done.bias.T, done.gain_1, done.wq_two, done.wk_two, done.wv_two, done.out_two.T, done.gain_2,
+        done.gate.T, done.up.T, done.down.T,
     )
 
 

time: 267 us -> 228 us (0.85)
  Pallas kernels: 133 us -> 175 us
  local copies, waits for them, and re-layouts: 36.7 us -> 0.54 us
  waiting for transfers between devices: 19.7 us -> 0 us
  other arithmetic: 12.8 us -> 3.5 us
  matrix products: 52.8 us -> 45 us
  starting transfers between devices: 6.43 us -> 0 us
    pallas_call x2, Pallas kernels: 22.7 us -> 56.6 us  [the longest x1 52 us: forward_call(): pl.pallas_call(kernel, grid=(8,), in_specs=jax.tree.leaves(in_specs), out...]
    ppermute x12 -> x0, waiting for transfers between devices: 19.7 us -> none  [swap(): return lax.ppermute(array, axis, [(i, i ^ mask) for i in range(size)])]
    unnamed x89 -> x24, local copies, waits for them, and re-layouts: 20.2 us -> 0.54 us
    pallas_call x1, Pallas kernels: 110 us -> 118 us  [backward_call(): pl.pallas_call(kernel, grid=(8,), in_specs=jax.tree.leaves(in_specs), out...]
    ppermute x12 -> x0, starting transfers between devices: 6.43 us -> none  [swap(): return lax.ppermute(array, axis, [(i, i ^ mask) for i in range(size)])]
    dot_general x2 -> x0, matrix products: 5.75 us -> none  [the longest x1 3.73 us: on_device(): jnp.einsum('sad,dt->sat', wt_two[:, :QUERY_START], mem_rows, preferred_el...]
    another operation x3 -> x0, other arithmetic: 5.47 us -> none  [gathered(): return jnp.stack(slots)]
    squeeze x4 -> x0, local copies, waits for them, and re-layouts: 4.05 us -> none  [the longest x2 2.73 us: to_block(): mine = lax.dynamic_index_in_dim(array, core, 0, keepdims=False)]
  transfers between devices with their start and end apart: 12 -> 0, of which waited for: 3 -> 0; matrix products, arithmetic and copies ran while one was open for 16% -> 0% of each run, Pallas kernels for 9% -> 0%
where the time goes in v3:
time: 228 us; the launch traced here: 225 us
  Pallas kernels  175 us (77%)
  matrix products  45 us (20%)
  other arithmetic  3.5 us (2%)
    pallas_call x1, Pallas kernels, backward_call(): pl.pallas_call(kernel, grid=(8,), in_specs=jax.tree.leaves(in_specs), out...  118 us
    pallas_call x1, Pallas kernels, forward_call(): pl.pallas_call(kernel, grid=(8,), in_specs=jax.tree.leaves(in_specs), out...  52 us
    dot_general x8, matrix products, over_tokens(): lax.dot_general(left, right, (((0,), (0,)), ((), ())), preferred_element_...  23.8 us
    dot_general x3, matrix products, dot(): lax.dot_general(left, right, (((1,), (0,)), ((), ())), preferred_element_...  12.8 us
    dot_general x3, matrix products, by_transpose(): lax.dot_general(left, right, (((1,), (1,)), ((), ())), preferred_element_...  8.43 us
    pallas_call x1, Pallas kernels, finish_call(): pl.pallas_call(kernel, in_specs=[fixed(results['gains'].shape), fixed(res...  4.66 us

profile of v3, /device:TPU:0, one launch (start us, length us, event | category | flops | bytes accessed | tf_op | source)
XLA Modules:
  0.0 224.7 jit_solution(4507331791002053876)
XLA Ops:
  0.7 0.0 copy-start.2
  0.7 0.0 copy-start.3
  0.7 52.0 %shard_map.340 = (bf16[512,768]{1,0:T(8,128)(2,1)}, bf16[768,512]{1,0:T(8,128)(2,1)}, bf16[768,512]{1,0:T(8,128)(2,1)}, f32[512,768]{1,0:T(8,128)}, bf16[4,384,5...) custom-call(bf16[2,256,768]{2,1,0:T(8,128)(2,1)} %refs_0_.2, ...), custom_call_target="tpu_custom_call" | custom-call | flops 10000000000 | bytes 40000000 | tf_op jit(solution)/shard_map/pallas_call | solution.py:1261
  52.6 0.0 copy-start
  52.7 1.7 multiply_reduce_fusion.2
  54.4 0.0 copy-done.2
  54.4 0.1 copy-done
  54.5 0.2 multiply_convert_fusion.2
  54.7 0.0 copy-done.3
  54.7 0.0 copy-start.1
  54.7 0.0 copy-start.6
  54.8 1.8 fusion.28
  56.6 0.0 copy-done.1
  56.6 0.3 copy-done.6
  56.9 0.0 copy-start.4
  56.9 1.8 fusion.27
  58.7 0.1 copy-done.4
  58.8 6.4 %multiply_convert_fusion = (bf16[512,2048]{1,0:T(8,128)(2,1)}, bf16[512,2048]{1,0:T(8,128)(2,1)}, bf16[512,2048]{1,0:T(8,128)(2,1)}) fusion(f32[512,2048]{1,0:T(8,128)S(1)} %fusion.28, f32[512,2048]{1,0:T(8,128)S(1)} %fusion.27, bf16[512,768]{1,0:T(8,128)(2,1)S(1)} %multiply_convert_fusion.2, bf16[768,2048]{1,0:T(8,128)(2,1)S(1)} %copy-done.4), kind=kOutput, calls=%fused_computation.12 | convolution fusion | flops 1635778560 | bytes 18612224 | tf_op jit(solution)/shard_map/dot_general | solution.py:39
  65.2 0.0 copy-start.9
  65.2 4.3 %convolution_convert_fusion = bf16[2048,384]{1,0:T(8,128)(2,1)} fusion(bf16[512,2048]{1,0:T(8,128)(2,1)} %get-tuple-element.124, bf16[512,768]{1,0:T(8,128)(2,1)S(1)} %multiply_convert_fusion.2, s32[]{:T(128)S(6)} %select_n.25), kind=kOutput, calls=%fused_computation.15 | convolution fusion | flops 806092800 | bytes 4063236 | tf_op jit(solution)/shard_map/dot_general | solution.py:1328
  69.5 0.0 copy-done.9
  69.5 2.5 %convolution_convert_fusion.1 = bf16[2048,384]{1,0:T(8,128)(2,1)} fusion(bf16[512,2048]{1,0:T(8,128)(2,1)S(1)} %copy-done.9, bf16[512,768]{1,0:T(8,128)(2,1)S(1)} %multiply_convert_fusion.2, s32[]{:T(128)S(6)} %select_n.25), kind=kOutput, calls=%fused_computation.16 | convolution fusion | flops 806092800 | bytes 4063236 | tf_op jit(solution)/shard_map/dot_general | solution.py:1328
  71.9 2.5 %convolution_convert_fusion.4 = bf16[768,512]{1,0:T(8,128)(2,1)} fusion(bf16[512,768]{1,0:T(8,128)(2,1)S(1)} %copy-done.1, bf16[512,2048]{1,0:T(8,128)(2,1)} %get-tuple-element.122, s32[]{:T(128)S(6)} %select_n.24), kind=kOutput, calls=%fused_computation.26 | convolution fusion | flops 403046400 | bytes 2097156 | tf_op jit(solution)/shard_map/dot_general | solution.py:1328
  74.4 0.0 copy-start.10
  74.5 2.7 %convolution_convert_fusion.5 = bf16[768,512]{1,0:T(8,128)(2,1)} fusion(bf16[512,768]{1,0:T(8,128)(2,1)S(1)} %copy-done.1, bf16[512,2048]{1,0:T(8,128)(2,1)} %get-tuple-element.122, s32[]{:T(128)S(6)} %select_n.23), kind=kOutput, calls=%fused_computation.27 | convolution fusion | flops 403046400 | bytes 2097156 | tf_op jit(solution)/shard_map/dot_general | solution.py:1328
  77.1 0.0 copy-done.10
  77.1 0.0 copy-start.5
  77.1 0.0 copy-start.8
  77.1 4.0 %fusion.29 = f32[512,768]{1,0:T(8,128)S(1)} fusion(bf16[512,2048]{1,0:T(8,128)(2,1)S(1)} %copy-done.10, bf16[768,2048]{1,0:T(8,128)(2,1)} %param.38), kind=kOutput, calls=%fused_computation.51 | convolution fusion | flops 1610612736 | bytes 6815744 | tf_op jit(solution)/shard_map/dot_general | solution.py:1332
  81.1 0.0 copy-done.5
  81.1 0.0 copy-done.8
  81.1 2.7 %multiply_reduce_fusion = (f32[512]{0:T(512)S(1)}, f32[768]{0:T(1024)}, f32[512,768]{1,0:T(8,128)S(1)}) fusion(f32[512,768]{1,0:T(8,128)S(1)} %copy-done, f32[768]{0:T(1024)S(1)} %copy-done.2, f32[512]{0:T(512)S(1)} %add_rsqrt_fusion, f32[512,768]{1,0:T(8,128)S(1)} %fusion.29, bf16[512,2048]{1,0:T(8,128)(2,1)S(1)} %copy-done.8, ...), kind=kOutput, calls=%fused_computation.20 | convolution fusion | flops 1613363968 | bytes 9971712 | tf_op jit(solution)/shard_map/dot_general | solution.py:1332
  83.8 1.6 subtract_add_fusion.refs_9_
  85.4 0.0 copy-start.11
  85.4 4.2 %convolution_convert_fusion.2 = bf16[2048,384]{1,0:T(8,128)(2,1)} fusion(bf16[512,2048]{1,0:T(8,128)(2,1)} %get-tuple-element.124, bf16[512,768]{1,0:T(8,128)(2,1)S(1)} %multiply_convert_fusion.2, s32[]{:T(128)S(6)} %select_n.22), kind=kOutput, calls=%fused_computation.17 | convolution fusion | flops 806092800 | bytes 4063236 | tf_op jit(solution)/shard_map/dot_general | solution.py:1328
  89.5 0.0 copy-done.11
  89.5 2.5 %convolution_convert_fusion.3 = bf16[2048,384]{1,0:T(8,128)(2,1)} fusion(bf16[512,2048]{1,0:T(8,128)(2,1)S(1)} %copy-done.11, bf16[512,768]{1,0:T(8,128)(2,1)S(1)} %multiply_convert_fusion.2, s32[]{:T(128)S(6)} %select_n.22), kind=kOutput, calls=%fused_computation.18 | convolution fusion | flops 806092800 | bytes 4063236 | tf_op jit(solution)/shard_map/dot_general | solution.py:1328
  92.0 2.5 %convolution_convert_fusion.6 = bf16[768,512]{1,0:T(8,128)(2,1)} fusion(bf16[512,768]{1,0:T(8,128)(2,1)S(1)} %copy-done.1, bf16[512,2048]{1,0:T(8,128)(2,1)} %get-tuple-element.122, s32[]{:T(128)S(6)} %select_n.21), kind=kOutput, calls=%fused_computation.28 | convolution fusion | flops 403046400 | bytes 2097156 | tf_op jit(solution)/shard_map/dot_general | solution.py:1328
  94.6 0.0 copy-start.7
  94.6 2.7 %convolution_convert_fusion.7 = bf16[768,512]{1,0:T(8,128)(2,1)} fusion(bf16[512,768]{1,0:T(8,128)(2,1)S(1)} %copy-done.1, bf16[512,2048]{1,0:T(8,128)(2,1)} %get-tuple-element.122, s32[]{:T(128)S(6)} %select_n.20), kind=kOutput, calls=%fused_computation.29 | convolution fusion | flops 403046400 | bytes 2097156 | tf_op jit(solution)/shard_map/dot_general | solution.py:1328
  97.2 0.0 copy-done.7
  97.2 4.6 %add_convert_fusion = bf16[512,768]{1,0:T(8,128)(2,1)} fusion(f32[512,768]{1,0:T(8,128)S(1)} %copy-done, bf16[512,2048]{1,0:T(8,128)(2,1)S(1)} %copy-done.7, bf16[2048,768]{1,0:T(8,128)(2,1)} %param.40), kind=kOutput, calls=%fused_computation.21 | convolution fusion | flops 1611399168 | bytes 7602176 | tf_op jit(solution)/shard_map/dot_general | solution.py:39
  101.8 118.0 %shard_map.341 = (f32[8,128]{1,0:T(8,128)}, f32[24,2048]{1,0:T(8,128)}, f32[8,768]{1,0:T(8,128)}, f32[64,768]{1,0:T(8,128)}, bf16[2,256,768]{2,1,0:T(8,128)(2,1)...) custom-call(f32[768]{0:T(1024)} %refs_0_.3, ...), custom_call_target="tpu_custom_call" | custom-call | flops 20000000000 | bytes 40000000 | tf_op jit(solution)/shard_map/pallas_call | solution.py:962
  219.8 4.7 %shard_map.342 = (f32[3,32]{1,0:T(4,128)}, f32[24]{0:T(128)}, f32[24]{0:T(128)}, f32[24]{0:T(128)}, f32[24,2048]{1,0:T(8,128)}, /*index=5*/f32[64,768]{1,0:T(8,1...) custom-call(f32[8,768]{1,0:T(8,128)} %get-tuple-element.86.gains, ...), custom_call_target="tpu_custom_call" | custom-call | tf_op jit(solution)/shard_map/pallas_call | solution.py:1305
  (2 shorter events, 0.0 us)
Async XLA Ops:
  0.7 53.7 %copy-start.2 = (f32[768]{0:T(1024)S(1)}, f32[768]{0:T(1024)}, u32[]{:S(2)}) copy-start(f32[768]{0:T(1024)} %param.37) | copy-start | bytes 9220
  0.7 54.1 %copy-start.3 = (bf16[768,2048]{1,0:T(8,128)(2,1)S(1)}, bf16[768,2048]{1,0:T(8,128)(2,1)}, u32[]{:S(2)}) copy-start(bf16[768,2048]{1,0:T(8,128)(2,1)} %param.38) | copy-start | bytes 9437188
  52.6 1.9 copy-start
  54.7 1.8 copy-start.1
  54.7 2.1 copy-start.6
  56.9 1.9 copy-start.4
  65.2 4.3 %copy-start.9 = (bf16[512,2048]{1,0:T(8,128)(2,1)S(1)}, bf16[512,2048]{1,0:T(8,128)(2,1)}, u32[]{:S(2)}) copy-start(bf16[512,2048]{1,0:T(8,128)(2,1)} %get-tuple-element.123) | copy-start | bytes 6291460
  74.4 2.7 %copy-start.10 = (bf16[512,2048]{1,0:T(8,128)(2,1)S(1)}, bf16[512,2048]{1,0:T(8,128)(2,1)}, u32[]{:S(2)}) copy-start(bf16[512,2048]{1,0:T(8,128)(2,1)} %get-tuple-element.123) | copy-start | bytes 6291460
  77.1 4.0 %copy-start.5 = (bf16[768,2048]{1,0:T(8,128)(2,1)S(1)}, bf16[768,2048]{1,0:T(8,128)(2,1)}, u32[]{:S(2)}) copy-start(bf16[768,2048]{1,0:T(8,128)(2,1)} %param.39) | copy-start | bytes 9437188
  77.1 4.0 %copy-start.8 = (bf16[512,2048]{1,0:T(8,128)(2,1)S(1)}, bf16[512,2048]{1,0:T(8,128)(2,1)}, u32[]{:S(2)}) copy-start(bf16[512,2048]{1,0:T(8,128)(2,1)} %get-tuple-element.124) | copy-start | bytes 6291460
  85.4 4.2 %copy-start.11 = (bf16[512,2048]{1,0:T(8,128)(2,1)S(1)}, bf16[512,2048]{1,0:T(8,128)(2,1)}, u32[]{:S(2)}) copy-start(bf16[512,2048]{1,0:T(8,128)(2,1)} %get-tuple-element.123) | copy-start | bytes 6291460
  94.6 2.7 %copy-start.7 = (bf16[512,2048]{1,0:T(8,128)(2,1)S(1)}, bf16[512,2048]{1,0:T(8,128)(2,1)}, u32[]{:S(2)}) copy-start(bf16[512,2048]{1,0:T(8,128)(2,1)} %get-tuple-element.122) | copy-start | bytes 6291460

commit v4 on v3

--- a/solution.py
+++ b/solution.py
@@ -1086,13 +1086,16 @@
         plan.setdefault(point, []).extend(tasks)
 
     one, two = gather_one, gather_two
-    at((0, 1), lambda: one.pass_y(0))
-    at((1, 0), lambda: one.pass_y(1))
-    at((1, 1), lambda: one.pass_x(0), tables[1].got, tables[2].start)
-    at((2, 1), lambda: two.pass_y(0))
-    at((2, 2), lambda: two.pass_y(1), lambda: two.pass_x(0))
-    at((3, 1), lambda: two.pass_y(2), lambda: two.pass_x(1))
-    at((4, 0), lambda: two.pass_x(2))
+    at((0, 0), lambda: one.pass_y(1))
+    at((0, 2), lambda: one.pass_y(2))
+    at((1, 0), lambda: one.pass_x(0))
+    at((1, 1), tables[1].got, tables[2].start)
+    at((1, 2), lambda: one.pass_x(1))
+    at((2, 0), lambda: two.pass_y(1))
+    at((2, 2), lambda: two.pass_x(0))
+    at((3, 0), lambda: two.pass_y(2))
+    at((3, 2), lambda: two.pass_x(1))
+    at((4, 1), lambda: two.pass_x(2))
 
     def tick(steps, index):
         for k in steps:
@@ -1117,9 +1120,9 @@
             copy.wait()
         pl.semaphore_wait(barrier, 3)
         tok_swap.start()
-        gather_one.start()
         tables[0].start()
         tables[1].start()
+        gather_one.start()
         mem_swap.start()
         cot_swap.start()
         tok_own.wait()
@@ -1127,6 +1130,7 @@
         for half in range(2):
             r.tok[half * HALF : (half + 1) * HALF, :] = r.tok_in[half].astype(F32)
         puts.tok.start()
+        one.pass_y(0)
         normed(r.tok, ins.self_gain, r.n_one)
         puts.n_one.start()
         for copy in raw_two:
@@ -1150,11 +1154,10 @@
         for half in range(2):
             r.cot[half * HALF : (half + 1) * HALF, :] = r.cot_in[half]
         puts.cot.start()
-        one.pass_y(2)
-        one.pass_x(1)
         gather_two.core.got()
         cross_keys(0)
         cross_keys(1)
+        two.pass_y(0)
         one.pass_x(2)
         one.ready()
         puts.wt_one.start()
@@ -1312,32 +1315,141 @@
     return dict(zip(plain, rest[3:]), bias=bias, gain_0=rest[0], gain_1=rest[1], gain_2=rest[2])
 
 
-def norm(hidden, gain):
-    scale = lax.rsqrt(jnp.mean(hidden * hidden, axis=-1, keepdims=True) + NORM_EPS)
-    return (hidden * scale * gain).astype(BF16)
-
-
-def norm_back(hidden, gain, grad):
-    scale = lax.rsqrt(jnp.mean(hidden * hidden, axis=-1, keepdims=True) + NORM_EPS)
-    weighted = grad * gain
-    inner = jnp.mean(weighted * hidden, axis=-1, keepdims=True)
-    return weighted * scale - hidden * (scale * scale * scale * inner), jnp.sum(grad * hidden * scale, axis=0)
-
-
-def over_tokens(left, right):
-    return lax.dot_general(left, right, (((0,), (0,)), ((), ())), preferred_element_type=F32)
-
-
-def by_transpose(left, right):
+FF_STEPS = 4
+
+
+def ff_tile(t):
+    core = lax.axis_index("head") % 2
+    half = t // 2
+    other = 1 - core
+    return 2 * (half + other - 2 * half * other) + t % 2
+
+
+def over_rows(left, right):
     return lax.dot_general(left, right, (((1,), (1,)), ((), ())), preferred_element_type=F32)
 
 
-def gelu_parts(value):
-    inner = np.float32(np.sqrt(2.0 / np.pi)) * (value + 0.044715 * (value * value * value))
-    bend = jnp.tanh(inner)
-    slope = np.float32(np.sqrt(2.0 / np.pi)) * (1.0 + 3.0 * 0.044715 * (value * value))
-    gelu = 0.5 * value * (1.0 + bend)
-    return gelu, 0.5 * (1.0 + bend) + 0.5 * value * (1.0 - bend * bend) * slope
+def ff_kernel(ins, outs, r):
+    step = pl.program_id(0)
+    core = lax.axis_index("head") % 2
+    model = ins.second.shape[1]
+    root = np.float32(np.sqrt(2.0 / np.pi))
+
+    @pl.when(step == 0)
+    def _():
+        for part in range(4):
+            rows = slice(part * TILE, (part + 1) * TILE)
+            h = ins.second[rows, :]
+            scale = lax.rsqrt(jnp.mean(h * h, axis=-1, keepdims=True) + NORM_EPS)
+            r.normed[rows, :] = (h * scale * row_of(ins.gain)).astype(BF16)
+            r.cot[:, rows] = jnp.transpose(ins.cot[rows, :])
+            r.layer[rows, :] = h
+            r.back[rows, :] = jnp.zeros_like(h)
+
+    for part in range(4):
+        rows = slice(part * TILE, (part + 1) * TILE)
+        normed = r.normed[rows, :]
+        gate, up = dot(normed, ins.gate[...]), dot(normed, ins.up[...])
+        grad = over_rows(ins.cot[rows, :], ins.down[...])
+        square = gate * gate
+        half = 0.5 + 0.5 * jnp.tanh(gate * (root + (root * 0.044715) * square))
+        gelu = gate * half
+        slope = half + gelu * (2.0 - 2.0 * half) * (root + (3.0 * 0.044715 * root) * square)
+        activation = (gelu * up).astype(BF16)
+        grad_gate = (grad * up * slope).astype(BF16)
+        grad_up = (grad * gelu).astype(BF16)
+        r.act[rows, :] = activation
+        r.grad_gate[:, rows] = jnp.transpose(grad_gate)
+        r.grad_up[:, rows] = jnp.transpose(grad_up)
+        r.layer[rows, :] = r.layer[rows, :] + dot(activation, ins.down[...])
+        r.back[rows, :] = r.back[rows, :] + over_rows(grad_gate, ins.gate[...]) + over_rows(grad_up, ins.up[...])
+
+    lanes = model // 2
+
+    def spread_out(target, product, first):
+        rows = target.shape[3]
+        for piece in range(product.shape[0] // rows):
+            at = first + piece
+            target[at // 4, (at // 2) % 2, at % 2] = product[piece * rows : (piece + 1) * rows]
+
+    for which, name in ((1 - core, 0), (core, 1)):
+        right = r.normed[:, pl.ds(pl.multiple_of(which * lanes, 128), lanes)]
+        for grads, target in ((r.grad_gate, outs.gate[name]), (r.grad_up, outs.up[name])):
+            spread_out(target, dot(grads[...], right).astype(BF16), 0)
+    for t, target in enumerate((outs.down_a[0], outs.down_b[0], outs.down_a[1], outs.down_b[1])):
+
+        @pl.when(step == t)
+        def _(target=target):
+            per = model // 2
+            for part in range(2):
+                product = dot(r.cot[part * per : (part + 1) * per, :], r.act[...]).astype(BF16)
+                spread_out(target, product, part * (per // target.shape[3]))
+
+    @pl.when(step == FF_STEPS - 1)
+    def _():
+        total = jnp.zeros((1, model), F32)
+        for part in range(4):
+            rows = slice(part * TILE, (part + 1) * TILE)
+            h, e = ins.second[rows, :], r.back[rows, :]
+            scale = lax.rsqrt(jnp.mean(h * h, axis=-1, keepdims=True) + NORM_EPS)
+            weighted = e * row_of(ins.gain)
+            inner = jnp.mean(weighted * h, axis=-1, keepdims=True)
+            outs.after[rows, :] = ins.cot[rows, :].astype(F32) + weighted * scale - h * (scale * scale * scale * inner)
+            total = total + jnp.sum(e * h * scale, axis=0, keepdims=True)
+            outs.layer[part // 2, (part % 2) * TILE : (part % 2 + 1) * TILE, :] = r.layer[rows, :].astype(BF16)
+        outs.gain_grad[...] = jnp.reshape(total, (model,))
+
+
+def ff_call(depth, operands):
+    model, columns = operands["gate"].shape
+    tile = columns // FF_STEPS
+
+    def fixed(shape):
+        return pl.BlockSpec(shape, lambda t: (0,) * len(shape))
+
+    in_specs = {name: fixed(a.shape) for name, a in operands.items()}
+    in_specs.update(
+        gate=pl.BlockSpec((model, tile), lambda t: (0, ff_tile(t))),
+        up=pl.BlockSpec((model, tile), lambda t: (0, ff_tile(t))),
+        down=pl.BlockSpec((tile, model), lambda t: (ff_tile(t), 0)),
+    )
+    wide = jax.ShapeDtypeStruct((depth, 2, 2, columns // (4 * depth), model // 2), BF16)
+    deep = jax.ShapeDtypeStruct((depth, 2, 2, model // (4 * depth), tile), BF16)
+    by_tile = pl.BlockSpec((depth // FF_STEPS,) + wide.shape[1:], lambda t: (ff_tile(t), 0, 0, 0, 0))
+    outs = dict(
+        layer=jax.ShapeDtypeStruct((2, HALF, model), BF16), after=jax.ShapeDtypeStruct((BLOCK, model), F32),
+        gain_grad=jax.ShapeDtypeStruct((model,), F32), gate=[wide, wide], up=[wide, wide],
+        down_a=[deep, deep], down_b=[deep, deep],
+    )
+    out_specs = jax.tree.map(lambda a: by_tile if a is wide else fixed(a.shape), outs)
+    scratch = dict(
+        normed=pltpu.VMEM((BLOCK, model), BF16), cot=pltpu.VMEM((model, BLOCK), BF16),
+        layer=pltpu.VMEM((BLOCK, model), F32), back=pltpu.VMEM((BLOCK, model), F32),
+        act=pltpu.VMEM((BLOCK, tile), BF16), grad_gate=pltpu.VMEM((tile, BLOCK), BF16),
+        grad_up=pltpu.VMEM((tile, BLOCK), BF16),
+    )
+    arrays, in_tree = jax.tree.flatten(operands)
+    out_shapes, out_tree = jax.tree.flatten(outs)
+    rooms, room_tree = jax.tree.flatten(scratch)
+
+    def kernel(*refs):
+        a, b = len(arrays), len(arrays) + len(out_shapes)
+        ff_kernel(
+            Named(jax.tree.unflatten(in_tree, refs[:a])), Named(jax.tree.unflatten(out_tree, refs[a:b])),
+            Named(jax.tree.unflatten(room_tree, refs[b:])),
+        )
+
+    results = pl.pallas_call(
+        kernel,
+        grid=(FF_STEPS,),
+        in_specs=jax.tree.leaves(in_specs),
+        out_specs=jax.tree.leaves(out_specs),
+        out_shape=out_shapes,
+        scratch_shapes=rooms,
+        compiler_params=pltpu.CompilerParams(vmem_limit_bytes=60_000_000, dimension_semantics=("arbitrary",)),
+        cost_estimate=pl.CostEstimate(flops=14_500_000_000, bytes_accessed=24_000_000, transcendentals=1_000_000),
+    )(*arrays)
+    return Named(jax.tree.unflatten(out_tree, results))
 
 
 def on_device(
@@ -1346,7 +1458,6 @@
     ff_gain, ff_gate, ff_up, ff_down,
 ):
     heads_axis, batch_axis = lax.axis_size("head"), lax.axis_size("batch")
-    core = lax.axis_index("head") & 1
     rows, part, model = tokens.shape
     assert part * 2 == BLOCK and rows == 2 and heads_axis == 4
     assert position_bias.shape[1] == HEADS and self_query.shape[1] == GROUP
@@ -1360,51 +1471,24 @@
             cross_query=cross_query.T, cross_key=cross_key.T, cross_value=cross_value.T, cross_out=cross_out,
         )
     )
-    second_sum, cot = fwd.second, fwd.cot
-    normed_three = norm(second_sum, ff_gain)
-    gate_value = dot(normed_three, ff_gate)
-    up_value = dot(normed_three, ff_up)
-    gelu, slope = gelu_parts(gate_value)
-    activation = (gelu * up_value).astype(BF16)
-    layer = (second_sum + dot(activation, ff_down)).astype(BF16)
-
-    grad_act = by_transpose(cot, ff_down)
-    grad_gate = (grad_act * up_value * slope).astype(BF16)
-    grad_up = (grad_act * gelu).astype(BF16)
-    grad_three = by_transpose(grad_gate, ff_gate) + by_transpose(grad_up, ff_up)
-    back, ff_gain_grad = norm_back(second_sum, ff_gain, grad_three)
-    grad_second = cot.astype(F32) + back
-
-    def halves(left, right, pieces):
-        lanes = left.shape[1] // (2 * pieces)
-        chunks = batch_axis // 2, 2, 2, right.shape[1] // (2 * batch_axis), lanes
-        found = []
-        for piece in range(pieces):
-            found.append([
-                over_tokens(
-                    right, lax.dynamic_slice_in_dim(left, (which * pieces + piece) * lanes, lanes, 1)
-                ).astype(BF16).reshape(chunks)
-                for which in (1 - core, core)
-            ])
-        return found
-
-    (gate,) = halves(normed_three, grad_gate, 1)
-    (up,) = halves(normed_three, grad_up, 1)
-    down_a, down_b = halves(activation, cot, 2)
+    ff = ff_call(
+        batch_axis // 2,
+        dict(second=fwd.second, cot=fwd.cot, gain=ff_gain, gate=ff_gate, up=ff_up, down=ff_down),
+    )
     done = backward_call(
         batch_axis,
         dict(
             segs=target_segments, memsegs=memory_segments, hot=one_hot, self_gain=self_gain, cross_gain=cross_gain,
-            ff_gain_grad=ff_gain_grad,
+            ff_gain_grad=ff.gain_grad,
             kv_two=fwd.kv_two, q_two=fwd.q_two, lse_two=fwd.lse_two, wt_two=fwd.wt_two,
             qkv_one=fwd.qkv_one, lse_one=fwd.lse_one, wt_one=fwd.wt_one, table=fwd.table,
             loaded=dict(
-                after=grad_second, wo_two=cross_out, ctx_two=fwd.ctx_two, n_two=fwd.n_two, mem=fwd.mem,
+                after=ff.after, wo_two=cross_out, ctx_two=fwd.ctx_two, n_two=fwd.n_two, mem=fwd.mem,
                 first=fwd.first, wo_one=self_out, ctx_one=fwd.ctx_one, n_one=fwd.n_one, tok=fwd.tok,
             ),
-            sends=dict(gate=gate[0], up=up[0], down_a=down_a[0], down_b=down_b[0]),
-            keeps=dict(gate=gate[1], up=up[1], down_a=down_a[1], down_b=down_b[1]),
-            layer=layer.reshape(2, part, model),
+            sends=dict(gate=ff.gate[0], up=ff.up[0], down_a=ff.down_a[0], down_b=ff.down_b[0]),
+            keeps=dict(gate=ff.gate[1], up=ff.up[1], down_a=ff.down_a[1], down_b=ff.down_b[1]),
+            layer=ff.layer,
         ),
     )
     done = Named(finish_call(vars(done), heads_axis * batch_axis, position_bias.shape[0]))

time: 228 us -> 193 us (0.85); the launches traced: 225 us -> 192 us
  matrix products: 45 us -> 0 us
  Pallas kernels: 175 us -> 191 us
  other arithmetic: 3.5 us -> 0 us
    dot_general x14 -> x0, matrix products: 45 us -> none  [the longest x8 23.8 us: over_tokens(): lax.dot_general(left, right, (((0,), (0,)), ((), ())), preferred_element_...]
    pallas_call x0 -> x1, Pallas kernels: none -> 32.4 us  [ff_call(): pl.pallas_call(kernel, grid=(FF_STEPS,), in_specs=jax.tree.leaves(in_spec...]
    pallas_call x1, Pallas kernels: 118 us -> 108 us  [backward_call(): pl.pallas_call(kernel, grid=(8,), in_specs=jax.tree.leaves(in_specs), out...]
    pallas_call x1, Pallas kernels: 52 us -> 46.7 us  [forward_call(): pl.pallas_call(kernel, grid=(8,), in_specs=jax.tree.leaves(in_specs), out...]
where the time goes in v4:
time: 193 us; the launch traced here: 192 us
  Pallas kernels  191 us (99%)
    pallas_call x1, Pallas kernels, backward_call(): pl.pallas_call(kernel, grid=(8,), in_specs=jax.tree.leaves(in_specs), out...  108 us
    pallas_call x1, Pallas kernels, forward_call(): pl.pallas_call(kernel, grid=(8,), in_specs=jax.tree.leaves(in_specs), out...  46.7 us
    pallas_call x1, Pallas kernels, ff_call(): pl.pallas_call(kernel, grid=(FF_STEPS,), in_specs=jax.tree.leaves(in_spec...  32.4 us
    pallas_call x1, Pallas kernels, finish_call(): pl.pallas_call(kernel, in_specs=[fixed(results['gains'].shape), fixed(res...  4.66 us

profile of v4, /device:TPU:0, one launch (start us, length us, event | category | flops | bytes accessed | tf_op | source)
XLA Modules:
  0.0 192.3 jit_solution(2554698959429116839)
XLA Ops:
  0.7 46.7 %shard_map.340 = (bf16[512,768]{1,0:T(8,128)(2,1)}, bf16[768,512]{1,0:T(8,128)(2,1)}, bf16[768,512]{1,0:T(8,128)(2,1)}, f32[512,768]{1,0:T(8,128)}, bf16[4,384,5...) custom-call(bf16[2,256,768]{2,1,0:T(8,128)(2,1)} %refs_0_.2, ...), custom_call_target="tpu_custom_call" | custom-call | flops 10000000000 | bytes 40000000 | tf_op jit(solution)/shard_map/pallas_call | solution.py:1264
  47.3 32.4 %shard_map.341 = (f32[512,768]{1,0:T(8,128)}, bf16[4,2,2,48,512]{4,3,2,1,0:T(8,128)(2,1)}, bf16[4,2,2,48,512]{4,3,2,1,0:T(8,128)(2,1)}, bf16[4,2,2,48,512]{4,3,2...) custom-call(bf16[512,768]{1,0:T(8,128)(2,1)} %get-tuple-element.80.r, ...), custom_call_target="tpu_custom_call" | custom-call | flops 14499999744 | bytes 24000000 | tf_op jit(solution)/shard_map/pallas_call | solution.py:1442
  79.7 107.7 %shard_map.342 = (f32[8,128]{1,0:T(8,128)}, f32[24,2048]{1,0:T(8,128)}, f32[8,768]{1,0:T(8,128)}, f32[64,768]{1,0:T(8,128)}, bf16[2,256,768]{2,1,0:T(8,128)(2,1)...) custom-call(f32[768]{0:T(1024)} %refs_0_.3, ...), custom_call_target="tpu_custom_call" | custom-call | flops 20000000000 | bytes 40000000 | tf_op jit(solution)/shard_map/pallas_call | solution.py:962
  187.4 4.7 %shard_map.343 = (f32[3,32]{1,0:T(4,128)}, f32[24]{0:T(128)}, f32[24]{0:T(128)}, f32[24]{0:T(128)}, f32[24,2048]{1,0:T(8,128)}, /*index=5*/f32[64,768]{1,0:T(8,1...) custom-call(f32[8,768]{1,0:T(8,128)} %get-tuple-element.108.gains, ...), custom_call_target="tpu_custom_call" | custom-call | tf_op jit(solution)/shard_map/pallas_call | solution.py:1308

commit v5 on v4

--- a/solution.py
+++ b/solution.py
@@ -294,6 +294,9 @@
         self.to_y = (b, h + 2 - 4 * self.y)
         self.to_x = (b + 1 - 2 * self.x, h)
         self.to_z = [(lax.rem(self.z + k, depth) * 2 + self.x, h) for k in range(1, depth)]
+        self.z0, self.zh, self.far = self.z % 2, self.z // 2, depth // 2
+        self.to_z0 = ((self.z + 1 - 2 * self.z0) * 2 + self.x, h)
+        self.to_zh = [((lax.rem(self.zh + k, self.far) * 2 + self.z0) * 2 + self.x, h) for k in range(1, self.far)]
 
     def group(self, slot):
         low, high = slot % 2, slot // 2
@@ -303,7 +306,7 @@
         return [self.to_core, self.to_y, self.to_x] + self.to_z
 
 
-Z, X, Y = range(3)
+ZH, Z0, X, Y = range(4)
 
 
 class Sum:
@@ -313,29 +316,33 @@
         self.stages = []
         for at, axis in enumerate(order):
             room = got[at]
-            if axis == Z:
+            if axis == ZH:
                 stage = [
-                    copies.new(self.source(at, k), (lambda room, k: lambda: room.at[k - 1])(room, k), place.to_z[k - 1])
-                    for k in range(1, place.depth)
+                    copies.new(self.source(at, k), (lambda room, k: lambda: room.at[k - 1])(room, k), place.to_zh[k - 1])
+                    for k in range(1, place.far)
                 ]
             else:
-                device = place.to_x if axis == X else place.to_y
+                device = (None, place.to_z0, place.to_x, place.to_y)[axis]
                 stage = [copies.new(self.source(at, 1), (lambda room: lambda: room)(room), device)]
             self.stages.append(stage)
 
     @staticmethod
-    def rooms(depth, dims, order, rows, lanes):
-        sizes = {Z: depth, X: 2, Y: 2}
+    def rooms(far, dims, order, rows, lanes):
+        sizes = (far, 2, 2, 2)
         free = list(range(dims))
         shapes = []
         for axis in order:
             free.remove(axis)
-            lead = (depth - 1,) if axis == Z else ()
+            lead = (far - 1,) if axis == ZH else ()
             shapes.append(lead + tuple(sizes[d] for d in free) + (rows, lanes))
         return shapes
 
+    @staticmethod
+    def count(far, order):
+        return sum(far - 1 if axis == ZH else 1 for axis in order)
+
     def mine(self, axis):
-        return (self.place.z, self.place.x, self.place.y)[axis]
+        return (self.place.zh, self.place.z0, self.place.x, self.place.y)[axis]
 
     def source(self, at, k):
         def view():
@@ -343,7 +350,7 @@
             for axis in self.order[:at]:
                 index[axis] = self.mine(axis)
             axis = self.order[at]
-            index[axis] = lax.rem(self.place.z + k, self.place.depth) if axis == Z else 1 - self.mine(axis)
+            index[axis] = lax.rem(self.place.zh + k, self.place.far) if axis == ZH else 1 - self.mine(axis)
             return self.total.at[tuple(index)]
 
         return view
@@ -360,7 +367,7 @@
             index[done] = self.mine(done)
         for d, i in zip(later, free):
             index[d] = i
-        got = [self.got[at].at[k] for k in range(self.place.depth - 1)] if axis == Z else [self.got[at]]
+        got = [self.got[at].at[k] for k in range(self.place.far - 1)] if axis == ZH else [self.got[at]]
         return tuple(index), [g[tuple(free)] if free else g[...] for g in got]
 
     def add(self, at):
@@ -381,9 +388,9 @@
         def over(dims, free):
             if not dims:
                 one(free)
-            elif dims[0] == Z:
-
-                @pl.loop(0, self.place.depth)
+            elif dims[0] == ZH:
+
+                @pl.loop(0, self.place.far)
                 def _(z):
                     over(dims[1:], free + [z])
 
@@ -410,8 +417,10 @@
                 copy.sent()
 
 
-def add_loop(depth, target, other, inner):
-    @pl.loop(0, depth)
+def add_loop(target, other):
+    inner = target.shape[1:-2]
+
+    @pl.loop(0, target.shape[0])
     def _(z):
         for index in np.ndindex(*inner):
             target[(z, *index)] = target[(z, *index)] + other[(z, *index)]
@@ -428,7 +437,7 @@
         self.pair.got()
         if keep is not None:
             keep.wait()
-        add_loop(self.place.depth, self.room.total, self.from_pair, (2, 2))
+        add_loop(self.room.total, self.from_pair)
         self.sum.start(0)
 
     def last(self):
@@ -464,7 +473,7 @@
 
     def enter(self, j):
         self.pair[j].got()
-        add_loop(self.place.depth, self.room.total.at[j], self.room.pair.at[j], (2,))
+        add_loop(self.room.total.at[j], self.room.pair.at[j])
         if j == 1:
             if self.y_first:
                 self.across.start()
@@ -475,7 +484,7 @@
 
     def take(self):
         self.across.got()
-        add_loop(self.place.depth, self.room.total.at[0], self.room.across, (2,))
+        add_loop(self.room.total.at[0], self.room.across)
         self.own.start(0)
 
     def give(self):
@@ -497,11 +506,32 @@
 
 
 SHARED_ORDER = dict(
-    gate=(Z, X, Y), up=(Y, X, Z), down_a=(X, Y, Z), down_b=(X, Y, Z), out_two=(X, Y, Z), out_one=(X, Y, Z)
+    gate=(Y, X, Z0, ZH), up=(Z0, Y, X, ZH), down_a=(X, Z0, Y, ZH), down_b=(Y, X, Z0, ZH),
+    out_two=(Z0, X, Y, ZH), out_one=(Y, Z0, X, ZH),
 )
-SLOT_ORDER = dict(kv_two=(True, (X, Z)), q_two=(False, (X, Z)), kv_one=(True, (X, Z)), q_one=(True, (X, Z)))
+SLOT_ORDER = dict(
+    kv_two=(False, (X, Z0, ZH)), q_two=(True, (X, Z0, ZH)), kv_one=(False, (X, Z0, ZH)), q_one=(True, (X, Z0, ZH))
+)
 KV = slice(0, 2 * GROUP)
 QS = slice(2 * GROUP, 3 * GROUP)
+
+
+def packed(share):
+    return share % 32 == 0
+
+
+def query_shape(share):
+    return (share + share // 2, 128) if packed(share) else (share, GROUP)
+
+
+def put_query(ref, total):
+    share = ref.shape[0]
+    if not packed(share):
+        ref[...] = total
+        return
+    ref[:, :128] = total[:share]
+    ref[: share // 2, 128:] = total[share:, :64]
+    ref[share // 2 :, 128:] = total[share:, 64:]
 
 
 def put_heads(ref, kv):
@@ -526,10 +556,8 @@
         for name, order in SHARED_ORDER.items()
     })
     slots = Named({
-        name: Slots(place, copies, getattr(r, name), r.kv_send if order_at < 1 else r.q_send, y_first, order)
-        for name, (y_first, order), order_at in (
-            (n, o, int(getattr(r, n).total.shape[-1] == GROUP)) for n, o in SLOT_ORDER.items()
-        )
+        name: Slots(place, copies, getattr(r, name), r.kv_send if name.startswith("kv") else r.q_send, *way)
+        for name, way in SLOT_ORDER.items()
     })
     layer_swap = copies.new(lambda: r.block.at[1 - core], lambda: outs.layer.at[core], place.to_core)
     memory_swap = copies.new(lambda: r.block.at[1 - core], lambda: outs.memory.at[core], place.to_core)
@@ -571,21 +599,29 @@
             per = branch.shape[0] // 2
             for part in range(2):
                 product = dot(branch[part * per : (part + 1) * per, :], side).astype(BF16)
-                rows = target.shape[3]
+                rows = target.shape[4]
                 for piece in range(per // rows):
                     at = part * (per // rows) + piece
-                    target[at // 4, (at // 2) % 2, at % 2] = product[piece * rows : (piece + 1) * rows]
+                    to = (at // 8, (at // 4) % 2, (at // 2) % 2, at % 2)
+                    target[to] = product[piece * rows : (piece + 1) * rows]
             if which is not core:
                 unit.pair.start()
 
     def weight_products(target, left, lanes):
-        rows = target.shape[2]
+        rows = left.shape[0] // (2 * depth)
         per = left.shape[0] // 2
         for part in range(2):
             product = dot(left[part * per : (part + 1) * per, :], r.dqkv[:, lanes]).astype(BF16)
             for piece in range(per // rows):
                 at = part * (per // rows) + piece
-                target[at // 2, at % 2] = product[piece * rows : (piece + 1) * rows]
+                to = (at // 4, (at // 2) % 2, at % 2)
+                share = product[piece * rows : (piece + 1) * rows]
+                if target.shape[-1] == share.shape[1]:
+                    target[to] = share
+                else:
+                    target[(*to, slice(0, rows))] = share[:, :128]
+                    rest = share[:, 128:]
+                    target[(*to, slice(rows, rows + rows // 2))] = jnp.concatenate((rest[: rows // 2], rest[rows // 2 :]), axis=1)
 
     def add_rows(target, lanes, weights, fresh):
         for part in range(2):
@@ -624,25 +660,32 @@
         plan.setdefault(point, []).extend(tasks)
 
     sh, sl = shared, slots
-    at((0, 0), lambda: sh.up.enter(keeps.up), sh.out_two.enter)
+    at((0, 0), sh.out_two.enter, lambda: sh.up.enter(keeps.up))
     at((0, 1), lambda: sh.down_a.enter(keeps.down_a))
     at((0, 2), lambda: sh.down_b.enter(keeps.down_b))
     at((0, 3), sl.kv_two.pair[1].start, sl.q_two.pair[1].start)
-    at((1, 0), lambda: sh.out_two.sum.add(0))
+    at((1, 1), lambda: sh.out_two.sum.add(0))
     at((1, 3), lambda: sl.kv_two.enter(1), lambda: sl.q_two.enter(1))
-    at((2, 3), sl.kv_two.pair[0].start, sl.q_two.pair[0].start)
-    at((3, 0), lambda: sh.up.sum.add(0), lambda: sh.down_a.sum.add(0))
+    at((2, 0), lambda: sh.down_a.sum.add(0))
+    at((2, 2), lambda: sh.out_two.sum.add(1))
+    at((2, 3), sl.kv_two.pair[0].start, sl.q_two.pair[0].start, lambda: sh.gate.sum.add(0))
+    at((3, 2), lambda: sl.kv_two.far.add(0))
     at((3, 3), lambda: sl.kv_two.enter(0), lambda: sl.q_two.enter(0))
-    at((4, 0), lambda: sh.down_b.sum.add(0), sh.out_one.enter, lambda: sl.q_two.far.add(0))
-    at((4, 2), sl.kv_two.take)
-    at((4, 3), sl.kv_one.pair[1].start, sl.q_one.pair[1].start, lambda: sh.gate.sum.add(0), lambda: sl.q_two.own.add(0))
-    at((5, 0), lambda: sh.out_two.sum.add(1))
-    at((5, 2), lambda: sh.down_a.sum.add(1))
-    at((5, 3), lambda: sl.kv_one.enter(1), lambda: sl.q_one.enter(1), sl.q_two.give)
+    at((3, 4), lambda: sh.up.sum.add(0), lambda: sh.down_b.sum.add(0))
+    at((4, 0), lambda: sh.down_a.sum.add(1), sh.out_one.enter, lambda: sh.gate.sum.add(1))
+    at((4, 1), sl.q_two.take)
+    at((4, 2), lambda: sl.kv_two.far.add(1), lambda: sh.out_two.sum.add(2))
+    at((4, 3), sl.kv_one.pair[1].start, sl.q_one.pair[1].start)
+    at((5, 0), lambda: sl.kv_two.own.add(0))
+    at((5, 1), lambda: sh.gate.sum.add(2))
+    at((5, 2), sl.kv_two.give)
+    at((5, 3), lambda: sl.kv_one.enter(1), lambda: sl.q_one.enter(1))
     at((6, 0), lambda: sh.up.sum.add(1), lambda: sh.down_b.sum.add(1))
-    at((6, 2), lambda: sh.out_one.sum.add(0))
+    at((6, 1), lambda: sl.kv_two.own.add(1), lambda: sl.q_two.own.add(0))
     at((6, 3), sl.kv_one.pair[0].start, sl.q_one.pair[0].start)
-    at((7, 2), lambda: sl.kv_two.own.add(0))
+    at((7, 0), lambda: sh.out_one.sum.add(0), lambda: sh.down_b.sum.add(2))
+    at((7, 1), lambda: sh.down_a.sum.add(2), lambda: sl.kv_one.far.add(0))
+    at((7, 2), lambda: sl.q_two.own.add(1))
 
     def tick(steps, index):
         for k in steps:
@@ -737,6 +780,8 @@
             copy.wait()
         sh.out_two.pair.sent()
         out_products(sh.out_one, r.ctx, r.branch)
+        for task in plan[3, 4]:
+            task()
 
     @pl.when(step >= 4)
     def _():
@@ -801,10 +846,8 @@
         gain_copies[0].start()
         bias_copies[0].start()
         bias_copies[1].start()
-        sl.kv_one.take()
-        sh.gate.sum.add(1)
-        sh.up.last()
-        sh.down_a.last()
+        sh.out_one.sum.add(1)
+        sh.up.sum.add(2)
         gain_copies[0].done()
         gains[...] = gains[...] + r.gains_got[0]
         bias_copies[0].done()
@@ -813,19 +856,23 @@
         bias[2] = bias[2] + r.bias_got[1]
         gain_copies[1].start()
         bias_copies[2].start()
+        sl.q_one.take()
+        sl.kv_one.far.add(1)
+        sl.kv_one.own.add(0)
+        sh.gate.last()
+        sh.out_two.last()
         sh.down_b.last()
-        sl.q_one.take()
-        sl.kv_one.own.add(0)
+        sh.out_one.sum.add(2)
         gain_copies[1].done()
         gains[...] = gains[...] + r.gains_got[1]
         bias_copies[2].done()
         bias[0] = bias[0] + r.bias_got[2]
         gain_copies[2].start()
         bias_copies[3].start()
-        sh.out_one.sum.add(1)
         sl.q_one.own.add(0)
-        sh.gate.last()
-        sh.out_two.last()
+        sl.kv_one.give()
+        sl.kv_one.own.add(1)
+        sh.down_a.last()
         gain_copies[2].done()
         gains[...] = gains[...] + r.gains_got[2]
         bias_copies[3].done()
@@ -833,8 +880,11 @@
         for k in range(depth - 1):
             gain_copies[3 + k].start()
             bias_copies[4 + k].start()
-        outs.wq_two[...] = sl.q_two.finish()
+        sl.q_one.own.add(1)
         put_heads((outs.wk_two, outs.wv_two), sl.kv_two.finish())
+        put_query(outs.wq_two, sl.q_two.finish())
+        sh.up.last()
+        sh.out_one.last()
         put_heads((outs.wk_one, outs.wv_one), sl.kv_one.finish())
         gain_total, bias_total = gains[...], bias[0]
         for k in range(depth - 1):
@@ -849,8 +899,7 @@
         sh.down_b.store(outs.down, outs.down.shape[1] // 4, outs.down.shape[1] // 2)
         sh.gate.store(outs.gate, 0, outs.gate.shape[1] // 2)
         sh.out_two.store(outs.out_two, 0, outs.out_two.shape[1] // 2)
-        sh.out_one.last()
-        outs.wq_one[...] = sl.q_one.finish()
+        put_query(outs.wq_one, sl.q_one.finish())
         sh.out_one.store(outs.out_one, 0, outs.out_one.shape[1] // 2)
         for name in SHARED_ORDER:
             unit = getattr(shared, name)
@@ -893,7 +942,7 @@
         name: jax.tree.map(kinds.get(name, lambda a: fixed(a.shape)), value) for name, value in operands.items()
     }
     keeps = operands["keeps"]
-    shapes = {name: keeps[name].shape[3:] for name in keeps}
+    shapes = {name: keeps[name].shape[4:] for name in keeps}
     shapes.update(out_two=(model // (4 * depth), model // 2), out_one=(model // (4 * depth), model // 2))
     block = jax.ShapeDtypeStruct((2, HALF, model), BF16)
 
@@ -918,23 +967,23 @@
     for name, order in SHARED_ORDER.items():
         rows, lanes = shapes[name]
         scratch[name] = dict(
-            total=room(depth, 2, 2, rows, lanes),
-            got=[room(*s) for s in Sum.rooms(depth, 3, order, rows, lanes)],
+            total=room(depth // 2, 2, 2, 2, rows, lanes),
+            got=[room(*s) for s in Sum.rooms(depth // 2, 4, order, rows, lanes)],
             last=room(2, rows // 2, lanes, kind=F32), other=room(rows // 2, lanes, kind=F32),
         )
     for name, (y_first, order) in SLOT_ORDER.items():
-        lanes = 2 * GROUP if name.startswith("kv") else GROUP
-        got = [room(*s) for s in Sum.rooms(depth, 2, order, share, lanes)]
-        both = room(2, depth, 2, share, lanes)
+        piece = (share, 2 * GROUP) if name.startswith("kv") else query_shape(share)
+        got = [room(*s) for s in Sum.rooms(depth // 2, 3, order, *piece)]
+        both = room(2, depth // 2, 2, 2, *piece)
         scratch[name] = dict(total=both, pair=both, got=got)
         if y_first:
-            scratch[name].update(across=room(depth, 2, share, lanes))
+            scratch[name].update(across=room(depth // 2, 2, 2, *piece))
         else:
-            scratch[name].update(across=room(share, lanes), chunk=room(share, lanes), far=list(got))
+            scratch[name].update(across=room(*piece), chunk=room(*piece), far=list(got))
     scratch.update(
-        pairs={name: room(depth, 2, 2, *shapes[name]) for name in keeps},
-        out_send=room(depth, 2, 2, *shapes["out_one"]), out_pair=room(depth, 2, 2, *shapes["out_one"]), kv_send=room(2, depth, 2, share, 2 * GROUP),
-        q_send=room(2, depth, 2, share, GROUP), block=room(2, HALF, model), branch=room(model, BLOCK),
+        pairs={name: room(depth // 2, 2, 2, 2, *shapes[name]) for name in keeps},
+        out_send=room(depth // 2, 2, 2, 2, *shapes["out_one"]), out_pair=room(depth // 2, 2, 2, 2, *shapes["out_one"]), kv_send=room(2, depth // 2, 2, 2, share, 2 * GROUP),
+        q_send=room(2, depth // 2, 2, 2, *query_shape(share)), block=room(2, HALF, model), branch=room(model, BLOCK),
         acc_a=room(BLOCK, model, kind=F32), acc_b=room(BLOCK, model, kind=F32), dqkv=room(BLOCK, 3 * GROUP),
         dq=room(GROUP, BLOCK), do=room(GROUP, BLOCK), mask=room(BLOCK, BLOCK), gains=room(8, model, kind=F32),
         gains_got=room(depth + 2, 8, model, kind=F32), bias=room(4, 8, TILE, kind=F32),
@@ -943,8 +992,9 @@
         wo=room(model, model), ctx=room(model, BLOCK), n=room(model, BLOCK), mem=room(model, BLOCK),
     )
     z = depth - 1
-    copies = sum(2 + 2 + z for _ in SHARED_ORDER) + 3 + (3 + z) + (4 + z)
-    copies += sum(2 + (1 + z) + 1 + (0 if y_first else 1 + z) for y_first, _ in SLOT_ORDER.values())
+    copies = 3 + (3 + z) + (4 + z)
+    copies += sum(2 + Sum.count(depth // 2, order) for order in SHARED_ORDER.values())
+    copies += sum(3 + (1 if y_first else 2) * Sum.count(depth // 2, order) for y_first, order in SLOT_ORDER.values())
     scratch.update(send=pltpu.SemaphoreType.DMA((copies,)), recv=pltpu.SemaphoreType.DMA((copies,)))
     scratch.update(load=pltpu.SemaphoreType.DMA((18,)))
 
@@ -1025,7 +1075,7 @@
 
 
 def forward_kernel(ins, outs, r):
-    place = Place(1)
+    place = Place(2)
     step = pl.program_id(0)
     core = place.core
     copies = Copies(r.send, r.recv)
@@ -1475,6 +1525,10 @@
         batch_axis // 2,
         dict(second=fwd.second, cot=fwd.cot, gain=ff_gain, gate=ff_gate, up=ff_up, down=ff_down),
     )
+
+    def split(array):
+        return array.reshape(batch_axis // 4, 2, *array.shape[1:])
+
     done = backward_call(
         batch_axis,
         dict(
@@ -1486,8 +1540,8 @@
                 after=ff.after, wo_two=cross_out, ctx_two=fwd.ctx_two, n_two=fwd.n_two, mem=fwd.mem,
                 first=fwd.first, wo_one=self_out, ctx_one=fwd.ctx_one, n_one=fwd.n_one, tok=fwd.tok,
             ),
-            sends=dict(gate=ff.gate[0], up=ff.up[0], down_a=ff.down_a[0], down_b=ff.down_b[0]),
-            keeps=dict(gate=ff.gate[1], up=ff.up[1], down_a=ff.down_a[1], down_b=ff.down_b[1]),
+            sends=dict(gate=split(ff.gate[0]), up=split(ff.up[0]), down_a=split(ff.down_a[0]), down_b=split(ff.down_b[0])),
+            keeps=dict(gate=split(ff.gate[1]), up=split(ff.up[1]), down_a=split(ff.down_a[1]), down_b=split(ff.down_b[1])),
             layer=ff.layer,
         ),
     )

time: 193 us -> 179 us (0.927)
  Pallas kernels: 191 us -> 178 us
    pallas_call x1, Pallas kernels: 108 us -> 94.7 us  [backward_call(): pl.pallas_call(kernel, grid=(8,), in_specs=jax.tree.leaves(in_specs), out...]
where the time goes in v5:
time: 179 us
  Pallas kernels  178 us (99%)
    pallas_call x1, Pallas kernels, backward_call(): pl.pallas_call(kernel, grid=(8,), in_specs=jax.tree.leaves(in_specs), out...  94.7 us
    pallas_call x1, Pallas kernels, forward_call(): pl.pallas_call(kernel, grid=(8,), in_specs=jax.tree.leaves(in_specs), out...  46.7 us
    pallas_call x1, Pallas kernels, ff_call(): pl.pallas_call(kernel, grid=(FF_STEPS,), in_specs=jax.tree.leaves(in_spec...  32.4 us
    pallas_call x1, Pallas kernels, finish_call(): pl.pallas_call(kernel, in_specs=[fixed(results['gains'].shape), fixed(res...  4.66 us

profile of v5, /device:TPU:0, one launch (start us, length us, event | category | flops | bytes accessed | tf_op | source)
XLA Modules:
  0.0 179.2 jit_solution(572909245602992384)
XLA Ops:
  0.7 46.7 %shard_map.340 = (bf16[512,768]{1,0:T(8,128)(2,1)}, bf16[768,512]{1,0:T(8,128)(2,1)}, bf16[768,512]{1,0:T(8,128)(2,1)}, f32[512,768]{1,0:T(8,128)}, bf16[4,384,5...) custom-call(bf16[2,256,768]{2,1,0:T(8,128)(2,1)} %refs_0_.2, ...), custom_call_target="tpu_custom_call" | custom-call | flops 10000000000 | bytes 40000000 | tf_op jit(solution)/shard_map/pallas_call | solution.py:1314
  47.3 32.4 %shard_map.341 = (f32[512,768]{1,0:T(8,128)}, bf16[4,2,2,48,512]{4,3,2,1,0:T(8,128)(2,1)}, bf16[4,2,2,48,512]{4,3,2,1,0:T(8,128)(2,1)}, bf16[4,2,2,48,512]{4,3,2...) custom-call(bf16[512,768]{1,0:T(8,128)(2,1)} %get-tuple-element.80.r, ...), custom_call_target="tpu_custom_call" | custom-call | flops 14499999744 | bytes 24000000 | tf_op jit(solution)/shard_map/pallas_call | solution.py:1492
  79.7 94.7 %shard_map.342 = (f32[8,128]{1,0:T(8,128)}, f32[24,2048]{1,0:T(8,128)}, f32[8,768]{1,0:T(8,128)}, f32[64,768]{1,0:T(8,128)}, bf16[2,256,768]{2,1,0:T(8,128)(2,1)...) custom-call(f32[768]{0:T(1024)} %refs_0_.3, ...), custom_call_target="tpu_custom_call" | custom-call | flops 20000000000 | bytes 40000000 | tf_op jit(solution)/shard_map/pallas_call | solution.py:1012
  174.4 4.7 %shard_map.343 = (f32[3,32]{1,0:T(4,128)}, f32[24]{0:T(128)}, f32[24]{0:T(128)}, f32[24]{0:T(128)}, f32[24,2048]{1,0:T(8,128)}, /*index=5*/f32[64,768]{1,0:T(8,1...) custom-call(f32[8,768]{1,0:T(8,128)} %get-tuple-element.108.gains, ...), custom_call_target="tpu_custom_call" | custom-call | tf_op jit(solution)/shard_map/pallas_call | solution.py:1358

commit v6 on v5

--- a/solution.py
+++ b/solution.py
@@ -310,12 +310,22 @@
 
 
 class Sum:
-    def __init__(self, place, copies, total, got, order):
+    def __init__(self, place, copies, total, got, order, tiles=()):
         self.place, self.total, self.got, self.order = place, total, got, order
         self.dims = len(total.shape) - 2
         self.stages = []
         for at, axis in enumerate(order):
             room = got[at]
+            if at == 0 and tiles:
+                assert axis in (X, Y)
+                self.stages.append([
+                    copies.new(
+                        self.source(0, 1, tile), (lambda room, tile: lambda: room.at[tile])(room, tile),
+                        place.to_x if axis == X else place.to_y,
+                    )
+                    for tile in tiles
+                ])
+                continue
             if axis == ZH:
                 stage = [
                     copies.new(self.source(at, k), (lambda room, k: lambda: room.at[k - 1])(room, k), place.to_zh[k - 1])
@@ -344,9 +354,9 @@
     def mine(self, axis):
         return (self.place.zh, self.place.z0, self.place.x, self.place.y)[axis]
 
-    def source(self, at, k):
+    def source(self, at, k, tile=()):
         def view():
-            index = [slice(None)] * self.dims
+            index = list(tile) + [slice(None)] * (self.dims - len(tile))
             for axis in self.order[:at]:
                 index[axis] = self.mine(axis)
             axis = self.order[at]
@@ -433,10 +443,8 @@
         self.pair = copies.new(lambda: send, lambda: pair, place.to_core)
         self.swap = copies.new(lambda: room.last.at[1 - place.core], lambda: room.other, place.to_core)
 
-    def enter(self, keep=None):
+    def enter(self):
         self.pair.got()
-        if keep is not None:
-            keep.wait()
         add_loop(self.room.total, self.from_pair)
         self.sum.start(0)
 
@@ -458,6 +466,36 @@
     def sent(self):
         self.swap.sent()
         self.sum.sent()
+
+
+class Tiled(Shared):
+    def __init__(self, place, copies, room, order, stage, pair):
+        self.place, self.room, self.from_pair = place, room, pair
+        self.tiles = [tile_of_steps(place.far, t) for t in range(FF_STEPS)]
+        self.sum = Sum(place, copies, room.total, room.got, order, self.tiles)
+        self.pairs = [
+            copies.new(
+                (lambda t: lambda: stage.at[t % stage.shape[0]])(t), (lambda tile: lambda: pair.at[tile])(tile), place.to_core
+            )
+            for t, tile in enumerate(self.tiles)
+        ]
+        self.swap = copies.new(lambda: room.last.at[1 - place.core], lambda: room.other, place.to_core)
+
+    def enter_tile(self, t):
+        self.pairs[t].got()
+        add_loop(self.room.total.at[self.tiles[t]], self.from_pair.at[self.tiles[t]])
+        self.sum.stages[0][t].start()
+
+
+FF_STEPS = 4
+
+
+def tile_of_steps(far, t):
+    return (t // 2, t % 2) if far == 2 else (slice(t * far // FF_STEPS, (t + 1) * far // FF_STEPS),)
+
+
+def over_rows(left, right):
+    return lax.dot_general(left, right, (((1,), (1,)), ((), ())), preferred_element_type=F32)
 
 
 class Slots:
@@ -506,11 +544,11 @@
 
 
 SHARED_ORDER = dict(
-    gate=(Y, X, Z0, ZH), up=(Z0, Y, X, ZH), down_a=(X, Z0, Y, ZH), down_b=(Y, X, Z0, ZH),
-    out_two=(Z0, X, Y, ZH), out_one=(Y, Z0, X, ZH),
+    gate=(Y, X, Z0, ZH), up=(X, Z0, Y, ZH), down_a=(Y, X, Z0, ZH), down_b=(Z0, X, Y, ZH),
+    out_two=(X, Z0, ZH, Y), out_one=(Y, X, Z0, ZH),
 )
 SLOT_ORDER = dict(
-    kv_two=(False, (X, Z0, ZH)), q_two=(True, (X, Z0, ZH)), kv_one=(False, (X, Z0, ZH)), q_one=(True, (X, Z0, ZH))
+    kv_two=(True, (X, Z0, ZH)), q_two=(True, (X, Z0, ZH)), kv_one=(False, (X, Z0, ZH)), q_one=(True, (Z0, X, ZH))
 )
 KV = slice(0, 2 * GROUP)
 QS = slice(2 * GROUP, 3 * GROUP)
@@ -549,9 +587,12 @@
     copies = Copies(r.send, r.recv)
     segs = Tiles(place, ins.segs)
 
+    parities, downs = r.gate_stage.shape[0], r.down_stage.shape[0]
+    down_stages = [r.down_stage.at[t % downs] for t in range(2)]
+    stages = dict(gate=r.gate_stage, up=r.up_stage, down_a=down_stages[0], down_b=down_stages[1])
     shared = Named({
-        name: Shared(
-            place, copies, getattr(r, name), order, getattr(ins.sends, name, r.out_send), getattr(r.pairs, name, r.out_pair)
+        name: (Tiled if name in ("gate", "up") else Shared)(
+            place, copies, getattr(r, name), order, stages.get(name, r.out_send), getattr(r.pairs, name, r.out_pair)
         )
         for name, order in SHARED_ORDER.items()
     })
@@ -581,13 +622,10 @@
         return loads[-1]
 
     i = ins.loaded
-    after, wo_two, ctx_two = load(i.after, r.after), load(i.wo_two, r.wo), load(i.ctx_two, r.ctx)
+    second, wo_two, ctx_two = load(i.second, r.hidden), load(i.wo_two, r.wo), load(i.ctx_two, r.ctx)
+    cots = [load(i.cot.at[pl.ds(half * HALF, HALF)], r.block.at[half]) for half in range(2)]
     n_two, mem, first, tok = load(i.n_two, r.n), load(i.mem, r.mem), load(i.first, r.hidden), load(i.tok, r.hidden)
     wo_one, ctx_one, n_one = load(i.wo_one, r.wo), load(i.ctx_one, r.ctx), load(i.n_one, r.n)
-    keeps = Named({
-        name: load(getattr(ins.keeps, name), getattr(r, name).total) for name in SHARED_ORDER if hasattr(ins.keeps, name)
-    })
-    layer_in = load(ins.layer, r.block)
     layer_put = load(r.block.at[core], outs.layer.at[core])
     memory_put = load(r.block.at[core], outs.memory.at[core])
     tokens_put = load(r.block.at[core], outs.tokens.at[core])
@@ -660,32 +698,45 @@
         plan.setdefault(point, []).extend(tasks)
 
     sh, sl = shared, slots
-    at((0, 0), sh.out_two.enter, lambda: sh.up.enter(keeps.up))
-    at((0, 1), lambda: sh.down_a.enter(keeps.down_a))
-    at((0, 2), lambda: sh.down_b.enter(keeps.down_b))
-    at((0, 3), sl.kv_two.pair[1].start, sl.q_two.pair[1].start)
-    at((1, 1), lambda: sh.out_two.sum.add(0))
-    at((1, 3), lambda: sl.kv_two.enter(1), lambda: sl.q_two.enter(1))
-    at((2, 0), lambda: sh.down_a.sum.add(0))
-    at((2, 2), lambda: sh.out_two.sum.add(1))
-    at((2, 3), sl.kv_two.pair[0].start, sl.q_two.pair[0].start, lambda: sh.gate.sum.add(0))
-    at((3, 2), lambda: sl.kv_two.far.add(0))
-    at((3, 3), lambda: sl.kv_two.enter(0), lambda: sl.q_two.enter(0))
-    at((3, 4), lambda: sh.up.sum.add(0), lambda: sh.down_b.sum.add(0))
-    at((4, 0), lambda: sh.down_a.sum.add(1), sh.out_one.enter, lambda: sh.gate.sum.add(1))
-    at((4, 1), sl.q_two.take)
-    at((4, 2), lambda: sl.kv_two.far.add(1), lambda: sh.out_two.sum.add(2))
-    at((4, 3), sl.kv_one.pair[1].start, sl.q_one.pair[1].start)
-    at((5, 0), lambda: sl.kv_two.own.add(0))
-    at((5, 1), lambda: sh.gate.sum.add(2))
-    at((5, 2), sl.kv_two.give)
-    at((5, 3), lambda: sl.kv_one.enter(1), lambda: sl.q_one.enter(1))
-    at((6, 0), lambda: sh.up.sum.add(1), lambda: sh.down_b.sum.add(1))
-    at((6, 1), lambda: sl.kv_two.own.add(1), lambda: sl.q_two.own.add(0))
-    at((6, 3), sl.kv_one.pair[0].start, sl.q_one.pair[0].start)
-    at((7, 0), lambda: sh.out_one.sum.add(0), lambda: sh.down_b.sum.add(2))
-    at((7, 1), lambda: sh.down_a.sum.add(2), lambda: sl.kv_one.far.add(0))
-    at((7, 2), lambda: sl.q_two.own.add(1))
+    def when_core(which, *tasks):
+        def run():
+            for task in tasks:
+                task()
+
+        return lambda: pl.when(core == which)(run)
+
+    for t in range(FF_STEPS):
+        at((t, 4), sh.gate.pairs[t].start, sh.up.pairs[t].start)
+        if t < FF_STEPS - 1:
+            at((t + 1, 1), lambda t=t: sh.gate.enter_tile(t), lambda t=t: sh.up.enter_tile(t))
+        at((t, 5), when_core(1 - t // 2, (sh.down_a, sh.down_b)[t % 2].pair.start))
+    at((2, 2), when_core(0, sh.down_a.enter))
+    at((2, 3), when_core(0, sh.down_b.enter))
+    at((4, 0), when_core(1, sh.down_a.enter, sh.down_b.enter))
+    at((4, 1), sh.out_two.enter)
+    at((4, 3), sl.kv_two.pair[1].start, sl.q_two.pair[1].start)
+    at((5, 0), lambda: sh.gate.sum.add(0), lambda: sh.up.sum.add(0))
+    at((5, 3), lambda: sl.kv_two.enter(1), lambda: sl.q_two.enter(1))
+    at((6, 0), lambda: sh.out_two.sum.add(0), lambda: sh.down_b.sum.add(0))
+    at((6, 1), lambda: sh.down_a.sum.add(0))
+    at((6, 3), sl.kv_two.pair[0].start, sl.q_two.pair[0].start)
+    at((7, 0), lambda: sh.up.sum.add(1), lambda: sh.gate.sum.add(1))
+    at((7, 2), lambda: sh.out_two.sum.add(1))
+    at((7, 3), lambda: sl.kv_two.enter(0), lambda: sl.q_two.enter(0), lambda: sh.down_b.sum.add(1))
+    at((7, 4), sl.kv_two.take, lambda: sh.gate.sum.add(2), lambda: sh.down_a.sum.add(1))
+    at((8, 0), lambda: sh.out_two.sum.add(2), sh.out_one.enter)
+    at((8, 2), sl.q_two.take, lambda: sh.down_a.sum.add(2))
+    at((8, 3), sl.kv_one.pair[1].start, sl.q_one.pair[1].start)
+    at((9, 0), lambda: sl.kv_two.own.add(0), sh.gate.last)
+    at((9, 1), lambda: sh.up.sum.add(2))
+    at((9, 2), lambda: sl.q_two.own.add(0))
+    at((9, 3), lambda: sl.kv_one.enter(1), lambda: sl.q_one.enter(1), lambda: sh.down_b.sum.add(2), sh.down_a.last)
+    at((10, 0), lambda: sl.kv_two.own.add(1), sh.out_two.last)
+    at((10, 1), lambda: sh.out_one.sum.add(0), lambda: sl.q_two.own.add(1))
+    at((10, 2), sh.up.last, sh.down_b.last)
+    at((10, 3), sl.kv_one.pair[0].start, sl.q_one.pair[0].start)
+    at((11, 1), lambda: sl.kv_one.far.add(0))
+    at((11, 3), lambda: sl.kv_one.enter(0), lambda: sl.q_one.enter(0), lambda: sh.out_one.sum.add(1))
 
     def tick(steps, index):
         for k in steps:
@@ -702,31 +753,114 @@
         barrier = pltpu.get_barrier_semaphore()
         for device in place.everyone():
             pl.semaphore_signal(barrier, inc=1, device_id=device, device_id_type=MESH)
-        for copy in (after, wo_two, ctx_two, layer_in):
+        for copy in [second] + cots + [wo_two, ctx_two, n_two, mem]:
             copy.start()
-        pl.semaphore_wait(barrier, len(place.everyone()))
-        for name in SHARED_ORDER:
-            if hasattr(keeps, name):
-                getattr(shared, name).pair.start()
-                getattr(keeps, name).start()
-        for copy in (n_two, mem, first):
-            copy.start()
-        after.wait()
+        r.gains[...] = jnp.zeros_like(r.gains)
+        second.wait()
         for part in range(4):
             rows = slice(part * TILE, (part + 1) * TILE)
-            r.branch[:, rows] = jnp.transpose(r.after[rows, :].astype(BF16))
-        key_mask(segs, key_segments(place, ins.memsegs), r.mask)
-        wo_two.wait()
-        ctx_two.wait()
-        layer_in.wait()
+            h = r.hidden[rows, :]
+            scale = lax.rsqrt(jnp.mean(h * h, axis=-1, keepdims=True) + NORM_EPS)
+            r.normed[rows, :] = (h * scale * row_of(ins.ff_gain)).astype(BF16)
+            r.acc_a[rows, :] = h
+            r.acc_b[rows, :] = jnp.zeros_like(h)
+        for part in range(4):
+            if part % 2 == 0:
+                cots[part // 2].wait()
+            rows = slice(part * TILE, (part + 1) * TILE)
+            r.branch[:, rows] = jnp.transpose(r.block[part // 2, (part % 2) * TILE : (part % 2 + 1) * TILE, :])
+        pl.semaphore_wait(barrier, len(place.everyone()))
+
+    for t in range(parities, FF_STEPS):
+
+        @pl.when(step == t)
+        def _(t=t):
+            sh.gate.pairs[t - parities].sent()
+            sh.up.pairs[t - parities].sent()
+
+    @pl.when(step < FF_STEPS)
+    def _():
+        root = np.float32(np.sqrt(2.0 / np.pi))
+        model = r.normed.shape[1]
+        for part in range(4):
+            rows = slice(part * TILE, (part + 1) * TILE)
+            normed = r.normed[rows, :]
+            gate, up = dot(normed, ins.ff_gate[...]), dot(normed, ins.ff_up[...])
+            grad = over_rows(r.block[part // 2, (part % 2) * TILE : (part % 2 + 1) * TILE, :], ins.ff_down[...])
+            square = gate * gate
+            half = 0.5 + 0.5 * jnp.tanh(gate * (root + (root * 0.044715) * square))
+            gelu = gate * half
+            slope = half + gelu * (2.0 - 2.0 * half) * (root + (3.0 * 0.044715 * root) * square)
+            activation = (gelu * up).astype(BF16)
+            grad_gate = (grad * up * slope).astype(BF16)
+            grad_up = (grad * gelu).astype(BF16)
+            r.mask[rows, :] = activation
+            r.grad_gate[:, rows] = jnp.transpose(grad_gate)
+            r.grad_up[:, rows] = jnp.transpose(grad_up)
+            r.acc_a[rows, :] = r.acc_a[rows, :] + dot(activation, ins.ff_down[...])
+            r.acc_b[rows, :] = r.acc_b[rows, :] + over_rows(grad_gate, ins.ff_gate[...]) + over_rows(grad_up, ins.ff_up[...])
+            tick(range(FF_STEPS), part)
+        lanes = model // 2
+        for which, keep in ((1 - core, False), (core, True)):
+            right = r.normed[:, pl.ds(pl.multiple_of(which * lanes, 128), lanes)]
+            for grads, total, stage in ((r.grad_gate, r.gate.total, r.gate_stage), (r.grad_up, r.up.total, r.up_stage)):
+                product = dot(grads[...], right).astype(BF16)
+                rows = total.shape[4]
+                for piece in range(product.shape[0] // rows):
+                    inner = ((piece // 4) % 2, (piece // 2) % 2, piece % 2)
+                    share = product[piece * rows : (piece + 1) * rows]
+                    if place.far == 2:
+                        head = (step // 2, step % 2) if keep else (step % parities,)
+                        inner = inner[1:]
+                    else:
+                        head = (step * (place.far // FF_STEPS) + piece // 8,) if keep else (step % parities, piece // 8)
+                    (total if keep else stage)[(*head, *inner)] = share
+            if not keep:
+                tick(range(FF_STEPS), 4)
+        per = model // 2
+        for part in range(2):
+            product = dot(r.branch[part * per : (part + 1) * per, :], r.mask[...]).astype(BF16)
+            for t in range(FF_STEPS):
+                total = (r.down_a, r.down_b)[t % 2].total
+                for target, mine in ((total, t // 2), (down_stages[t % 2], 1 - t // 2)):
+
+                    @pl.when(jnp.logical_and(step == t, core == mine))
+                    def _(target=target, product=product, part=part, t=t, mine=mine):
+                        if downs == 1 and t % 2 == 1 and part == 0 and mine != t // 2:
+                            sh.down_a.pair.sent()
+                        rows = target.shape[4]
+                        for piece in range(per // rows):
+                            to = part * (per // rows) + piece
+                            to = (to // 8, (to // 4) % 2, (to // 2) % 2, to % 2)
+                            target[to] = product[piece * rows : (piece + 1) * rows]
+
+        tick(range(FF_STEPS), 5)
+
+    @pl.when(step == FF_STEPS - 1)
+    def _():
+        total = jnp.zeros((1, r.hidden.shape[1]), F32)
+        for part in range(4):
+            rows = slice(part * TILE, (part + 1) * TILE)
+            block_rows = (part // 2, slice((part % 2) * TILE, (part % 2 + 1) * TILE))
+            h, e = r.hidden[rows, :], r.acc_b[rows, :]
+            scale = lax.rsqrt(jnp.mean(h * h, axis=-1, keepdims=True) + NORM_EPS)
+            weighted = e * row_of(ins.ff_gain)
+            inner = jnp.mean(weighted * h, axis=-1, keepdims=True)
+            result = r.block[block_rows].astype(F32) + weighted * scale - h * (scale * scale * scale * inner)
+            total = total + jnp.sum(e * h * scale, axis=0, keepdims=True)
+            r.after[rows, :] = result
+            r.branch[:, rows] = jnp.transpose(result.astype(BF16))
+            r.block[block_rows] = r.acc_a[rows, :].astype(BF16)
+        r.gains[2:3, :] = total
         layer_swap.start()
         layer_put.start()
-        sh.gate.enter(keeps.gate)
+        sh.gate.enter_tile(FF_STEPS - 1)
+        sh.up.enter_tile(FF_STEPS - 1)
+        key_mask(segs, key_segments(place, ins.memsegs), r.mask)
+        first.start()
+        for copy in (wo_two, ctx_two, n_two, mem):
+            copy.wait()
         out_products(sh.out_two, r.ctx, r.branch)
-        n_two.wait()
-        mem.wait()
-        r.gains[...] = jnp.zeros_like(r.gains)
-        r.gains[2:3, :] = row_of(ins.ff_gain_grad)
 
     slot = 3 - step % 4
     odd = slot % 2 == 1
@@ -743,7 +877,7 @@
             weight_products(kv.room.total.at[slot // 2], kv_left, KV)
             weight_products(q.room.total.at[slot // 2], q_left, QS)
 
-    @pl.when(step < 4)
+    @pl.when(step // 4 == 1)
     def _():
         r.do[...] = dot(r.wo[rows_at, :], r.branch[...]).astype(BF16)
         kv, q, lse = ins.kv_two, ins.q_two, ins.lse_two
@@ -756,13 +890,13 @@
         def tile_of(scores, index, kt, qt):
             return scores + r.mask[kt * TILE : (kt + 1) * TILE, qt * TILE : (qt + 1) * TILE].astype(F32)
 
-        attention_back(read, tile_of, False, lambda *a: None, r.dq, r.dqkv, lambda h: tick(range(4), h))
+        attention_back(read, tile_of, False, lambda *a: None, r.dq, r.dqkv, lambda h: tick(range(4, 8), h))
         slot_products(sl.kv_two, sl.q_two, r.mem, r.n)
-        tick(range(4), 3)
-        add_rows(r.acc_b, KV, ins.wt_two[0, KV, :], step == 0)
-        add_rows(r.acc_a, QS, ins.wt_two[0, QS, :], step == 0)
-
-    @pl.when(step == 3)
+        tick(range(4, 8), 3)
+        add_rows(r.acc_b, KV, ins.wt_two[0, KV, :], step == 4)
+        add_rows(r.acc_a, QS, ins.wt_two[0, QS, :], step == 4)
+
+    @pl.when(step == 7)
     def _():
         for copy in (wo_one, ctx_one, n_one):
             copy.start()
@@ -780,10 +914,10 @@
             copy.wait()
         sh.out_two.pair.sent()
         out_products(sh.out_one, r.ctx, r.branch)
-        for task in plan[3, 4]:
+        for task in plan[7, 4]:
             task()
 
-    @pl.when(step >= 4)
+    @pl.when(step >= 8)
     def _():
         r.do[...] = dot(r.wo[rows_at, :], r.branch[...]).astype(BF16)
         qkv, lse = ins.qkv_one, ins.lse_one
@@ -803,7 +937,7 @@
 
         attention_back(
             read, lambda scores, index, kt, qt: self_tile(scores, kt, qt, tiles[index], segs, 0), True, note,
-            r.dq, r.dqkv, lambda h: tick(range(4, 8), h),
+            r.dq, r.dqkv, lambda h: tick(range(8, 12), h),
         )
         key = lax.broadcasted_iota(jnp.int32, (TILE, TILE), 0)
         query = lax.broadcasted_iota(jnp.int32, (TILE, TILE), 1)
@@ -821,7 +955,7 @@
         r.bias[slot] = lax.dot_general(
             by_distance, one_hot, (((1,), (1,)), ((), ())), precision=lax.Precision.HIGHEST, preferred_element_type=F32
         )
-        for k, j in ((4, 1), (6, 0)):
+        for k, j in ((8, 1), (10, 0)):
 
             @pl.when(step == k)
             def _(j=j):
@@ -829,13 +963,11 @@
                 sl.q_two.pair[j].sent()
 
         slot_products(sl.kv_one, sl.q_one, r.n, r.n)
-        tick(range(4, 8), 3)
-        add_rows(r.acc_a, slice(0, 3 * GROUP), ins.wt_one[0], step == 4)
-
-    @pl.when(step == 7)
+        tick(range(8, 12), 3)
+        add_rows(r.acc_a, slice(0, 3 * GROUP), ins.wt_one[0], step == 8)
+
+    @pl.when(step == 11)
     def _():
-        sl.kv_one.enter(0)
-        sl.q_one.enter(0)
         gains, bias = r.gains, r.bias
         memory_swap.sent()
         memory_put.wait()
@@ -846,8 +978,8 @@
         gain_copies[0].start()
         bias_copies[0].start()
         bias_copies[1].start()
-        sh.out_one.sum.add(1)
-        sh.up.sum.add(2)
+        sl.q_one.take()
+        sl.kv_one.far.add(1)
         gain_copies[0].done()
         gains[...] = gains[...] + r.gains_got[0]
         bias_copies[0].done()
@@ -856,23 +988,20 @@
         bias[2] = bias[2] + r.bias_got[1]
         gain_copies[1].start()
         bias_copies[2].start()
-        sl.q_one.take()
-        sl.kv_one.far.add(1)
+        sl.q_one.own.add(0)
+        sh.out_one.sum.add(2)
         sl.kv_one.own.add(0)
-        sh.gate.last()
-        sh.out_two.last()
-        sh.down_b.last()
-        sh.out_one.sum.add(2)
+        put_heads((outs.wk_two, outs.wv_two), sl.kv_two.finish())
+        put_query(outs.wq_two, sl.q_two.finish())
         gain_copies[1].done()
         gains[...] = gains[...] + r.gains_got[1]
         bias_copies[2].done()
         bias[0] = bias[0] + r.bias_got[2]
         gain_copies[2].start()
         bias_copies[3].start()
-        sl.q_one.own.add(0)
         sl.kv_one.give()
-        sl.kv_one.own.add(1)
-        sh.down_a.last()
+        sl.q_one.own.add(1)
+        sh.out_one.last()
         gain_copies[2].done()
         gains[...] = gains[...] + r.gains_got[2]
         bias_copies[3].done()
@@ -880,12 +1009,13 @@
         for k in range(depth - 1):
             gain_copies[3 + k].start()
             bias_copies[4 + k].start()
-        sl.q_one.own.add(1)
-        put_heads((outs.wk_two, outs.wv_two), sl.kv_two.finish())
-        put_query(outs.wq_two, sl.q_two.finish())
-        sh.up.last()
-        sh.out_one.last()
-        put_heads((outs.wk_one, outs.wv_one), sl.kv_one.finish())
+        sl.kv_one.own.add(1)
+        sh.up.store(outs.up, 0, outs.up.shape[1] // 2)
+        sh.down_a.store(outs.down, 0, outs.down.shape[1] // 2)
+        sh.down_b.store(outs.down, outs.down.shape[1] // 4, outs.down.shape[1] // 2)
+        sh.gate.store(outs.gate, 0, outs.gate.shape[1] // 2)
+        sh.out_two.store(outs.out_two, 0, outs.out_two.shape[1] // 2)
+        sh.out_one.store(outs.out_one, 0, outs.out_one.shape[1] // 2)
         gain_total, bias_total = gains[...], bias[0]
         for k in range(depth - 1):
             gain_copies[3 + k].done()
@@ -894,17 +1024,15 @@
             bias_total = bias_total + r.bias_got[4 + k]
         outs.gains[...] = gain_total
         outs.bias[...] = bias_total
-        sh.up.store(outs.up, 0, outs.up.shape[1] // 2)
-        sh.down_a.store(outs.down, 0, outs.down.shape[1] // 2)
-        sh.down_b.store(outs.down, outs.down.shape[1] // 4, outs.down.shape[1] // 2)
-        sh.gate.store(outs.gate, 0, outs.gate.shape[1] // 2)
-        sh.out_two.store(outs.out_two, 0, outs.out_two.shape[1] // 2)
         put_query(outs.wq_one, sl.q_one.finish())
-        sh.out_one.store(outs.out_one, 0, outs.out_one.shape[1] // 2)
+        put_heads((outs.wk_one, outs.wv_one), sl.kv_one.finish())
         for name in SHARED_ORDER:
             unit = getattr(shared, name)
             unit.sent()
-            if unit is not sh.out_two:
+            if name in ("gate", "up"):
+                for copy in unit.pairs[-parities:]:
+                    copy.sent()
+            elif unit is not sh.out_two and (unit is not sh.down_a or downs == 2):
                 unit.pair.sent()
         for name in SLOT_ORDER:
             getattr(slots, name).sent()
@@ -919,6 +1047,8 @@
 
 def backward_call(batch_size, operands):
     depth = batch_size // 2
+    tight = depth > 4
+    once = dict(pipeline_mode=pl.Buffered(1)) if tight else {}
     tok = operands["loaded"]["tok"]
     model = tok.shape[1]
     share = model // batch_size
@@ -927,23 +1057,43 @@
     def fixed(shape):
         return pl.BlockSpec(shape, lambda t: (0,) * len(shape))
 
+    def phase(t):
+        c = t // 4
+        return (1 - c) * (2 - c) // 2, c * (2 - c), c * (c - 1) // 2
+
     def early(array):
-        return pl.BlockSpec((1,) + array.shape[1:], lambda t: (3 - t + (t // 4) * (t - 3), 0, 0))
+        def at(t):
+            _, cross, own = phase(t)
+            return (3 - cross * (t % 4) - 3 * own, 0, 0)
+
+        return pl.BlockSpec((1,) + array.shape[1:], at, **once)
 
     def late(array):
-        return pl.BlockSpec((1,) + array.shape[1:], lambda t: (3 - (t // 4) * (t - 4), 0, 0))
+        return pl.BlockSpec((1,) + array.shape[1:], lambda t: (3 - phase(t)[2] * (t % 4), 0, 0))
+
+    def tile(t):
+        return 3 - phase(t)[0] * (3 - t % 4)
+
+    def wide_tile(array):
+        return pl.BlockSpec((array.shape[0], array.shape[1] // FF_STEPS), lambda t: (0, tile(t)), **once)
+
+    def deep_tile(array):
+        return pl.BlockSpec((array.shape[0] // FF_STEPS, array.shape[1]), lambda t: (tile(t), 0), **once)
 
     kinds = dict(
         segs=lambda a: pl.BlockSpec(memory_space=pltpu.SMEM), kv_two=early, q_two=early, lse_two=early, wt_two=early,
-        qkv_one=late, lse_one=late, wt_one=late, table=late, loaded=lambda a: anywhere, sends=lambda a: anywhere,
-        keeps=lambda a: anywhere, layer=lambda a: anywhere,
+        qkv_one=late, lse_one=late, wt_one=late, table=late, loaded=lambda a: anywhere,
+        ff_gate=wide_tile, ff_up=wide_tile, ff_down=deep_tile,
     )
     in_specs = {
         name: jax.tree.map(kinds.get(name, lambda a: fixed(a.shape)), value) for name, value in operands.items()
     }
-    keeps = operands["keeps"]
-    shapes = {name: keeps[name].shape[4:] for name in keeps}
+    columns = operands["ff_gate"].shape[1]
+    made = ("gate", "up", "down_a", "down_b")
+    shapes = dict(gate=(columns // (4 * depth), model // 2), down_a=(model // (4 * depth), columns // 4))
+    shapes.update(up=shapes["gate"], down_b=shapes["down_a"])
     shapes.update(out_two=(model // (4 * depth), model // 2), out_one=(model // (4 * depth), model // 2))
+    tile_room = (2, 2, 2) if depth == 4 else (1, depth // 8, 2, 2, 2)
     block = jax.ShapeDtypeStruct((2, HALF, model), BF16)
 
     def wide(rows, columns):
@@ -981,11 +1131,15 @@
         else:
             scratch[name].update(across=room(*piece), chunk=room(*piece), far=list(got))
     scratch.update(
-        pairs={name: room(depth // 2, 2, 2, 2, *shapes[name]) for name in keeps},
+        pairs={name: room(depth // 2, 2, 2, 2, *shapes[name]) for name in made},
+        gate_stage=room(*tile_room, *shapes["gate"]), up_stage=room(*tile_room, *shapes["up"]),
+        down_stage=room(1 if tight else 2, depth // 2, 2, 2, 2, *shapes["down_a"]), normed=room(BLOCK, model),
+        grad_gate=room(columns // FF_STEPS, BLOCK),
+        grad_up=room(columns // FF_STEPS, BLOCK),
         out_send=room(depth // 2, 2, 2, 2, *shapes["out_one"]), out_pair=room(depth // 2, 2, 2, 2, *shapes["out_one"]), kv_send=room(2, depth // 2, 2, 2, share, 2 * GROUP),
         q_send=room(2, depth // 2, 2, 2, *query_shape(share)), block=room(2, HALF, model), branch=room(model, BLOCK),
         acc_a=room(BLOCK, model, kind=F32), acc_b=room(BLOCK, model, kind=F32), dqkv=room(BLOCK, 3 * GROUP),
-        dq=room(GROUP, BLOCK), do=room(GROUP, BLOCK), mask=room(BLOCK, BLOCK), gains=room(8, model, kind=F32),
+        dq=room(GROUP, BLOCK), do=room(GROUP, BLOCK), mask=room(BLOCK, columns // FF_STEPS), gains=room(8, model, kind=F32),
         gains_got=room(depth + 2, 8, model, kind=F32), bias=room(4, 8, TILE, kind=F32),
         bias_got=room(depth + 3, 8, TILE, kind=F32),
         after=room(BLOCK, model, kind=F32), hidden=room(BLOCK, model, kind=F32),
@@ -993,7 +1147,7 @@
     )
     z = depth - 1
     copies = 3 + (3 + z) + (4 + z)
-    copies += sum(2 + Sum.count(depth // 2, order) for order in SHARED_ORDER.values())
+    copies += sum(2 + Sum.count(depth // 2, order) for order in SHARED_ORDER.values()) + 2 * 2 * (FF_STEPS - 1)
     copies += sum(3 + (1 if y_first else 2) * Sum.count(depth // 2, order) for y_first, order in SLOT_ORDER.values())
     scratch.update(send=pltpu.SemaphoreType.DMA((copies,)), recv=pltpu.SemaphoreType.DMA((copies,)))
     scratch.update(load=pltpu.SemaphoreType.DMA((18,)))
@@ -1011,13 +1165,13 @@
 
     results = pl.pallas_call(
         kernel,
-        grid=(8,),
+        grid=(12,),
         in_specs=jax.tree.leaves(in_specs),
         out_specs=jax.tree.leaves(out_specs),
         out_shape=out_shapes,
         scratch_shapes=rooms,
         compiler_params=pltpu.CompilerParams(
-            collective_id=0, has_side_effects=True, vmem_limit_bytes=66_000_000, dimension_semantics=("arbitrary",)
+            collective_id=0, has_side_effects=True, vmem_limit_bytes=67_000_000, dimension_semantics=("arbitrary",)
         ),
         cost_estimate=pl.CostEstimate(flops=20_000_000_000, bytes_accessed=40_000_000, transcendentals=6_000_000),
     )(*arrays)
@@ -1365,143 +1519,6 @@
     return dict(zip(plain, rest[3:]), bias=bias, gain_0=rest[0], gain_1=rest[1], gain_2=rest[2])
 
 
-FF_STEPS = 4
-
-
-def ff_tile(t):
-    core = lax.axis_index("head") % 2
-    half = t // 2
-    other = 1 - core
-    return 2 * (half + other - 2 * half * other) + t % 2
-
-
-def over_rows(left, right):
-    return lax.dot_general(left, right, (((1,), (1,)), ((), ())), preferred_element_type=F32)
-
-
-def ff_kernel(ins, outs, r):
-    step = pl.program_id(0)
-    core = lax.axis_index("head") % 2
-    model = ins.second.shape[1]
-    root = np.float32(np.sqrt(2.0 / np.pi))
-
-    @pl.when(step == 0)
-    def _():
-        for part in range(4):
-            rows = slice(part * TILE, (part + 1) * TILE)
-            h = ins.second[rows, :]
-            scale = lax.rsqrt(jnp.mean(h * h, axis=-1, keepdims=True) + NORM_EPS)
-            r.normed[rows, :] = (h * scale * row_of(ins.gain)).astype(BF16)
-            r.cot[:, rows] = jnp.transpose(ins.cot[rows, :])
-            r.layer[rows, :] = h
-            r.back[rows, :] = jnp.zeros_like(h)
-
-    for part in range(4):
-        rows = slice(part * TILE, (part + 1) * TILE)
-        normed = r.normed[rows, :]
-        gate, up = dot(normed, ins.gate[...]), dot(normed, ins.up[...])
-        grad = over_rows(ins.cot[rows, :], ins.down[...])
-        square = gate * gate
-        half = 0.5 + 0.5 * jnp.tanh(gate * (root + (root * 0.044715) * square))
-        gelu = gate * half
-        slope = half + gelu * (2.0 - 2.0 * half) * (root + (3.0 * 0.044715 * root) * square)
-        activation = (gelu * up).astype(BF16)
-        grad_gate = (grad * up * slope).astype(BF16)
-        grad_up = (grad * gelu).astype(BF16)
-        r.act[rows, :] = activation
-        r.grad_gate[:, rows] = jnp.transpose(grad_gate)
-        r.grad_up[:, rows] = jnp.transpose(grad_up)
-        r.layer[rows, :] = r.layer[rows, :] + dot(activation, ins.down[...])
-        r.back[rows, :] = r.back[rows, :] + over_rows(grad_gate, ins.gate[...]) + over_rows(grad_up, ins.up[...])
-
-    lanes = model // 2
-
-    def spread_out(target, product, first):
-        rows = target.shape[3]
-        for piece in range(product.shape[0] // rows):
-            at = first + piece
-            target[at // 4, (at // 2) % 2, at % 2] = product[piece * rows : (piece + 1) * rows]
-
-    for which, name in ((1 - core, 0), (core, 1)):
-        right = r.normed[:, pl.ds(pl.multiple_of(which * lanes, 128), lanes)]
-        for grads, target in ((r.grad_gate, outs.gate[name]), (r.grad_up, outs.up[name])):
-            spread_out(target, dot(grads[...], right).astype(BF16), 0)
-    for t, target in enumerate((outs.down_a[0], outs.down_b[0], outs.down_a[1], outs.down_b[1])):
-
-        @pl.when(step == t)
-        def _(target=target):
-            per = model // 2
-            for part in range(2):
-                product = dot(r.cot[part * per : (part + 1) * per, :], r.act[...]).astype(BF16)
-                spread_out(target, product, part * (per // target.shape[3]))
-
-    @pl.when(step == FF_STEPS - 1)
-    def _():
-        total = jnp.zeros((1, model), F32)
-        for part in range(4):
-            rows = slice(part * TILE, (part + 1) * TILE)
-            h, e = ins.second[rows, :], r.back[rows, :]
-            scale = lax.rsqrt(jnp.mean(h * h, axis=-1, keepdims=True) + NORM_EPS)
-            weighted = e * row_of(ins.gain)
-            inner = jnp.mean(weighted * h, axis=-1, keepdims=True)
-            outs.after[rows, :] = ins.cot[rows, :].astype(F32) + weighted * scale - h * (scale * scale * scale * inner)
-            total = total + jnp.sum(e * h * scale, axis=0, keepdims=True)
-            outs.layer[part // 2, (part % 2) * TILE : (part % 2 + 1) * TILE, :] = r.layer[rows, :].astype(BF16)
-        outs.gain_grad[...] = jnp.reshape(total, (model,))
-
-
-def ff_call(depth, operands):
-    model, columns = operands["gate"].shape
-    tile = columns // FF_STEPS
-
-    def fixed(shape):
-        return pl.BlockSpec(shape, lambda t: (0,) * len(shape))
-
-    in_specs = {name: fixed(a.shape) for name, a in operands.items()}
-    in_specs.update(
-        gate=pl.BlockSpec((model, tile), lambda t: (0, ff_tile(t))),
-        up=pl.BlockSpec((model, tile), lambda t: (0, ff_tile(t))),
-        down=pl.BlockSpec((tile, model), lambda t: (ff_tile(t), 0)),
-    )
-    wide = jax.ShapeDtypeStruct((depth, 2, 2, columns // (4 * depth), model // 2), BF16)
-    deep = jax.ShapeDtypeStruct((depth, 2, 2, model // (4 * depth), tile), BF16)
-    by_tile = pl.BlockSpec((depth // FF_STEPS,) + wide.shape[1:], lambda t: (ff_tile(t), 0, 0, 0, 0))
-    outs = dict(
-        layer=jax.ShapeDtypeStruct((2, HALF, model), BF16), after=jax.ShapeDtypeStruct((BLOCK, model), F32),
-        gain_grad=jax.ShapeDtypeStruct((model,), F32), gate=[wide, wide], up=[wide, wide],
-        down_a=[deep, deep], down_b=[deep, deep],
-    )
-    out_specs = jax.tree.map(lambda a: by_tile if a is wide else fixed(a.shape), outs)
-    scratch = dict(
-        normed=pltpu.VMEM((BLOCK, model), BF16), cot=pltpu.VMEM((model, BLOCK), BF16),
-        layer=pltpu.VMEM((BLOCK, model), F32), back=pltpu.VMEM((BLOCK, model), F32),
-        act=pltpu.VMEM((BLOCK, tile), BF16), grad_gate=pltpu.VMEM((tile, BLOCK), BF16),
-        grad_up=pltpu.VMEM((tile, BLOCK), BF16),
-    )
-    arrays, in_tree = jax.tree.flatten(operands)
-    out_shapes, out_tree = jax.tree.flatten(outs)
-    rooms, room_tree = jax.tree.flatten(scratch)
-
-    def kernel(*refs):
-        a, b = len(arrays), len(arrays) + len(out_shapes)
-        ff_kernel(
-            Named(jax.tree.unflatten(in_tree, refs[:a])), Named(jax.tree.unflatten(out_tree, refs[a:b])),
-            Named(jax.tree.unflatten(room_tree, refs[b:])),
-        )
-
-    results = pl.pallas_call(
-        kernel,
-        grid=(FF_STEPS,),
-        in_specs=jax.tree.leaves(in_specs),
-        out_specs=jax.tree.leaves(out_specs),
-        out_shape=out_shapes,
-        scratch_shapes=rooms,
-        compiler_params=pltpu.CompilerParams(vmem_limit_bytes=60_000_000, dimension_semantics=("arbitrary",)),
-        cost_estimate=pl.CostEstimate(flops=14_500_000_000, bytes_accessed=24_000_000, transcendentals=1_000_000),
-    )(*arrays)
-    return Named(jax.tree.unflatten(out_tree, results))
-
-
 def on_device(
     tokens, memory, cotangent, target_segments, memory_segments, self_gain, self_query, self_key,
     self_value, self_out, position_bias, cross_gain, cross_query, cross_key, cross_value, cross_out,
@@ -1521,28 +1538,17 @@
             cross_query=cross_query.T, cross_key=cross_key.T, cross_value=cross_value.T, cross_out=cross_out,
         )
     )
-    ff = ff_call(
-        batch_axis // 2,
-        dict(second=fwd.second, cot=fwd.cot, gain=ff_gain, gate=ff_gate, up=ff_up, down=ff_down),
-    )
-
-    def split(array):
-        return array.reshape(batch_axis // 4, 2, *array.shape[1:])
-
     done = backward_call(
         batch_axis,
         dict(
             segs=target_segments, memsegs=memory_segments, hot=one_hot, self_gain=self_gain, cross_gain=cross_gain,
-            ff_gain_grad=ff.gain_grad,
+            ff_gain=ff_gain, ff_gate=ff_gate, ff_up=ff_up, ff_down=ff_down,
             kv_two=fwd.kv_two, q_two=fwd.q_two, lse_two=fwd.lse_two, wt_two=fwd.wt_two,
             qkv_one=fwd.qkv_one, lse_one=fwd.lse_one, wt_one=fwd.wt_one, table=fwd.table,
             loaded=dict(
-                after=ff.after, wo_two=cross_out, ctx_two=fwd.ctx_two, n_two=fwd.n_two, mem=fwd.mem,
+                second=fwd.second, cot=fwd.cot, wo_two=cross_out, ctx_two=fwd.ctx_two, n_two=fwd.n_two, mem=fwd.mem,
                 first=fwd.first, wo_one=self_out, ctx_one=fwd.ctx_one, n_one=fwd.n_one, tok=fwd.tok,
             ),
-            sends=dict(gate=split(ff.gate[0]), up=split(ff.up[0]), down_a=split(ff.down_a[0]), down_b=split(ff.down_b[0])),
-            keeps=dict(gate=split(ff.gate[1]), up=split(ff.up[1]), down_a=split(ff.down_a[1]), down_b=split(ff.down_b[1])),
-            layer=ff.layer,
         ),
     )
     done = Named(finish_call(vars(done), heads_axis * batch_axis, position_bias.shape[0]))

time: 179 us -> 174 us (0.972)
  Pallas kernels: 178 us -> 173 us
    pallas_call x2 -> x1, Pallas kernels: 127 us -> 121 us  [backward_call(): pl.pallas_call(kernel, grid=(12,), in_specs=jax.tree.leaves(in_specs), ou...]
where the time goes in v6:
time: 174 us; the launch traced here: 173 us
  Pallas kernels  173 us (99%)
    pallas_call x1, Pallas kernels, backward_call(): pl.pallas_call(kernel, grid=(12,), in_specs=jax.tree.leaves(in_specs), ou...  121 us
    pallas_call x1, Pallas kernels, forward_call(): pl.pallas_call(kernel, grid=(8,), in_specs=jax.tree.leaves(in_specs), out...  46.6 us
    pallas_call x1, Pallas kernels, finish_call(): pl.pallas_call(kernel, in_specs=[fixed(results['gains'].shape), fixed(res...  4.66 us

profile of v6, /device:TPU:0, one launch (start us, length us, event | category | flops | bytes accessed | tf_op | source)
XLA Modules:
  0.0 173.5 jit_solution(16127319959101524991)
XLA Ops:
  0.7 46.6 %shard_map.340 = (bf16[512,768]{1,0:T(8,128)(2,1)}, bf16[768,512]{1,0:T(8,128)(2,1)}, bf16[768,512]{1,0:T(8,128)(2,1)}, f32[512,768]{1,0:T(8,128)}, bf16[4,384,5...) custom-call(bf16[2,256,768]{2,1,0:T(8,128)(2,1)} %refs_0_.2, ...), custom_call_target="tpu_custom_call" | custom-call | flops 10000000000 | bytes 40000000 | tf_op jit(solution)/shard_map/pallas_call | solution.py:1468
  47.3 121.4 %shard_map.341 = (f32[8,128]{1,0:T(8,128)}, f32[24,2048]{1,0:T(8,128)}, f32[8,768]{1,0:T(8,128)}, f32[64,768]{1,0:T(8,128)}, bf16[2,256,768]{2,1,0:T(8,128)(2,1)...) custom-call(f32[768]{0:T(1024)} %refs_0_.3, ...), custom_call_target="tpu_custom_call" | custom-call | flops 20000000000 | bytes 40000000 | tf_op jit(solution)/shard_map/pallas_call | solution.py:1166
  168.7 4.7 %shard_map.342 = (f32[3,32]{1,0:T(4,128)}, f32[24]{0:T(128)}, f32[24]{0:T(128)}, f32[24]{0:T(128)}, f32[24,2048]{1,0:T(8,128)}, /*index=5*/f32[64,768]{1,0:T(8,1...) custom-call(f32[8,768]{1,0:T(8,128)} %get-tuple-element.86.gains, ...), custom_call_target="tpu_custom_call" | custom-call | tf_op jit(solution)/shard_map/pallas_call | solution.py:1512

commit v7 on v6

--- a/solution.py
+++ b/solution.py
@@ -647,8 +647,8 @@
 
     def weight_products(target, left, lanes):
         rows = left.shape[0] // (2 * depth)
-        per = left.shape[0] // 2
-        for part in range(2):
+        per = left.shape[0]
+        for part in range(1):
             product = dot(left[part * per : (part + 1) * per, :], r.dqkv[:, lanes]).astype(BF16)
             for piece in range(per // rows):
                 at = part * (per // rows) + piece
@@ -662,8 +662,8 @@
                     target[(*to, slice(rows, rows + rows // 2))] = jnp.concatenate((rest[: rows // 2], rest[rows // 2 :]), axis=1)
 
     def add_rows(target, lanes, weights, fresh):
-        for part in range(2):
-            rows = slice(part * HALF, (part + 1) * HALF)
+        for part in range(1):
+            rows = slice(0, BLOCK)
             product = dot(r.dqkv[rows, lanes], weights)
 
             @pl.when(fresh)
@@ -782,11 +782,11 @@
     def _():
         root = np.float32(np.sqrt(2.0 / np.pi))
         model = r.normed.shape[1]
-        for part in range(4):
-            rows = slice(part * TILE, (part + 1) * TILE)
+        for part in range(2):
+            rows = slice(part * HALF, (part + 1) * HALF)
             normed = r.normed[rows, :]
             gate, up = dot(normed, ins.ff_gate[...]), dot(normed, ins.ff_up[...])
-            grad = over_rows(r.block[part // 2, (part % 2) * TILE : (part % 2 + 1) * TILE, :], ins.ff_down[...])
+            grad = over_rows(r.block[part], ins.ff_down[...])
             square = gate * gate
             half = 0.5 + 0.5 * jnp.tanh(gate * (root + (root * 0.044715) * square))
             gelu = gate * half
@@ -799,7 +799,8 @@
             r.grad_up[:, rows] = jnp.transpose(grad_up)
             r.acc_a[rows, :] = r.acc_a[rows, :] + dot(activation, ins.ff_down[...])
             r.acc_b[rows, :] = r.acc_b[rows, :] + over_rows(grad_gate, ins.ff_gate[...]) + over_rows(grad_up, ins.ff_up[...])
-            tick(range(FF_STEPS), part)
+            for point in (2 * part, 2 * part + 1):
+                tick(range(FF_STEPS), point)
         lanes = model // 2
         for which, keep in ((1 - core, False), (core, True)):
             right = r.normed[:, pl.ds(pl.multiple_of(which * lanes, 128), lanes)]

time: 174 us -> 162 us (0.931)
  Pallas kernels: 173 us -> 161 us
    pallas_call x1, Pallas kernels: 121 us -> 109 us  [backward_call(): pl.pallas_call(kernel, grid=(12,), in_specs=jax.tree.leaves(in_specs), ou...]
where the time goes in v7:
time: 162 us; the launch traced here: 161 us
  Pallas kernels  161 us (99%)
    pallas_call x1, Pallas kernels, backward_call(): pl.pallas_call(kernel, grid=(12,), in_specs=jax.tree.leaves(in_specs), ou...  109 us
    pallas_call x1, Pallas kernels, forward_call(): pl.pallas_call(kernel, grid=(8,), in_specs=jax.tree.leaves(in_specs), out...  46.6 us
    pallas_call x1, Pallas kernels, finish_call(): pl.pallas_call(kernel, in_specs=[fixed(results['gains'].shape), fixed(res...  4.66 us

profile of v7, /device:TPU:0, one launch (start us, length us, event | category | flops | bytes accessed | tf_op | source)
XLA Modules:
  0.0 161.5 jit_solution(5596708645480202749)
XLA Ops:
  0.7 46.6 %shard_map.340 = (bf16[512,768]{1,0:T(8,128)(2,1)}, bf16[768,512]{1,0:T(8,128)(2,1)}, bf16[768,512]{1,0:T(8,128)(2,1)}, f32[512,768]{1,0:T(8,128)}, bf16[4,384,5...) custom-call(bf16[2,256,768]{2,1,0:T(8,128)(2,1)} %refs_0_.2, ...), custom_call_target="tpu_custom_call" | custom-call | flops 10000000000 | bytes 40000000 | tf_op jit(solution)/shard_map/pallas_call | solution.py:1469
  47.3 109.4 %shard_map.341 = (f32[8,128]{1,0:T(8,128)}, f32[24,2048]{1,0:T(8,128)}, f32[8,768]{1,0:T(8,128)}, f32[64,768]{1,0:T(8,128)}, bf16[2,256,768]{2,1,0:T(8,128)(2,1)...) custom-call(f32[768]{0:T(1024)} %refs_0_.3, ...), custom_call_target="tpu_custom_call" | custom-call | flops 20000000000 | bytes 40000000 | tf_op jit(solution)/shard_map/pallas_call | solution.py:1167
  156.7 4.7 %shard_map.342 = (f32[3,32]{1,0:T(4,128)}, f32[24]{0:T(128)}, f32[24]{0:T(128)}, f32[24]{0:T(128)}, f32[24,2048]{1,0:T(8,128)}, /*index=5*/f32[64,768]{1,0:T(8,1...) custom-call(f32[8,768]{1,0:T(8,128)} %get-tuple-element.86.gains, ...), custom_call_target="tpu_custom_call" | custom-call | tf_op jit(solution)/shard_map/pallas_call | solution.py:1513

commit v8 on v7

--- a/solution.py
+++ b/solution.py
@@ -970,6 +970,7 @@
     @pl.when(step == 11)
     def _():
         gains, bias = r.gains, r.bias
+        sl.q_one.take()
         memory_swap.sent()
         memory_put.wait()
         tok.wait()
@@ -979,7 +980,6 @@
         gain_copies[0].start()
         bias_copies[0].start()
         bias_copies[1].start()
-        sl.q_one.take()
         sl.kv_one.far.add(1)
         gain_copies[0].done()
         gains[...] = gains[...] + r.gains_got[0]
@@ -1404,6 +1404,12 @@
             cross_keys(slot)
 
         r.q_two[slot] = dot(r.wt_two[slot, QS, :], r.n_two[...]).astype(BF16)
+
+        @pl.when(step == 7)
+        def _():
+            puts.q_two.start()
+            puts.kv_two.start()
+
         cross_forward(
             r.kv_two.at[slot], r.q_two.at[slot], r.mask, r.ctx_two.at[rows_at], r.lse_two.at[slot],
             lambda h: tick(range(4, 8), h),
@@ -1413,7 +1419,7 @@
     def _():
         out_two.wait()
         project_out(r.ctx_two, r.wo_two, r.first, r.second)
-        for put in (puts.second, puts.ctx_two, puts.q_two, puts.kv_two, puts.lse_two):
+        for put in (puts.second, puts.ctx_two, puts.lse_two):
             put.start()
         gather_one.sent()
         gather_two.sent()

time: 162 us -> 161 us (level)
  no operation moved by 1% of the time
where the time goes in v8:
time: 161 us
  Pallas kernels  160 us (99%)
    pallas_call x1, Pallas kernels, backward_call(): pl.pallas_call(kernel, grid=(12,), in_specs=jax.tree.leaves(in_specs), ou...  109 us
    pallas_call x1, Pallas kernels, forward_call(): pl.pallas_call(kernel, grid=(8,), in_specs=jax.tree.leaves(in_specs), out...  46 us
    pallas_call x1, Pallas kernels, finish_call(): pl.pallas_call(kernel, in_specs=[fixed(results['gains'].shape), fixed(res...  4.66 us

profile of v8, /device:TPU:0, one launch (start us, length us, event | category | flops | bytes accessed | tf_op | source)
XLA Modules:
  0.0 160.5 jit_solution(16271497645052995179)
XLA Ops:
  0.7 46.0 %shard_map.340 = (bf16[512,768]{1,0:T(8,128)(2,1)}, bf16[768,512]{1,0:T(8,128)(2,1)}, bf16[768,512]{1,0:T(8,128)(2,1)}, f32[512,768]{1,0:T(8,128)}, bf16[4,384,5...) custom-call(bf16[2,256,768]{2,1,0:T(8,128)(2,1)} %refs_0_.2, ...), custom_call_target="tpu_custom_call" | custom-call | flops 10000000000 | bytes 40000000 | tf_op jit(solution)/shard_map/pallas_call | solution.py:1475
  46.6 109.1 %shard_map.341 = (f32[8,128]{1,0:T(8,128)}, f32[24,2048]{1,0:T(8,128)}, f32[8,768]{1,0:T(8,128)}, f32[64,768]{1,0:T(8,128)}, bf16[2,256,768]{2,1,0:T(8,128)(2,1)...) custom-call(f32[768]{0:T(1024)} %refs_0_.3, ...), custom_call_target="tpu_custom_call" | custom-call | flops 20000000000 | bytes 40000000 | tf_op jit(solution)/shard_map/pallas_call | solution.py:1167
  155.7 4.7 %shard_map.342 = (f32[3,32]{1,0:T(4,128)}, f32[24]{0:T(128)}, f32[24]{0:T(128)}, f32[24]{0:T(128)}, f32[24,2048]{1,0:T(8,128)}, /*index=5*/f32[64,768]{1,0:T(8,1...) custom-call(f32[8,768]{1,0:T(8,128)} %get-tuple-element.86.gains, ...), custom_call_target="tpu_custom_call" | custom-call | tf_op jit(solution)/shard_map/pallas_call | solution.py:1519
